TPU v7x, 32 devices: a whole 2x2x4 slice. The times are simulated.
32 devices in a mesh: wide: 16 (over z, x, core), narrow: 2 (over y).
Axes of the slice: x: 2, y: 2, z: 4, core: 2. Of those that a mesh axis runs over, the one named last changes fastest.
Arguments:
- dosage: bfloat16 [2048, 32768], P(None, 'wide'), may hold values from -4 to 6, as said below
- annotations: int32 [128, 32768], P(None, 'wide'), may hold values from 0 to 1, as said below
- test_statistic_table: float32 [32768, 512], P('wide', 'narrow'), may hold values from 0 to 200
Outputs:
- ld_scores: float32 [128, 32768], P(None, ('wide', 'narrow'))
- fitted: float32 [32768, 512], P('wide', 'narrow')
Inputs may be any that keep to these rules, and one draw needn't show every extreme that they name: `dosage`: dosages of each variant follow a correlated process along the variants. `annotations`: 1 where a variant belongs to an annotation.
All inputs are finite; a program needn't handle non-finite values.
Results may differ from a plain program's by a relative error of at most 0.0023.
Values may be sent and summed in bfloat16 or wider, within the bound.
No kernel may reach another device: no remote copies, remote signals or barrier semaphores. Data moves between devices by JAX's collectives and lax.ppermute only.
A program may use at most 128 MiB of HBM per device.

v0:
```python
import functools

import jax
import jax.numpy as jnp
from jax import lax
from jax.experimental import pallas as pl
from jax.experimental.pallas import tpu as pltpu
from jax.sharding import PartitionSpec as P


EPS = 1e-05
TILE = 256
LANES = 128
ROWS = 256
PAD = 8
PIVOTS = 4
VMEM_LIMIT = 36 * 1024 * 1024

highest_precision = lax.Precision.HIGHEST
both = ("wide", "narrow")
in_vmem = pl.BlockSpec(memory_space=pltpu.VMEM)
in_place = pl.BlockSpec(memory_space=pl.ANY)
in_smem = pl.BlockSpec(memory_space=pltpu.SMEM)


def cols_at(c):
    return pl.ds(pl.multiple_of(c * TILE, TILE), TILE)


def standardized(read, write, wide_values, samples):
    steps = samples // ROWS
    empty = jnp.zeros((4 * PAD, TILE), jnp.float32)

    def folded(values):
        return jnp.sum(values.reshape(-1, 4 * PAD, TILE), axis=0)

    def rows_at(r):
        return pl.ds(pl.multiple_of(r * ROWS, ROWS), ROWS)

    def total(r, carry):
        values = read(rows_at(r)).astype(jnp.float32)
        wide_values[rows_at(r), :] = values
        return carry + folded(values)

    mean = jnp.sum(lax.fori_loop(0, steps, total, empty), axis=0, keepdims=True) / samples

    def squares(r, carry):
        away = wide_values[rows_at(r), :] - mean
        return carry + folded(away * away)

    variance = jnp.sum(lax.fori_loop(0, steps, squares, empty), axis=0, keepdims=True) / samples
    scale = 1.0 / jnp.sqrt(variance + EPS)

    def store(r, carry):
        write(rows_at(r), ((wide_values[rows_at(r), :] - mean) * scale).astype(jnp.bfloat16))
        return carry

    lax.fori_loop(0, steps, store, 0)


def into(geno, tile):
    def write(rows, value):
        geno[2 * tile, rows, :] = value[:, :LANES]
        geno[2 * tile + 1, rows, :] = value[:, LANES:]

    return write


def columns_of(geno, tile):
    return jnp.concatenate([geno[2 * tile], geno[2 * tile + 1]], axis=1)


def rows_of(turned, tile):
    return jnp.concatenate([turned[tile, k] for k in range(turned.shape[1])], axis=1)


def band_weights(rows, columns, inside=None):
    samples = rows.shape[1]
    products = jnp.dot(rows, columns, preferred_element_type=jnp.float32)
    unit = 1.0 / (samples - 2)
    weights = products * products * ((1.0 + unit) / (samples * samples)) - unit
    if inside is not None:
        weights = jnp.where(inside, weights, 0.0)
    return weights.astype(jnp.bfloat16)


def along_rows(annot, weights):
    return jnp.dot(annot, weights, preferred_element_type=jnp.float32)


def along_columns(annot, weights):
    return lax.dot_general(
        annot, weights, (((1,), (1,)), ((), ())), preferred_element_type=jnp.float32
    )


def tile_offset():
    shape = (TILE, TILE)
    return lax.broadcasted_iota(jnp.int32, shape, 0) - lax.broadcasted_iota(jnp.int32, shape, 1)


def sizes(dosage):
    samples, strip = dosage.shape
    return samples, strip, strip // (2 * TILE)


def outgoing_kernel(order, n_ref, dosage_ref, annot_ref, out_ref, given_annot, arrived):
    samples, strip = dosage_ref.shape
    annots = annot_ref.shape[0]
    n = n_ref[0]
    column = cols_at((1 - n) * (strip // TILE - 1 - order) + n * order)
    copies = [
        pltpu.make_async_copy(dosage_ref.at[:, column], out_ref.at[:samples, :], arrived.at[0]),
        pltpu.make_async_copy(annot_ref.at[:, column], given_annot, arrived.at[1]),
    ]
    for copy in copies:
        copy.start()
    row = lax.broadcasted_iota(jnp.int32, (PAD, TILE), 0)
    out_ref[samples + annots :, :] = jnp.where(row == 0, 1.0, 0.0).astype(jnp.bfloat16)
    copies[1].wait()
    out_ref[samples : samples + annots, :] = given_annot[...].astype(jnp.float32).astype(jnp.bfloat16)
    copies[0].wait()


def outgoing_columns(order, n, dosage, annotations):
    samples, _, _ = sizes(dosage)
    annots = annotations.shape[0]
    rows = samples + annots + PAD
    return pl.pallas_call(
        functools.partial(outgoing_kernel, order),
        out_shape=jax.ShapeDtypeStruct((rows, TILE), jnp.bfloat16),
        in_specs=[in_smem, in_place, in_place],
        out_specs=in_vmem,
        scratch_shapes=[pltpu.VMEM((annots, TILE), jnp.int32), pltpu.SemaphoreType.DMA((2,))],
        cost_estimate=pl.CostEstimate(flops=0, bytes_accessed=4 * rows * TILE, transcendentals=0),
        name="outgoing",
    )(n, dosage, annotations)


def strip_kernel(
    n_ref, dosage_ref, annot_ref, sums_ref, turned_ref, given, geno, turned, wide_values, came, went
):
    samples, strip = dosage_ref.shape
    tiles = strip // TILE
    mine = tiles // 2
    n = n_ref[0]

    def column(t):
        owner = n if t < mine else 1 - n
        return owner * mine + t % mine

    arrivals = [
        pltpu.make_async_copy(dosage_ref.at[:, cols_at(column(t))], given.at[t], came.at[t])
        for t in range(tiles)
    ]
    departures = [
        pltpu.make_async_copy(turned.at[t], turned_ref.at[t], went.at[t]) for t in range(mine)
    ]
    for copy in arrivals:
        copy.start()
    sums_ref[...] = jnp.zeros_like(sums_ref)
    for t in range(tiles):
        arrivals[t].wait()
        standardized(lambda rows: given[t, rows, :], into(geno, t), wide_values, samples)
        if t < mine:
            for k in range(samples // LANES):
                for part in range(2):
                    turned[t, k, part * LANES : (part + 1) * LANES, :] = geno[
                        2 * t + part, k * LANES : (k + 1) * LANES, :
                    ].T
            departures[t].start()
    for y in range(mine):
        for x in range(y + 1):
            weights = band_weights(rows_of(turned, x), columns_of(geno, y))
            sums_ref[:, y * TILE : (y + 1) * TILE] += along_rows(
                annot_ref[:, cols_at(column(x))], weights
            )
            if x < y:
                sums_ref[:, x * TILE : (x + 1) * TILE] += along_columns(
                    annot_ref[:, cols_at(column(y))], weights
                )
    inside = (1 - 2 * n) * tile_offset() >= 0
    for high in range(mine):
        for low in range(high + 1):
            theirs = low + n * (high - low)
            ours = high - n * (high - low)
            columns = jnp.concatenate(
                [geno[2 * (mine + theirs)], geno[2 * (mine + theirs) + 1]], axis=1
            )
            weights = band_weights(
                rows_of(turned, ours), columns, inside if low == high else None
            )
            sums_ref[:, cols_at(ours)] += along_columns(
                annot_ref[:, cols_at((1 - n) * mine + theirs)], weights
            )
    for copy in departures:
        copy.wait()


def strip_sums(n, dosage, annot):
    samples, strip, mine = sizes(dosage)
    block = strip // 2
    chunks = samples // LANES
    return pl.pallas_call(
        strip_kernel,
        out_shape=(
            jax.ShapeDtypeStruct((annot.shape[0], block), jnp.float32),
            jax.ShapeDtypeStruct((mine, chunks, TILE, LANES), jnp.bfloat16),
        ),
        in_specs=[in_smem, in_place, in_vmem],
        out_specs=(in_vmem, in_place),
        scratch_shapes=[
            pltpu.VMEM((2 * mine, samples, TILE), jnp.bfloat16),
            pltpu.VMEM((4 * mine, samples, LANES), jnp.bfloat16),
            pltpu.VMEM((mine, chunks, TILE, LANES), jnp.bfloat16),
            pltpu.VMEM((samples, TILE), jnp.float32),
            pltpu.SemaphoreType.DMA((2 * mine,)),
            pltpu.SemaphoreType.DMA((mine,)),
        ],
        cost_estimate=pl.CostEstimate(
            flops=2 * samples * block * strip,
            bytes_accessed=3 * samples * strip,
            transcendentals=0,
        ),
        name="strip_sums",
    )(n, dosage, annot)


def rim_kernel(
    order, n_ref, arrived_ref, turned_ref, annot_ref, sums_in, sums_ref, back_ref,
    geno, turned, wide_values, came,
):
    mine = turned_ref.shape[0]
    samples = geno.shape[1]
    n = n_ref[0]
    arrivals = [
        pltpu.make_async_copy(turned_ref.at[t], turned.at[t], came.at[t]) for t in range(mine)
    ]
    for copy in arrivals:
        copy.start()
    standardized(lambda rows: arrived_ref[rows, :], into(geno, 0), wide_values, samples)
    arrived_annot = arrived_ref[samples:, :]
    sums_ref[...] = sums_in[...]
    back_ref[...] = jnp.zeros_like(back_ref)
    for copy in arrivals:
        copy.wait()

    def add(y, inside=None):
        weights = band_weights(rows_of(turned, y), columns_of(geno, 0), inside)
        sums_ref[:, cols_at(y)] += along_columns(arrived_annot, weights)
        back_ref[...] += along_rows(annot_ref[:, cols_at(n * mine + y)], weights)

    low, high = order, mine - 1 - order
    add((1 - n) * high + n * low, (1 - 2 * n) * tile_offset() <= 0)
    for y in range(mine):
        first, second = y < high, low < y < mine // 2
        if first or second:

            @pl.when(True if first and second else (n == 0 if first else n == 1))
            def _(y=y):
                add(y)


def rim_sums(order, n, arrived, turned, annot, sums):
    mine, chunks, _, _ = turned.shape
    samples = chunks * LANES
    return pl.pallas_call(
        functools.partial(rim_kernel, order),
        out_shape=(
            jax.ShapeDtypeStruct(sums.shape, jnp.float32),
            jax.ShapeDtypeStruct((sums.shape[0], TILE), jnp.float32),
        ),
        in_specs=[in_smem, in_vmem, in_place, in_vmem, in_vmem],
        out_specs=(in_vmem, in_vmem),
        scratch_shapes=[
            pltpu.VMEM((2, samples, LANES), jnp.bfloat16),
            pltpu.VMEM(turned.shape, jnp.bfloat16),
            pltpu.VMEM((samples, TILE), jnp.float32),
            pltpu.SemaphoreType.DMA((mine,)),
        ],
        cost_estimate=pl.CostEstimate(
            flops=2 * samples * TILE * mine * TILE,
            bytes_accessed=2 * samples * TILE * (mine + 1),
            transcendentals=0,
        ),
        name="rim_sums",
    )(n, arrived, turned, annot, sums)


def eye(size):
    shape = (size, size)
    return lax.broadcasted_iota(jnp.int32, shape, 0) == lax.broadcasted_iota(jnp.int32, shape, 1)


def upright(row):
    size = row.shape[1]
    return jnp.sum(jnp.where(eye(size), jnp.broadcast_to(row, (size, size)), 0.0), axis=1, keepdims=True)


def moments_kernel(total_variants, place_ref, counts_ref, sums_ref, first_ref, second_ref, scores_ref, payload_ref, whole):
    annots = counts_ref.shape[1]
    block = sums_ref.shape[1]
    mine = block // TILE
    n, slot = place_ref[0], place_ref[1]
    whole[...] = sums_ref[...]
    for order, back_ref in enumerate((first_ref, second_ref)):
        whole[:, cols_at((1 - n) * order + n * (mine - 1 - order))] += back_ref[...]
    shares = upright(counts_ref[...]) / total_variants
    high = (1.0 - shares).astype(jnp.bfloat16).astype(jnp.float32)
    low = (0.0 - shares).astype(jnp.bfloat16).astype(jnp.float32)
    members = whole[:annots, :]
    scores = high * members + low * (whole[annots : annots + 1, :] - members)
    scores_ref[:annots, :] = scores
    row = lax.broadcasted_iota(jnp.int32, (2 * PAD, block), 0)
    scores_ref[annots:, :] = jnp.where(row == 0, 1.0, 0.0)
    mean = jnp.sum(scores, axis=1, keepdims=True) / block
    deviation = scores - mean
    payload_ref[:annots, :] = lax.dot_general(
        deviation,
        deviation,
        (((1,), (1,)), ((), ())),
        precision=highest_precision,
        preferred_element_type=jnp.float32,
    )
    mean_row = jnp.sum(
        jnp.where(eye(annots), jnp.broadcast_to(mean, (annots, annots)), 0.0), axis=0, keepdims=True
    )
    slots = payload_ref.shape[0] - annots
    at = lax.broadcasted_iota(jnp.int32, (slots, annots), 0)
    payload_ref[annots:, :] = jnp.where(at == slot, mean_row, 0.0)


def moments_of(total_variants, slots, place, counts, sums, back):
    annots = counts.shape[0]
    block = sums.shape[1]
    return pl.pallas_call(
        functools.partial(moments_kernel, total_variants),
        out_shape=(
            jax.ShapeDtypeStruct((annots + 2 * PAD, block), jnp.float32),
            jax.ShapeDtypeStruct((annots + slots, annots), jnp.float32),
        ),
        in_specs=[in_smem] + [in_vmem] * 4,
        out_specs=(in_vmem, in_vmem),
        scratch_shapes=[pltpu.VMEM(sums.shape, jnp.float32)],
        compiler_params=pltpu.CompilerParams(vmem_limit_bytes=VMEM_LIMIT),
        cost_estimate=pl.CostEstimate(
            flops=12 * annots * annots * block, bytes_accessed=12 * annots * block, transcendentals=0
        ),
        name="moments",
    )(place, counts.reshape(1, annots), sums, *back)


def inverse_kernel(divisor, payload_ref, inverse_ref, moments_ref):
    size = payload_ref.shape[1]
    slots = payload_ref.shape[0] - size
    means = payload_ref[size:, :]
    mean = jnp.sum(means, axis=0, keepdims=True) / slots
    between = means - mean
    covariance = (
        payload_ref[:size, :]
        + lax.dot_general(
            between,
            between,
            (((0,), (0,)), ((), ())),
            precision=highest_precision,
            preferred_element_type=jnp.float32,
        )
        * (divisor // slots)
    ) / divisor
    row = lax.broadcasted_iota(jnp.int32, (size, size), 0)
    lane = lax.broadcasted_iota(jnp.int32, (size, size), 1)
    diagonal = jnp.where(row == lane, covariance, 0.0)
    across = 1.0 / jnp.sqrt(jnp.sum(diagonal, axis=0, keepdims=True) + EPS)
    down = 1.0 / jnp.sqrt(jnp.sum(diagonal, axis=1, keepdims=True) + EPS)
    mean_down = jnp.sum(jnp.where(row == lane, jnp.broadcast_to(mean, (size, size)), 0.0), axis=1, keepdims=True)
    moments_ref[...] = jnp.where(lane == 0, mean_down, down)
    gram = covariance * down * across
    groups = [gram[PAD * g : PAD * (g + 1), :] for g in range(size // PAD)]
    lane_of = lax.broadcasted_iota(jnp.int32, (1, size), 1)
    row_of = lax.broadcasted_iota(jnp.int32, (PAD, size), 0)

    def pair_inverse(a, b, c):
        scale = 1.0 / (a * c - b * b)
        return c * scale, -b * scale, a * scale

    for k in range(0, size, PIVOTS):
        g, i = divmod(k, PAD)
        spread = [
            [jnp.broadcast_to(old[:, k + j : k + j + 1], (PAD, size)) for j in range(PIVOTS)]
            for old in groups
        ]
        m = [[spread[g][c][i + r : i + r + 1, :] for c in range(PIVOTS)] for r in range(PIVOTS)]
        rows = [
            groups[g][i + j : i + j + 1, :] - jnp.where(lane_of == k + j, 1.0, 0.0)
            for j in range(PIVOTS)
        ]
        a, b, c = pair_inverse(m[0][0], m[0][1], m[1][1])
        u = a * rows[0] + b * rows[1], b * rows[0] + c * rows[1]
        v = [(a * m[0][j] + b * m[1][j], b * m[0][j] + c * m[1][j]) for j in (2, 3)]
        rest = [rows[j] - m[0][j] * u[0] - m[1][j] * u[1] for j in (2, 3)]
        d, e, f = pair_inverse(
            m[2][2] - m[0][2] * v[0][0] - m[1][2] * v[0][1],
            m[2][3] - m[0][2] * v[1][0] - m[1][2] * v[1][1],
            m[3][3] - m[0][3] * v[1][0] - m[1][3] * v[1][1],
        )
        third = d * rest[0] + e * rest[1]
        fourth = e * rest[0] + f * rest[1]
        solved = [
            u[0] - v[0][0] * third - v[1][0] * fourth,
            u[1] - v[0][1] * third - v[1][1] * fourth,
            third,
            fourth,
        ]
        solved = [jnp.broadcast_to(value, (PAD, size)) for value in solved]
        for h, old in enumerate(groups):
            for j in range(PIVOTS):
                old = old - spread[h][j] * solved[j]
                if h == g:
                    old = old + jnp.where(row_of == i + j, solved[j], 0.0)
            groups[h] = old
    swept = jnp.concatenate(groups, axis=0)
    inverse = jnp.where(row == lane, 2.0, 0.0) - swept
    inverse_ref[...] = inverse * down * across / divisor


def gram_inverse(divisor, payload):
    size = payload.shape[1]
    square = jax.ShapeDtypeStruct((size, size), jnp.float32)
    return pl.pallas_call(
        functools.partial(inverse_kernel, divisor),
        out_shape=(square, square),
        in_specs=[in_vmem],
        out_specs=(in_vmem, in_vmem),
        compiler_params=pltpu.CompilerParams(vmem_limit_bytes=VMEM_LIMIT),
        cost_estimate=pl.CostEstimate(flops=20_000_000_000, bytes_accessed=4 * size * size, transcendentals=0),
        name="gram_inverse",
    )(payload)


def halves(value):
    upper = value.astype(jnp.bfloat16)
    return upper, (value - upper.astype(jnp.float32)).astype(jnp.bfloat16)


def fit_kernel(divisor, n_ref, inverse_ref, moments_ref, proj_ref, scores_ref, other_ref, own_ref, fitted_ref):
    annots = own_ref.shape[0]
    block = scores_ref.shape[1]
    n = n_ref[0]
    mean = moments_ref[:, 0:1]
    sums = proj_ref[annots : annots + 1, :]
    coefficient = jnp.dot(
        inverse_ref[...],
        proj_ref[:annots, :] - mean * sums,
        precision=highest_precision,
        preferred_element_type=jnp.float32,
    )
    upper, lower = halves(coefficient)
    right = jnp.concatenate([upper, upper, lower], axis=0)

    def fit(values, place):
        upper, lower = halves(values)
        fitted = lax.dot_general(
            jnp.concatenate([upper, lower, upper], axis=0),
            right,
            (((0,), (0,)), ((), ())),
            preferred_element_type=jnp.float32,
        )
        rows = pl.ds(pl.multiple_of(place * block, block), block)
        fitted_ref[rows, :] = sums / divisor + fitted

    centred = scores_ref[:annots, :] - mean
    own_ref[...] = centred * moments_ref[:, 1:2]
    fit(centred, n)
    fit(other_ref[...] - mean, 1 - n)


def fitted_values(divisor, n, inverse, moments, projection, scores, scores_other):
    annots, block = scores_other.shape
    traits = projection.shape[1]
    return pl.pallas_call(
        functools.partial(fit_kernel, divisor),
        out_shape=(
            jax.ShapeDtypeStruct((annots, block), jnp.float32),
            jax.ShapeDtypeStruct((2 * block, traits), jnp.float32),
        ),
        in_specs=[in_smem] + [in_vmem] * 5,
        out_specs=(in_vmem, in_vmem),
        compiler_params=pltpu.CompilerParams(vmem_limit_bytes=VMEM_LIMIT),
        cost_estimate=pl.CostEstimate(
            flops=4 * annots * block * traits, bytes_accessed=8 * block * traits, transcendentals=0
        ),
        name="fitted_values",
    )(n, inverse, moments, projection, scores, scores_other)


def flipped(value, axis, bit):
    length = lax.axis_size(axis)
    return lax.ppermute(value, axis, [(i, i ^ bit) for i in range(length)])


def wide_bits():
    length = lax.axis_size("wide")
    bits = []
    bit = 1
    while bit < length:
        bits.append(bit)
        bit *= 2
    return bits


def wide_sum(value):
    for bit in wide_bits():
        value = value + flipped(value, "wide", bit)
    return value


def split_wide_sum(value):
    half = value.shape[0] // 2
    low = lax.axis_index("wide") % 2
    kept = lax.dynamic_slice_in_dim(value, low * half, half, 0)
    given = lax.dynamic_slice_in_dim(value, (1 - low) * half, half, 0)
    kept = kept + flipped(given, "wide", 1)
    for bit in wide_bits()[1:]:
        kept = kept + flipped(kept, "wide", bit)
    other = flipped(kept, "wide", 1)
    return jnp.where(
        low == 0, jnp.concatenate([kept, other], 0), jnp.concatenate([other, kept], 0)
    )


def whole_step(dosage, annotations, test_statistic_table):
    _, strip = dosage.shape
    annots = annotations.shape[0]
    wide = lax.axis_size("wide")
    total_variants = wide * strip
    w = lax.axis_index("wide")
    n = lax.axis_index("narrow")
    block = strip // 2
    n_array = jnp.reshape(n, (1,)).astype(jnp.int32)

    annot = jnp.concatenate(
        [
            annotations.astype(jnp.bfloat16),
            jnp.ones((1, strip), jnp.bfloat16),
            jnp.zeros((PAD - 1, strip), jnp.bfloat16),
        ],
        axis=0,
    )
    rim_pairs = []
    back_pairs = []
    for i in range(wide - 1):
        rim_pairs += [(2 * i, 2 * i + 2), (2 * i + 3, 2 * i + 1)]
        back_pairs += [(2 * i + 1, 2 * i + 2), (2 * i + 2, 2 * i + 1)]
    arrived = []
    for order in range(2):
        outgoing = outgoing_columns(order, n_array, dosage, annotations)
        arrived.append(lax.ppermute(outgoing, both, rim_pairs))
    annotations, chi, _ = lax.optimization_barrier((annotations, test_statistic_table, outgoing))

    chi_own = lax.dynamic_slice_in_dim(chi, n * block, block, 0)
    chi_other = flipped(lax.dynamic_slice_in_dim(chi, (1 - n) * block, block, 0), "narrow", 1)
    counts = wide_sum(jnp.sum(annotations, axis=1).astype(jnp.float32))

    sums, turned = strip_sums(n_array, dosage, annot)
    back = []
    for order in range(2):
        sums, part = rim_sums(order, n_array, arrived[order], turned, annot, sums)
        back.append(lax.ppermute(part, both, back_pairs))

    place = jnp.stack([n, 2 * w + n]).astype(jnp.int32)
    extended, payload = moments_of(total_variants, 2 * wide, place, counts, sums, back)
    scores = extended[:annots]
    payload = payload + flipped(payload, "narrow", 1)
    payload = split_wide_sum(payload)
    proj_own, proj_other = (
        jnp.dot(
            extended, values, precision=lax.Precision.HIGH, preferred_element_type=jnp.float32
        )
        for values in (chi_own, chi_other)
    )
    projection = proj_own + flipped(proj_other, "narrow", 1)
    projection = split_wide_sum(projection)
    scores_other = flipped(scores, "narrow", 1)

    inverse, moments = gram_inverse(total_variants, payload)
    return fitted_values(
        total_variants, n_array, inverse, moments, projection, extended, scores_other
    )


def solution(mesh):
    in_specs = (P(None, "wide"), P(None, "wide"), P("wide", "narrow"))
    out_specs = (P(None, both), P("wide", "narrow"))
    return jax.shard_map(whole_step, mesh=mesh, in_specs=in_specs, out_specs=out_specs, check_vma=False)
```

profile of v0, /device:TPU:0, one launch (start us, length us, event | category | flops | bytes accessed | tf_op | source)
XLA Modules:
  0.0 111.9 jit_solution(12326727112463576382)
XLA Ops:
  0.6 0.0 copy-start
  0.6 0.0 copy-start.2
  0.7 2.4 %outgoing.2 = bf16[2184,256]{1,0:T(8,128)(2,1)} custom-call(s32[1]{0:T(128)} %bitcast.n_ref, bf16[2048,2048]{1,0:T(8,128)(2,1)} %dosage_ref.5, s32[128,2048]{1,0:T(8,128)} %annot_ref.3), custom_call_target="tpu_custom_call" | custom-call | bytes 2236416 | tf_op jit(solution)/shard_map/outgoing/pallas_call | solution.py:129
  3.1 3.5 %collective-permute-start.4 = (bf16[2184,256]{1,0:T(8,128)(2,1)}, bf16[2184,256]{1,0:T(8,128)(2,1)}, u32[]{:S(2)}, u32[]{:S(2)}) collective-permute-start(bf16[2184,256]{1,0:T(8,128)(2,1)} %outgoing.2), channel_id=1, source_target_pairs={{0,2},{3,1},{2,4},{5,3},{4,6},{7,5},{6,8},{9,7},{8,10},{11,9},{10,... | collective-permute-start | bytes 3354632 | tf_op jit(solution)/shard_map/ppermute | solution.py:557
  6.5 0.1 reduce_sum.9
  6.7 1.6 %collective-permute-start = (f32[128]{0:T(128)S(1)}, f32[128]{0:T(128)S(1)}, u32[]{:S(2)}, u32[]{:S(2)}) collective-permute-start(f32[128]{0:T(128)S(1)} %convert_element_type.6), channel_id=1, source_target_pairs={{0,2},{2,0},{4,6},{6,4},{8,10},{10,8},{12,14},{14,12},{16,18},{18,... | collective-permute-start | bytes 1544 | tf_op jit(solution)/shard_map/ppermute | solution.py:498
  8.3 2.3 %outgoing.3 = bf16[2184,256]{1,0:T(8,128)(2,1)} custom-call(s32[1]{0:T(128)} %bitcast.n_ref, bf16[2048,2048]{1,0:T(8,128)(2,1)} %dosage_ref.5, s32[128,2048]{1,0:T(8,128)} %annot_ref.3), custom_call_target="tpu_custom_call" | custom-call | bytes 2236416 | tf_op jit(solution)/shard_map/outgoing/pallas_call | solution.py:129
  10.6 3.1 %collective-permute-start.5 = (bf16[2184,256]{1,0:T(8,128)(2,1)}, bf16[2184,256]{1,0:T(8,128)(2,1)}, u32[]{:S(2)}, u32[]{:S(2)}) collective-permute-start(bf16[2184,256]{1,0:T(8,128)(2,1)} %outgoing.3), channel_id=1, source_target_pairs={{0,2},{3,1},{2,4},{5,3},{4,6},{7,5},{6,8},{9,7},{8,10},{11,9},{10,... | collective-permute-start | bytes 3354632 | tf_op jit(solution)/shard_map/ppermute | solution.py:557
  13.7 1.1 %constant_dynamic-slice_fusion.1 = f32[1024,256]{1,0:T(8,128)} fusion(f32[2048,256]{1,0:T(8,128)S(1)} %copy-done, s32[]{:T(128)S(6)} %select_n.50), kind=kLoop, calls=%fused_computation.8 | loop fusion | bytes 2097156 | tf_op jit(solution)/shard_map/dynamic_slice | solution.py:561
  14.8 0.1 convert_element_type.7
  14.9 0.1 pad.10.clone
  15.0 1.2 %maximum_maximum_fusion.annot_ref = bf16[136,2048]{1,0:T(8,128)(2,1)} fusion(bf16[128,2048]{1,0:T(8,128)(2,1)S(1)} %convert_element_type.7, bf16[136]{0:T(256)(128)(2,1)S(1)} %pad.10.clone, bf16[136]{0:T(256)(128)(2,1)S(1)} %pad.9.clone), kind=kLoop, calls=%fused_computation.2 | loop fusion | flops 1671168 | bytes 1081888 | tf_op jit(solution)/shard_map/concatenate | solution.py:541
  16.2 1.0 collective-permute-start.1
  17.2 21.7 %strip_sums.1 = (f32[136,1024]{1,0:T(8,128)}, bf16[4,16,256,128]{3,2,1,0:T(8,128)(2,1)}) custom-call(s32[1]{0:T(128)} %bitcast.n_ref, bf16[2048,2048]{1,0:T(8,128)(2,1)} %dosage_ref.5, bf16[136,2048]{1,0:T(8,128)(2,1)} %maximum_maximum_fusion.annot_ref), custom_call_target="tpu_custom_call" | custom-call | flops 8589934592 | bytes 12582912 | tf_op jit(solution)/shard_map/strip_sums/pallas_call | solution.py:204
  38.9 2.4 %collective-permute-start.2 = (f32[128]{0:T(128)S(1)}, f32[128]{0:T(128)S(1)}, u32[]{:S(2)}, u32[]{:S(2)}) collective-permute-start(f32[128]{0:T(128)S(1)} %add.71), channel_id=1, source_target_pairs={{0,8},{2,10},{4,12},{6,14},{8,0},{10,2},{12,4},{14,6},{16,24},{18,... | collective-permute-start | bytes 1544 | tf_op jit(solution)/shard_map/ppermute | solution.py:498
  41.4 0.1 pad_add_fusion.place_ref
  41.5 1.5 %collective-permute-done.2 = f32[128]{0:T(128)S(1)} collective-permute-done((f32[128]{0:T(128)S(1)}, f32[128]{0:T(128)S(1)}, u32[]{:S(2)}, u32[]{:S(2)}) %collective-permute-start.2) | collective-permute-done | bytes 544 | tf_op jit(solution)/shard_map/ppermute | solution.py:498
  42.9 3.0 %collective-permute-start.3 = (f32[128]{0:T(128)S(1)}, f32[128]{0:T(128)S(1)}, u32[]{:S(2)}, u32[]{:S(2)}) collective-permute-start(f32[128]{0:T(128)S(1)} %add.72), channel_id=1, source_target_pairs={{0,16},{2,18},{4,20},{6,22},{8,24},{10,26},{12,28},{14,30},{16,0},... | collective-permute-start | bytes 1544 | tf_op jit(solution)/shard_map/ppermute | solution.py:498
  46.0 7.6 %rim_sums.2 = (f32[136,1024]{1,0:T(8,128)}, f32[136,256]{1,0:T(8,128)}) custom-call(s32[1]{0:T(128)} %bitcast.n_ref, bf16[2184,256]{1,0:T(8,128)(2,1)} %collective-permute-done.5.arrived_ref, bf16[4,16,256,128]{3,2,1,0:T(8,128)(2,1)} %get-tuple-element.15.turned_ref, bf16[136,2048]{1,0:T(8,128)(2,1)} %maximum_maximum_fusion.annot_ref, ...), custom_call_target="tpu_custom_call" | custom-call | flops 1073741824 | bytes 5242880 | tf_op jit(solution)/shard_map/rim_sums/pallas_call | solution.py:267
  53.6 0.0 copy-start.4
  53.6 6.9 %rim_sums.3 = (f32[136,1024]{1,0:T(8,128)}, f32[136,256]{1,0:T(8,128)}) custom-call(s32[1]{0:T(128)} %bitcast.n_ref, bf16[2184,256]{1,0:T(8,128)(2,1)} %collective-permute-done.4.arrived_ref, bf16[4,16,256,128]{3,2,1,0:T(8,128)(2,1)} %get-tuple-element.15.turned_ref, bf16[136,2048]{1,0:T(8,128)(2,1)} %maximum_maximum_fusion.annot_ref, ...), custom_call_target="tpu_custom_call" | custom-call | flops 1073741824 | bytes 5242880 | tf_op jit(solution)/shard_map/rim_sums/pallas_call | solution.py:267
  60.5 0.7 collective-permute-start.7
  61.2 0.7 collective-permute-start.6
  61.9 1.0 copy-done.1
  63.0 1.4 %moments.1 = (f32[144,1024]{1,0:T(8,128)S(1)}, f32[160,128]{1,0:T(8,128)S(1)}) custom-call(s32[2]{0:T(128)S(1)} %pad_add_fusion.place_ref, f32[1,128]{1,0:T(1,128)S(1)} %add_bitcast_fusion.counts_ref, f32[136,1024]{1,0:T(8,128)S(1)} %copy-done.1, f32[136,256]{1,0:T(8,128)S(1)} %collective-permute-done.6.first_ref, ...), custom_call_target="tpu_custom_call" | custom-call | flops 201326592 | bytes 1572864 | tf_op jit(solution)/shard_map/moments/pallas_call | solution.py:336
  64.4 8.0 %collective-permute-start.8 = (f32[160,128]{1,0:T(8,128)S(1)}, f32[160,128]{1,0:T(8,128)S(1)}, u32[]{:S(2)}, u32[]{:S(2)}) collective-permute-start(f32[160,128]{1,0:T(8,128)S(1)} %get-tuple-element.21), channel_id=1, source_target_pairs={{0,1},{1,0},{2,3},{3,2},{4,5},{5,4},{6,7},{7,6},{8,9},{9,8},{10,11... | collective-permute-start | bytes 245768 | tf_op jit(solution)/shard_map/ppermute | solution.py:498
  72.4 1.7 %fusion.2 = f32[144,256]{1,0:T(8,128)S(1)} fusion(f32[144,1024]{1,0:T(8,128)S(1)} %get-tuple-element.24.scores_ref, f32[1024,256]{1,0:T(8,128)} %collective-permute-done.14), kind=kOutput, calls=%fused_computation.14 | convolution fusion | flops 226492416 | bytes 1785856 | tf_op jit(solution)/shard_map/dot_general | solution.py:576
  74.1 0.1 collective-permute-start.15
  74.2 0.6 collective-permute-done.8
  74.9 1.2 %collective-permute-start.9 = (f32[80,128]{1,0:T(8,128)S(1)}, f32[80,128]{1,0:T(8,128)S(1)}, u32[]{:S(2)}, u32[]{:S(2)}) collective-permute-start(f32[80,128]{1,0:T(8,128)S(1)} %constant_dynamic-slice_fusion.2), channel_id=1, source_target_pairs={{0,2},{2,0},{4,6},{6,4},{8,10},{10,8},{12,14},{14,12},{16,18},{18,... | collective-permute-start | bytes 122888 | tf_op jit(solution)/shard_map/ppermute | solution.py:498
  76.0 4.1 %collective-permute-done.15 = f32[144,256]{1,0:T(8,128)S(1)} collective-permute-done((f32[144,256]{1,0:T(8,128)S(1)}, f32[144,256]{1,0:T(8,128)S(1)}, u32[]{:S(2)}, u32[]{:S(2)}) %collective-permute-start.15) | collective-permute-done | bytes 147488 | tf_op jit(solution)/shard_map/ppermute | solution.py:498
  80.1 0.4 convolution_add_fusion
  80.6 0.6 collective-permute-start.16
  81.2 2.7 %collective-permute-start.10 = (f32[80,128]{1,0:T(8,128)S(1)}, f32[80,128]{1,0:T(8,128)S(1)}, u32[]{:S(2)}, u32[]{:S(2)}) collective-permute-start(f32[80,128]{1,0:T(8,128)S(1)} %dynamic-slice_add_fusion.1), channel_id=1, source_target_pairs={{0,4},{2,6},{4,0},{6,2},{8,12},{10,14},{12,8},{14,10},{16,20},{18,... | collective-permute-start | bytes 122888 | tf_op jit(solution)/shard_map/ppermute | solution.py:498
  83.9 0.9 collective-permute-start.17
  84.8 1.1 collective-permute-done.10
  85.9 1.9 %collective-permute-start.11 = (f32[80,128]{1,0:T(8,128)S(1)}, f32[80,128]{1,0:T(8,128)S(1)}, u32[]{:S(2)}, u32[]{:S(2)}) collective-permute-start(f32[80,128]{1,0:T(8,128)S(1)} %add.78), channel_id=1, source_target_pairs={{0,8},{2,10},{4,12},{6,14},{8,0},{10,2},{12,4},{14,6},{16,24},{18,... | collective-permute-start | bytes 122888 | tf_op jit(solution)/shard_map/ppermute | solution.py:498
  87.8 2.1 %collective-permute-done.11 = f32[80,128]{1,0:T(8,128)S(1)} collective-permute-done((f32[80,128]{1,0:T(8,128)S(1)}, f32[80,128]{1,0:T(8,128)S(1)}, u32[]{:S(2)}, u32[]{:S(2)}) %collective-permute-start.11) | collective-permute-done | bytes 40992 | tf_op jit(solution)/shard_map/ppermute | solution.py:498
  89.9 0.4 collective-permute-start.12
  90.3 2.0 %collective-permute-start.18 = (f32[72,256]{1,0:T(8,128)S(1)}, f32[72,256]{1,0:T(8,128)S(1)}, u32[]{:S(2)}, u32[]{:S(2)}) collective-permute-start(f32[72,256]{1,0:T(8,128)S(1)} %add.87), channel_id=1, source_target_pairs={{0,8},{2,10},{4,12},{6,14},{8,0},{10,2},{12,4},{14,6},{16,24},{18,... | collective-permute-start | bytes 221192 | tf_op jit(solution)/shard_map/ppermute | solution.py:498
  92.3 2.6 %collective-permute-done.12 = f32[80,128]{1,0:T(8,128)S(1)} collective-permute-done((f32[80,128]{1,0:T(8,128)S(1)}, f32[80,128]{1,0:T(8,128)S(1)}, u32[]{:S(2)}, u32[]{:S(2)}) %collective-permute-start.12) | collective-permute-done | bytes 40992 | tf_op jit(solution)/shard_map/ppermute | solution.py:498
  95.0 1.6 %collective-permute-start.21 = (f32[128,1024]{1,0:T(8,128)S(1)}, f32[128,1024]{1,0:T(8,128)S(1)}, u32[]{:S(2)}, u32[]{:S(2)}) collective-permute-start(f32[128,1024]{1,0:T(8,128)S(1)} %slice.3), channel_id=1, source_target_pairs={{0,1},{1,0},{2,3},{3,2},{4,5},{5,4},{6,7},{7,6},{8,9},{9,8},{10,11... | collective-permute-start | bytes 1572872 | tf_op jit(solution)/shard_map/ppermute | solution.py:498
  96.6 1.4 %collective-permute-start.19 = (f32[72,256]{1,0:T(8,128)S(1)}, f32[72,256]{1,0:T(8,128)S(1)}, u32[]{:S(2)}, u32[]{:S(2)}) collective-permute-start(f32[72,256]{1,0:T(8,128)S(1)} %add.88), channel_id=1, source_target_pairs={{0,16},{2,18},{4,20},{6,22},{8,24},{10,26},{12,28},{14,30},{16,0},... | collective-permute-start | bytes 221192 | tf_op jit(solution)/shard_map/ppermute | solution.py:498
  98.0 3.9 %collective-permute-done.19 = f32[72,256]{1,0:T(8,128)S(1)} collective-permute-done((f32[72,256]{1,0:T(8,128)S(1)}, f32[72,256]{1,0:T(8,128)S(1)}, u32[]{:S(2)}, u32[]{:S(2)}) %collective-permute-start.19) | collective-permute-done | bytes 73760 | tf_op jit(solution)/shard_map/ppermute | solution.py:498
  101.9 0.1 collective-permute-start.20
  102.0 6.5 %gram_inverse.1 = (f32[128,128]{1,0:T(8,128)S(1)}, f32[128,128]{1,0:T(8,128)S(1)}) custom-call(f32[160,128]{1,0:T(8,128)S(1)} %maximum_select_fusion.1.payload_ref), custom_call_target="tpu_custom_call" | custom-call | flops 20000000000 | bytes 65536 | tf_op jit(solution)/shard_map/gram_inverse/pallas_call | solution.py:429
  108.6 0.8 collective-permute-done.21.other_ref
  109.4 2.6 %fitted_values.1 = (f32[128,1024]{1,0:T(8,128)}, f32[2048,256]{1,0:T(8,128)}) custom-call(s32[1]{0:T(128)} %bitcast.n_ref, f32[128,128]{1,0:T(8,128)S(1)} %get-tuple-element.22.inverse_ref, f32[128,128]{1,0:T(8,128)S(1)} %get-tuple-element.23.moments_ref, f32[144,256]{1,0:T(8,128)S(1)} %maximum_select_fusion.proj_ref, ...), custom_call_target="tpu_custom_call" | custom-call | flops 134217728 | bytes 2097152 | tf_op jit(solution)/shard_map/fitted_values/pallas_call | solution.py:480
  (43 shorter events, 0.3 us)
Async XLA Ops:
  0.6 13.1 %copy-start = (f32[2048,256]{1,0:T(8,128)S(1)}, f32[2048,256]{1,0:T(8,128)}, u32[]{:S(2)}) copy-start(f32[2048,256]{1,0:T(8,128)} %param.5) | copy-start | bytes 6291460
  0.6 5.9 %copy-start.2 = (s32[128,2048]{1,0:T(8,128)S(1)}, s32[128,2048]{1,0:T(8,128)}, u32[]{:S(2)}) copy-start(s32[128,2048]{1,0:T(8,128)} %annot_ref.3) | copy-start | bytes 3145732
  3.1 50.5 %collective-permute-start.4 = (bf16[2184,256]{1,0:T(8,128)(2,1)}, bf16[2184,256]{1,0:T(8,128)(2,1)}, u32[]{:S(2)}, u32[]{:S(2)}) collective-permute-start(bf16[2184,256]{1,0:T(8,128)(2,1)} %outgoing.2), channel_id=1, source_target_pairs={{0,2},{3,1},{2,4},{5,3},{4,6},{7,5},{6,8},{9,7},{8,10},{11,9},{10,... | collective-permute-start | bytes 3354632 | tf_op jit(solution)/shard_map/ppermute | solution.py:557
  6.7 9.5 %collective-permute-start = (f32[128]{0:T(128)S(1)}, f32[128]{0:T(128)S(1)}, u32[]{:S(2)}, u32[]{:S(2)}) collective-permute-start(f32[128]{0:T(128)S(1)} %convert_element_type.6), channel_id=1, source_target_pairs={{0,2},{2,0},{4,6},{6,4},{8,10},{10,8},{12,14},{14,12},{16,18},{18,... | collective-permute-start | bytes 1544 | tf_op jit(solution)/shard_map/ppermute | solution.py:498
  10.6 4.2 %copy-start.3 = (s32[128,2048]{1,0:T(8,128)S(1)}, s32[128,2048]{1,0:T(8,128)}, u32[]{:S(2)}) copy-start(s32[128,2048]{1,0:T(8,128)} %annot_ref.3) | copy-start | bytes 3145732
  10.6 35.4 %collective-permute-start.5 = (bf16[2184,256]{1,0:T(8,128)(2,1)}, bf16[2184,256]{1,0:T(8,128)(2,1)}, u32[]{:S(2)}, u32[]{:S(2)}) collective-permute-start(bf16[2184,256]{1,0:T(8,128)(2,1)} %outgoing.3), channel_id=1, source_target_pairs={{0,2},{3,1},{2,4},{5,3},{4,6},{7,5},{6,8},{9,7},{8,10},{11,9},{10,... | collective-permute-start | bytes 3354632 | tf_op jit(solution)/shard_map/ppermute | solution.py:557
  14.8 57.6 %collective-permute-start.14 = (f32[1024,256]{1,0:T(8,128)}, f32[1024,256]{1,0:T(8,128)}, u32[]{:S(2)}, u32[]{:S(2)}) collective-permute-start(f32[1024,256]{1,0:T(8,128)} %constant_dynamic-slice_fusion.1), channel_id=1, source_target_pairs={{0,1},{1,0},{2,3},{3,2},{4,5},{5,4},{6,7},{7,6},{8,9},{9,8},{10,11... | collective-permute-start | bytes 3145736 | tf_op jit(solution)/shard_map/ppermute | solution.py:498
  16.2 22.8 %collective-permute-start.1 = (f32[128]{0:T(128)S(1)}, f32[128]{0:T(128)S(1)}, u32[]{:S(2)}, u32[]{:S(2)}) collective-permute-start(f32[128]{0:T(128)S(1)} %convert_add_fusion), channel_id=1, source_target_pairs={{0,4},{2,6},{4,0},{6,2},{8,12},{10,14},{12,8},{14,10},{16,20},{18,... | collective-permute-start | bytes 1544 | tf_op jit(solution)/shard_map/ppermute | solution.py:498
  38.9 4.0 %collective-permute-start.2 = (f32[128]{0:T(128)S(1)}, f32[128]{0:T(128)S(1)}, u32[]{:S(2)}, u32[]{:S(2)}) collective-permute-start(f32[128]{0:T(128)S(1)} %add.71), channel_id=1, source_target_pairs={{0,8},{2,10},{4,12},{6,14},{8,0},{10,2},{12,4},{14,6},{16,24},{18,... | collective-permute-start | bytes 1544 | tf_op jit(solution)/shard_map/ppermute | solution.py:498
  42.9 19.0 %collective-permute-start.3 = (f32[128]{0:T(128)S(1)}, f32[128]{0:T(128)S(1)}, u32[]{:S(2)}, u32[]{:S(2)}) collective-permute-start(f32[128]{0:T(128)S(1)} %add.72), channel_id=1, source_target_pairs={{0,16},{2,18},{4,20},{6,22},{8,24},{10,26},{12,28},{14,30},{16,0},... | collective-permute-start | bytes 1544 | tf_op jit(solution)/shard_map/ppermute | solution.py:498
  53.6 7.6 %copy-start.4 = (f32[136,256]{1,0:T(8,128)S(1)}, f32[136,256]{1,0:T(8,128)}, u32[]{:S(2)}) copy-start(f32[136,256]{1,0:T(8,128)} %get-tuple-element.19) | copy-start | bytes 417796
  60.5 1.4 %collective-permute-start.7 = (f32[136,256]{1,0:T(8,128)}, f32[136,256]{1,0:T(8,128)S(1)}, u32[]{:S(2)}, u32[]{:S(2)}) collective-permute-start(f32[136,256]{1,0:T(8,128)} %get-tuple-element.20), channel_id=1, source_target_pairs={{1,2},{2,1},{3,4},{4,3},{5,6},{6,5},{7,8},{8,7},{9,10},{10,9},{11,... | collective-permute-start | bytes 417800 | tf_op jit(solution)/shard_map/ppermute | solution.py:568
  61.2 0.7 collective-permute-start.6
  61.9 1.1 copy-start.1
  64.4 10.4 %collective-permute-start.8 = (f32[160,128]{1,0:T(8,128)S(1)}, f32[160,128]{1,0:T(8,128)S(1)}, u32[]{:S(2)}, u32[]{:S(2)}) collective-permute-start(f32[160,128]{1,0:T(8,128)S(1)} %get-tuple-element.21), channel_id=1, source_target_pairs={{0,1},{1,0},{2,3},{3,2},{4,5},{5,4},{6,7},{7,6},{8,9},{9,8},{10,11... | collective-permute-start | bytes 245768 | tf_op jit(solution)/shard_map/ppermute | solution.py:498
  74.1 6.1 %collective-permute-start.15 = (f32[144,256]{1,0:T(8,128)S(1)}, f32[144,256]{1,0:T(8,128)S(1)}, u32[]{:S(2)}, u32[]{:S(2)}) collective-permute-start(f32[144,256]{1,0:T(8,128)S(1)} %fusion.2), channel_id=1, source_target_pairs={{0,1},{1,0},{2,3},{3,2},{4,5},{5,4},{6,7},{7,6},{8,9},{9,8},{10,11... | collective-permute-start | bytes 442376 | tf_op jit(solution)/shard_map/ppermute | solution.py:498
  74.9 6.4 %collective-permute-start.9 = (f32[80,128]{1,0:T(8,128)S(1)}, f32[80,128]{1,0:T(8,128)S(1)}, u32[]{:S(2)}, u32[]{:S(2)}) collective-permute-start(f32[80,128]{1,0:T(8,128)S(1)} %constant_dynamic-slice_fusion.2), channel_id=1, source_target_pairs={{0,2},{2,0},{4,6},{6,4},{8,10},{10,8},{12,14},{14,12},{16,18},{18,... | collective-permute-start | bytes 122888 | tf_op jit(solution)/shard_map/ppermute | solution.py:498
  80.6 3.3 %collective-permute-start.16 = (f32[72,256]{1,0:T(8,128)S(1)}, f32[72,256]{1,0:T(8,128)S(1)}, u32[]{:S(2)}, u32[]{:S(2)}) collective-permute-start(f32[72,256]{1,0:T(8,128)S(1)} %constant_dynamic-slice_fusion), channel_id=1, source_target_pairs={{0,2},{2,0},{4,6},{6,4},{8,10},{10,8},{12,14},{14,12},{16,18},{18,... | collective-permute-start | bytes 221192 | tf_op jit(solution)/shard_map/ppermute | solution.py:498
  81.2 4.7 %collective-permute-start.10 = (f32[80,128]{1,0:T(8,128)S(1)}, f32[80,128]{1,0:T(8,128)S(1)}, u32[]{:S(2)}, u32[]{:S(2)}) collective-permute-start(f32[80,128]{1,0:T(8,128)S(1)} %dynamic-slice_add_fusion.1), channel_id=1, source_target_pairs={{0,4},{2,6},{4,0},{6,2},{8,12},{10,14},{12,8},{14,10},{16,20},{18,... | collective-permute-start | bytes 122888 | tf_op jit(solution)/shard_map/ppermute | solution.py:498
  83.9 6.3 %collective-permute-start.17 = (f32[72,256]{1,0:T(8,128)S(1)}, f32[72,256]{1,0:T(8,128)S(1)}, u32[]{:S(2)}, u32[]{:S(2)}) collective-permute-start(f32[72,256]{1,0:T(8,128)S(1)} %dynamic-slice_add_fusion), channel_id=1, source_target_pairs={{0,4},{2,6},{4,0},{6,2},{8,12},{10,14},{12,8},{14,10},{16,20},{18,... | collective-permute-start | bytes 221192 | tf_op jit(solution)/shard_map/ppermute | solution.py:498
  85.9 4.0 %collective-permute-start.11 = (f32[80,128]{1,0:T(8,128)S(1)}, f32[80,128]{1,0:T(8,128)S(1)}, u32[]{:S(2)}, u32[]{:S(2)}) collective-permute-start(f32[80,128]{1,0:T(8,128)S(1)} %add.78), channel_id=1, source_target_pairs={{0,8},{2,10},{4,12},{6,14},{8,0},{10,2},{12,4},{14,6},{16,24},{18,... | collective-permute-start | bytes 122888 | tf_op jit(solution)/shard_map/ppermute | solution.py:498
  89.9 5.0 %collective-permute-start.12 = (f32[80,128]{1,0:T(8,128)S(1)}, f32[80,128]{1,0:T(8,128)S(1)}, u32[]{:S(2)}, u32[]{:S(2)}) collective-permute-start(f32[80,128]{1,0:T(8,128)S(1)} %add.79), channel_id=1, source_target_pairs={{0,16},{2,18},{4,20},{6,22},{8,24},{10,26},{12,28},{14,30},{16,0},... | collective-permute-start | bytes 122888 | tf_op jit(solution)/shard_map/ppermute | solution.py:498
  90.3 6.3 %collective-permute-start.18 = (f32[72,256]{1,0:T(8,128)S(1)}, f32[72,256]{1,0:T(8,128)S(1)}, u32[]{:S(2)}, u32[]{:S(2)}) collective-permute-start(f32[72,256]{1,0:T(8,128)S(1)} %add.87), channel_id=1, source_target_pairs={{0,8},{2,10},{4,12},{6,14},{8,0},{10,2},{12,4},{14,6},{16,24},{18,... | collective-permute-start | bytes 221192 | tf_op jit(solution)/shard_map/ppermute | solution.py:498
  94.9 3.1 %collective-permute-start.13 = (f32[80,128]{1,0:T(8,128)S(1)}, f32[80,128]{1,0:T(8,128)S(1)}, u32[]{:S(2)}, u32[]{:S(2)}) collective-permute-start(f32[80,128]{1,0:T(8,128)S(1)} %add.80), channel_id=1, source_target_pairs={{0,2},{2,0},{4,6},{6,4},{8,10},{10,8},{12,14},{14,12},{16,18},{18,... | collective-permute-start | bytes 122888 | tf_op jit(solution)/shard_map/ppermute | solution.py:498
  95.0 14.4 %collective-permute-start.21 = (f32[128,1024]{1,0:T(8,128)S(1)}, f32[128,1024]{1,0:T(8,128)S(1)}, u32[]{:S(2)}, u32[]{:S(2)}) collective-permute-start(f32[128,1024]{1,0:T(8,128)S(1)} %slice.3), channel_id=1, source_target_pairs={{0,1},{1,0},{2,3},{3,2},{4,5},{5,4},{6,7},{7,6},{8,9},{9,8},{10,11... | collective-permute-start | bytes 1572872 | tf_op jit(solution)/shard_map/ppermute | solution.py:498
  96.6 5.4 %collective-permute-start.19 = (f32[72,256]{1,0:T(8,128)S(1)}, f32[72,256]{1,0:T(8,128)S(1)}, u32[]{:S(2)}, u32[]{:S(2)}) collective-permute-start(f32[72,256]{1,0:T(8,128)S(1)} %add.88), channel_id=1, source_target_pairs={{0,16},{2,18},{4,20},{6,22},{8,24},{10,26},{12,28},{14,30},{16,0},... | collective-permute-start | bytes 221192 | tf_op jit(solution)/shard_map/ppermute | solution.py:498
  101.9 6.6 %collective-permute-start.20 = (f32[72,256]{1,0:T(8,128)S(1)}, f32[72,256]{1,0:T(8,128)S(1)}, u32[]{:S(2)}, u32[]{:S(2)}) collective-permute-start(f32[72,256]{1,0:T(8,128)S(1)} %add.89), channel_id=1, source_target_pairs={{0,2},{2,0},{4,6},{6,4},{8,10},{10,8},{12,14},{14,12},{16,18},{18,... | collective-permute-start | bytes 221192 | tf_op jit(solution)/shard_map/ppermute | solution.py:498
where the time goes:
time: 112 us
  Pallas kernels  51.4 us (46%)
  starting transfers between devices  36.9 us (33%)
  waiting for transfers between devices  16.6 us (15%)
  local copies, waits for them, and re-layouts  2.36 us (2%)
  matrix products  2.09 us (2%)
  other arithmetic  1.57 us (1%)
    ppermute x18, starting transfers between devices, flipped(): return lax.ppermute(value, axis, [(i, i ^ bit) for i in range(length)])  29 us
    pallas_call x1, Pallas kernels, strip_sums(): pl.pallas_call(strip_kernel, out_shape=(jax.ShapeDtypeStruct((annot.shape...  21.7 us
    ppermute x18, waiting for transfers between devices, flipped(): return lax.ppermute(value, axis, [(i, i ^ bit) for i in range(length)])  16.6 us
    pallas_call x2, Pallas kernels, rim_sums(): pl.pallas_call(functools.partial(rim_kernel, order), out_shape=(jax.Shape...  14.5 us
    ppermute x2, starting transfers between devices, whole_step(): arrived.append(lax.ppermute(outgoing, both, rim_pairs))  6.55 us
    pallas_call x1, Pallas kernels, gram_inverse(): pl.pallas_call(functools.partial(inverse_kernel, divisor), out_shape=(squ...  6.54 us
    pallas_call x2, Pallas kernels, outgoing_columns(): pl.pallas_call(functools.partial(outgoing_kernel, order), out_shape=jax.S...  4.68 us
    pallas_call x1, Pallas kernels, fitted_values(): pl.pallas_call(functools.partial(fit_kernel, divisor), out_shape=(jax.Sha...  2.56 us
  transfers between devices with their start and end apart: 22, of which 8 were waited for; matrix products, arithmetic and copies ran while one was open for 4% of the time, Pallas kernels for 41%

commit v1 on v0

--- a/solution.py
+++ b/solution.py
@@ -19,7 +19,7 @@
 highest_precision = lax.Precision.HIGHEST
 both = ("wide", "narrow")
 in_vmem = pl.BlockSpec(memory_space=pltpu.VMEM)
-in_place = pl.BlockSpec(memory_space=pl.ANY)
+in_place = pl.BlockSpec(memory_space=pltpu.HBM)
 in_smem = pl.BlockSpec(memory_space=pltpu.SMEM)
 
 
@@ -30,6 +30,7 @@
 def standardized(read, write, wide_values, samples):
     steps = samples // ROWS
     empty = jnp.zeros((4 * PAD, TILE), jnp.float32)
+    pivot = read(pl.ds(0, 2 * PAD)).astype(jnp.float32)[:1, :]
 
     def folded(values):
         return jnp.sum(values.reshape(-1, 4 * PAD, TILE), axis=0)
@@ -38,21 +39,19 @@
         return pl.ds(pl.multiple_of(r * ROWS, ROWS), ROWS)
 
     def total(r, carry):
-        values = read(rows_at(r)).astype(jnp.float32)
+        values = read(rows_at(r)).astype(jnp.float32) - pivot
         wide_values[rows_at(r), :] = values
-        return carry + folded(values)
-
-    mean = jnp.sum(lax.fori_loop(0, steps, total, empty), axis=0, keepdims=True) / samples
-
-    def squares(r, carry):
-        away = wide_values[rows_at(r), :] - mean
-        return carry + folded(away * away)
-
-    variance = jnp.sum(lax.fori_loop(0, steps, squares, empty), axis=0, keepdims=True) / samples
+        return carry[0] + folded(values), carry[1] + folded(values * values)
+
+    first, second = (
+        jnp.sum(value, axis=0, keepdims=True) / samples
+        for value in lax.fori_loop(0, steps, total, (empty, empty))
+    )
+    variance = jnp.maximum(second - first * first, 0.0)
     scale = 1.0 / jnp.sqrt(variance + EPS)
 
     def store(r, carry):
-        write(rows_at(r), ((wide_values[rows_at(r), :] - mean) * scale).astype(jnp.bfloat16))
+        write(rows_at(r), ((wide_values[rows_at(r), :] - first) * scale).astype(jnp.bfloat16))
         return carry
 
     lax.fori_loop(0, steps, store, 0)
@@ -104,54 +103,65 @@
     return samples, strip, strip // (2 * TILE)
 
 
-def outgoing_kernel(order, n_ref, dosage_ref, annot_ref, out_ref, given_annot, arrived):
+def prepare_kernel(
+    n_ref, dosage_ref, annot_ref, chi_ref, out_ref, annot_out_ref, counts_ref, chi_out_ref, given_annot, came
+):
     samples, strip = dosage_ref.shape
     annots = annot_ref.shape[0]
+    block = strip // 2
+    width = out_ref.shape[1]
     n = n_ref[0]
-    column = cols_at((1 - n) * (strip // TILE - 1 - order) + n * order)
+    column = pl.ds(pl.multiple_of((1 - n) * (strip - width), width), width)
+    rows = pl.ds(pl.multiple_of((1 - n) * block, block), block)
     copies = [
-        pltpu.make_async_copy(dosage_ref.at[:, column], out_ref.at[:samples, :], arrived.at[0]),
-        pltpu.make_async_copy(annot_ref.at[:, column], given_annot, arrived.at[1]),
+        pltpu.make_async_copy(annot_ref, given_annot, came.at[0]),
+        pltpu.make_async_copy(dosage_ref.at[:, column], out_ref.at[:samples, :], came.at[1]),
+        pltpu.make_async_copy(chi_ref.at[rows, :], chi_out_ref, came.at[2]),
     ]
     for copy in copies:
         copy.start()
-    row = lax.broadcasted_iota(jnp.int32, (PAD, TILE), 0)
-    out_ref[samples + annots :, :] = jnp.where(row == 0, 1.0, 0.0).astype(jnp.bfloat16)
-    copies[1].wait()
-    out_ref[samples : samples + annots, :] = given_annot[...].astype(jnp.float32).astype(jnp.bfloat16)
+    row = lax.broadcasted_iota(jnp.int32, (PAD, strip), 0)
+    annot_out_ref[annots:, :] = jnp.where(row == 0, 1.0, 0.0).astype(jnp.bfloat16)
     copies[0].wait()
-
-
-def outgoing_columns(order, n, dosage, annotations):
-    samples, _, _ = sizes(dosage)
+    members = given_annot[...].astype(jnp.float32)
+    annot_out_ref[:annots, :] = members.astype(jnp.bfloat16)
+    counts = jnp.sum(members, axis=1, keepdims=True)
+    counts_ref[...] = lying(counts)
+    out_ref[samples:, :] = annot_out_ref[:, column]
+    for copy in copies[1:]:
+        copy.wait()
+
+
+def prepared(n, dosage, annotations, chi):
+    samples, strip, _ = sizes(dosage)
     annots = annotations.shape[0]
-    rows = samples + annots + PAD
+    rows = annots + PAD
+    width = strip // 4
     return pl.pallas_call(
-        functools.partial(outgoing_kernel, order),
-        out_shape=jax.ShapeDtypeStruct((rows, TILE), jnp.bfloat16),
-        in_specs=[in_smem, in_place, in_place],
-        out_specs=in_vmem,
-        scratch_shapes=[pltpu.VMEM((annots, TILE), jnp.int32), pltpu.SemaphoreType.DMA((2,))],
-        cost_estimate=pl.CostEstimate(flops=0, bytes_accessed=4 * rows * TILE, transcendentals=0),
-        name="outgoing",
-    )(n, dosage, annotations)
-
-
-def strip_kernel(
-    n_ref, dosage_ref, annot_ref, sums_ref, turned_ref, given, geno, turned, wide_values, came, went
-):
+        prepare_kernel,
+        out_shape=(
+            jax.ShapeDtypeStruct((samples + rows, width), jnp.bfloat16),
+            jax.ShapeDtypeStruct((rows, strip), jnp.bfloat16),
+            jax.ShapeDtypeStruct((1, annots), jnp.float32),
+            jax.ShapeDtypeStruct((strip // 2, chi.shape[1]), jnp.float32),
+        ),
+        in_specs=[in_smem, in_place, in_place, in_place],
+        out_specs=(in_vmem,) * 4,
+        scratch_shapes=[pltpu.VMEM(annotations.shape, jnp.int32), pltpu.SemaphoreType.DMA((3,))],
+        cost_estimate=pl.CostEstimate(
+            flops=0, bytes_accessed=4 * samples * width + 8 * strip * annots, transcendentals=0
+        ),
+        name="prepare",
+    )(n, dosage, annotations, chi)
+
+
+def own_kernel(n_ref, dosage_ref, annot_ref, sums_ref, turned_ref, given, geno, turned, wide_values, came, went):
     samples, strip = dosage_ref.shape
-    tiles = strip // TILE
-    mine = tiles // 2
+    mine = strip // (2 * TILE)
     n = n_ref[0]
-
-    def column(t):
-        owner = n if t < mine else 1 - n
-        return owner * mine + t % mine
-
     arrivals = [
-        pltpu.make_async_copy(dosage_ref.at[:, cols_at(column(t))], given.at[t], came.at[t])
-        for t in range(tiles)
+        pltpu.make_async_copy(dosage_ref.at[:, cols_at(n * mine + t)], given.at[t], came.at[t])
+        for t in range(mine)
     ]
     departures = [
         pltpu.make_async_copy(turned.at[t], turned_ref.at[t], went.at[t]) for t in range(mine)
@@ -159,128 +169,181 @@
     for copy in arrivals:
         copy.start()
     sums_ref[...] = jnp.zeros_like(sums_ref)
-    for t in range(tiles):
+    for t in range(mine):
         arrivals[t].wait()
         standardized(lambda rows: given[t, rows, :], into(geno, t), wide_values, samples)
-        if t < mine:
-            for k in range(samples // LANES):
-                for part in range(2):
-                    turned[t, k, part * LANES : (part + 1) * LANES, :] = geno[
-                        2 * t + part, k * LANES : (k + 1) * LANES, :
-                    ].T
-            departures[t].start()
+        for k in range(samples // LANES):
+            for part in range(2):
+                turned[t, k, part * LANES : (part + 1) * LANES, :] = geno[
+                    2 * t + part, k * LANES : (k + 1) * LANES, :
+                ].T
+        departures[t].start()
     for y in range(mine):
         for x in range(y + 1):
             weights = band_weights(rows_of(turned, x), columns_of(geno, y))
             sums_ref[:, y * TILE : (y + 1) * TILE] += along_rows(
-                annot_ref[:, cols_at(column(x))], weights
+                annot_ref[:, cols_at(n * mine + x)], weights
             )
             if x < y:
                 sums_ref[:, x * TILE : (x + 1) * TILE] += along_columns(
-                    annot_ref[:, cols_at(column(y))], weights
+                    annot_ref[:, cols_at(n * mine + y)], weights
                 )
+    for copy in departures:
+        copy.wait()
+
+
+def other_kernel(
+    n_ref, dosage_ref, annot_ref, turned_ref, sums_in, sums_ref, given, geno, turned, wide_values, came, back
+):
+    samples, strip = dosage_ref.shape
+    mine = strip // (2 * TILE)
+    n = n_ref[0]
+    arrivals = [
+        pltpu.make_async_copy(dosage_ref.at[:, cols_at((1 - n) * mine + t)], given.at[t], came.at[t])
+        for t in range(mine)
+    ]
+    returns = [
+        pltpu.make_async_copy(turned_ref.at[t], turned.at[t], back.at[t]) for t in range(mine)
+    ]
+    for copy in arrivals + returns:
+        copy.start()
+    sums_ref[...] = sums_in[...]
+    for t in range(mine):
+        arrivals[t].wait()
+        standardized(lambda rows: given[t, rows, :], into(geno, t), wide_values, samples)
+    for copy in returns:
+        copy.wait()
     inside = (1 - 2 * n) * tile_offset() >= 0
     for high in range(mine):
         for low in range(high + 1):
             theirs = low + n * (high - low)
             ours = high - n * (high - low)
-            columns = jnp.concatenate(
-                [geno[2 * (mine + theirs)], geno[2 * (mine + theirs) + 1]], axis=1
-            )
             weights = band_weights(
-                rows_of(turned, ours), columns, inside if low == high else None
+                rows_of(turned, ours), columns_of(geno, theirs), inside if low == high else None
             )
             sums_ref[:, cols_at(ours)] += along_columns(
                 annot_ref[:, cols_at((1 - n) * mine + theirs)], weights
             )
-    for copy in departures:
-        copy.wait()
-
-
-def strip_sums(n, dosage, annot):
+
+
+def own_sums(n, dosage, annot):
     samples, strip, mine = sizes(dosage)
-    block = strip // 2
     chunks = samples // LANES
+    turned = (mine, chunks, TILE, LANES)
     return pl.pallas_call(
-        strip_kernel,
+        own_kernel,
         out_shape=(
-            jax.ShapeDtypeStruct((annot.shape[0], block), jnp.float32),
-            jax.ShapeDtypeStruct((mine, chunks, TILE, LANES), jnp.bfloat16),
+            jax.ShapeDtypeStruct((annot.shape[0], strip // 2), jnp.float32),
+            jax.ShapeDtypeStruct(turned, jnp.bfloat16),
         ),
         in_specs=[in_smem, in_place, in_vmem],
         out_specs=(in_vmem, in_place),
+        scratch_shapes=strip_scratch(dosage),
+        cost_estimate=strip_cost(dosage),
+        name="own_sums",
+    )(n, dosage, annot)
+
+
+def other_sums(n, dosage, annot, turned, sums):
+    return pl.pallas_call(
+        other_kernel,
+        out_shape=jax.ShapeDtypeStruct(sums.shape, jnp.float32),
+        in_specs=[in_smem, in_place, in_vmem, in_place, in_vmem],
+        out_specs=in_vmem,
+        scratch_shapes=strip_scratch(dosage),
+        cost_estimate=strip_cost(dosage),
+        name="other_sums",
+    )(n, dosage, annot, turned, sums)
+
+
+def strip_scratch(dosage):
+    samples, _, mine = sizes(dosage)
+    return [
+        pltpu.VMEM((mine, samples, TILE), jnp.bfloat16),
+        pltpu.VMEM((2 * mine, samples, LANES), jnp.bfloat16),
+        pltpu.VMEM((mine, samples // LANES, TILE, LANES), jnp.bfloat16),
+        pltpu.VMEM((samples, TILE), jnp.float32),
+        pltpu.SemaphoreType.DMA((mine,)),
+        pltpu.SemaphoreType.DMA((mine,)),
+    ]
+
+
+def strip_cost(dosage):
+    samples, strip, _ = sizes(dosage)
+    return pl.CostEstimate(
+        flops=samples * strip * strip // 2, bytes_accessed=2 * samples * strip, transcendentals=0
+    )
+
+
+def rim_kernel(
+    n_ref, arrived_ref, turned_ref, annot_ref, sums_in, sums_ref, back_ref,
+    given, geno, turned, wide_values, came, back,
+):
+    mine = turned_ref.shape[0]
+    samples = geno.shape[1]
+    width = mine // 2
+    n = n_ref[0]
+    arrivals = [
+        pltpu.make_async_copy(
+            arrived_ref.at[:, c * TILE : (c + 1) * TILE], given.at[c], came.at[c]
+        )
+        for c in range(width)
+    ]
+    returns = [
+        pltpu.make_async_copy(turned_ref.at[t], turned.at[t], back.at[t]) for t in range(mine)
+    ]
+    for copy in arrivals + returns:
+        copy.start()
+    sums_ref[...] = sums_in[...]
+    back_ref[...] = jnp.zeros_like(back_ref)
+    for c in range(width):
+        arrivals[c].wait()
+        standardized(lambda rows: given[c, rows, :], into(geno, c), wide_values, samples)
+    for copy in returns:
+        copy.wait()
+
+    def add(c, y, inside=None):
+        weights = band_weights(rows_of(turned, y), columns_of(geno, c), inside)
+        sums_ref[:, cols_at(y)] += along_columns(given[c, samples:, :], weights)
+        back_ref[:, c * TILE : (c + 1) * TILE] += along_rows(
+            annot_ref[:, cols_at(n * mine + y)], weights
+        )
+
+    diagonal = (1 - 2 * n) * tile_offset() <= 0
+    for c in range(width):
+        add(c, c + (1 - n) * width, diagonal)
+        for y in range(mine):
+            first, second = y < c + width, c < y < width
+            if first or second:
+
+                @pl.when(True if first and second else (n == 0 if first else n == 1))
+                def _(c=c, y=y):
+                    add(c, y)
+
+
+def rim_sums(n, arrived, turned, annot, sums):
+    mine, chunks, _, _ = turned.shape
+    samples = chunks * LANES
+    width = mine // 2
+    return pl.pallas_call(
+        rim_kernel,
+        out_shape=(
+            jax.ShapeDtypeStruct(sums.shape, jnp.float32),
+            jax.ShapeDtypeStruct((sums.shape[0], width * TILE), jnp.float32),
+        ),
+        in_specs=[in_smem, in_place, in_place, in_vmem, in_vmem],
+        out_specs=(in_vmem, in_vmem),
         scratch_shapes=[
-            pltpu.VMEM((2 * mine, samples, TILE), jnp.bfloat16),
-            pltpu.VMEM((4 * mine, samples, LANES), jnp.bfloat16),
-            pltpu.VMEM((mine, chunks, TILE, LANES), jnp.bfloat16),
+            pltpu.VMEM((width, arrived.shape[0], TILE), jnp.bfloat16),
+            pltpu.VMEM((2 * width, samples, LANES), jnp.bfloat16),
+            pltpu.VMEM(turned.shape, jnp.bfloat16),
             pltpu.VMEM((samples, TILE), jnp.float32),
-            pltpu.SemaphoreType.DMA((2 * mine,)),
+            pltpu.SemaphoreType.DMA((width,)),
             pltpu.SemaphoreType.DMA((mine,)),
         ],
         cost_estimate=pl.CostEstimate(
-            flops=2 * samples * block * strip,
-            bytes_accessed=3 * samples * strip,
-            transcendentals=0,
-        ),
-        name="strip_sums",
-    )(n, dosage, annot)
-
-
-def rim_kernel(
-    order, n_ref, arrived_ref, turned_ref, annot_ref, sums_in, sums_ref, back_ref,
-    geno, turned, wide_values, came,
-):
-    mine = turned_ref.shape[0]
-    samples = geno.shape[1]
-    n = n_ref[0]
-    arrivals = [
-        pltpu.make_async_copy(turned_ref.at[t], turned.at[t], came.at[t]) for t in range(mine)
-    ]
-    for copy in arrivals:
-        copy.start()
-    standardized(lambda rows: arrived_ref[rows, :], into(geno, 0), wide_values, samples)
-    arrived_annot = arrived_ref[samples:, :]
-    sums_ref[...] = sums_in[...]
-    back_ref[...] = jnp.zeros_like(back_ref)
-    for copy in arrivals:
-        copy.wait()
-
-    def add(y, inside=None):
-        weights = band_weights(rows_of(turned, y), columns_of(geno, 0), inside)
-        sums_ref[:, cols_at(y)] += along_columns(arrived_annot, weights)
-        back_ref[...] += along_rows(annot_ref[:, cols_at(n * mine + y)], weights)
-
-    low, high = order, mine - 1 - order
-    add((1 - n) * high + n * low, (1 - 2 * n) * tile_offset() <= 0)
-    for y in range(mine):
-        first, second = y < high, low < y < mine // 2
-        if first or second:
-
-            @pl.when(True if first and second else (n == 0 if first else n == 1))
-            def _(y=y):
-                add(y)
-
-
-def rim_sums(order, n, arrived, turned, annot, sums):
-    mine, chunks, _, _ = turned.shape
-    samples = chunks * LANES
-    return pl.pallas_call(
-        functools.partial(rim_kernel, order),
-        out_shape=(
-            jax.ShapeDtypeStruct(sums.shape, jnp.float32),
-            jax.ShapeDtypeStruct((sums.shape[0], TILE), jnp.float32),
-        ),
-        in_specs=[in_smem, in_vmem, in_place, in_vmem, in_vmem],
-        out_specs=(in_vmem, in_vmem),
-        scratch_shapes=[
-            pltpu.VMEM((2, samples, LANES), jnp.bfloat16),
-            pltpu.VMEM(turned.shape, jnp.bfloat16),
-            pltpu.VMEM((samples, TILE), jnp.float32),
-            pltpu.SemaphoreType.DMA((mine,)),
-        ],
-        cost_estimate=pl.CostEstimate(
-            flops=2 * samples * TILE * mine * TILE,
-            bytes_accessed=2 * samples * TILE * (mine + 1),
+            flops=2 * samples * width * TILE * mine * TILE,
+            bytes_accessed=2 * samples * TILE * (mine + width),
             transcendentals=0,
         ),
         name="rim_sums",
@@ -297,14 +360,20 @@
     return jnp.sum(jnp.where(eye(size), jnp.broadcast_to(row, (size, size)), 0.0), axis=1, keepdims=True)
 
 
-def moments_kernel(total_variants, place_ref, counts_ref, sums_ref, first_ref, second_ref, scores_ref, payload_ref, whole):
+def lying(column):
+    size = column.shape[0]
+    return jnp.sum(
+        jnp.where(eye(size), jnp.broadcast_to(column, (size, size)), 0.0), axis=0, keepdims=True
+    )
+
+
+def moments_kernel(total_variants, place_ref, counts_ref, sums_ref, back_ref, scores_ref, payload_ref, whole):
     annots = counts_ref.shape[1]
     block = sums_ref.shape[1]
-    mine = block // TILE
+    width = back_ref.shape[1]
     n, slot = place_ref[0], place_ref[1]
     whole[...] = sums_ref[...]
-    for order, back_ref in enumerate((first_ref, second_ref)):
-        whole[:, cols_at((1 - n) * order + n * (mine - 1 - order))] += back_ref[...]
+    whole[:, pl.ds(pl.multiple_of(n * (block - width), width), width)] += back_ref[...]
     shares = upright(counts_ref[...]) / total_variants
     high = (1.0 - shares).astype(jnp.bfloat16).astype(jnp.float32)
     low = (0.0 - shares).astype(jnp.bfloat16).astype(jnp.float32)
@@ -322,16 +391,13 @@
         precision=highest_precision,
         preferred_element_type=jnp.float32,
     )
-    mean_row = jnp.sum(
-        jnp.where(eye(annots), jnp.broadcast_to(mean, (annots, annots)), 0.0), axis=0, keepdims=True
-    )
     slots = payload_ref.shape[0] - annots
     at = lax.broadcasted_iota(jnp.int32, (slots, annots), 0)
-    payload_ref[annots:, :] = jnp.where(at == slot, mean_row, 0.0)
+    payload_ref[annots:, :] = jnp.where(at == slot, lying(mean), 0.0)
 
 
 def moments_of(total_variants, slots, place, counts, sums, back):
-    annots = counts.shape[0]
+    annots = counts.shape[1]
     block = sums.shape[1]
     return pl.pallas_call(
         functools.partial(moments_kernel, total_variants),
@@ -339,15 +405,14 @@
             jax.ShapeDtypeStruct((annots + 2 * PAD, block), jnp.float32),
             jax.ShapeDtypeStruct((annots + slots, annots), jnp.float32),
         ),
-        in_specs=[in_smem] + [in_vmem] * 4,
+        in_specs=[in_smem] + [in_vmem] * 3,
         out_specs=(in_vmem, in_vmem),
         scratch_shapes=[pltpu.VMEM(sums.shape, jnp.float32)],
-        compiler_params=pltpu.CompilerParams(vmem_limit_bytes=VMEM_LIMIT),
         cost_estimate=pl.CostEstimate(
             flops=12 * annots * annots * block, bytes_accessed=12 * annots * block, transcendentals=0
         ),
         name="moments",
-    )(place, counts.reshape(1, annots), sums, *back)
+    )(place, counts, sums, back)
 
 
 def inverse_kernel(divisor, payload_ref, inverse_ref, moments_ref):
@@ -514,14 +579,22 @@
     return value
 
 
-def split_wide_sum(value):
+def split(value):
     half = value.shape[0] // 2
     low = lax.axis_index("wide") % 2
     kept = lax.dynamic_slice_in_dim(value, low * half, half, 0)
     given = lax.dynamic_slice_in_dim(value, (1 - low) * half, half, 0)
-    kept = kept + flipped(given, "wide", 1)
+    return kept + flipped(given, "wide", 1)
+
+
+def long_sum(value):
     for bit in wide_bits()[1:]:
-        kept = kept + flipped(kept, "wide", bit)
+        value = value + flipped(value, "wide", bit)
+    return value
+
+
+def joined(kept):
+    low = lax.axis_index("wide") % 2
     other = flipped(kept, "wide", 1)
     return jnp.where(
         low == 0, jnp.concatenate([kept, other], 0), jnp.concatenate([other, kept], 0)
@@ -538,48 +611,39 @@
     block = strip // 2
     n_array = jnp.reshape(n, (1,)).astype(jnp.int32)
 
-    annot = jnp.concatenate(
-        [
-            annotations.astype(jnp.bfloat16),
-            jnp.ones((1, strip), jnp.bfloat16),
-            jnp.zeros((PAD - 1, strip), jnp.bfloat16),
-        ],
-        axis=0,
-    )
     rim_pairs = []
     back_pairs = []
     for i in range(wide - 1):
         rim_pairs += [(2 * i, 2 * i + 2), (2 * i + 3, 2 * i + 1)]
         back_pairs += [(2 * i + 1, 2 * i + 2), (2 * i + 2, 2 * i + 1)]
-    arrived = []
-    for order in range(2):
-        outgoing = outgoing_columns(order, n_array, dosage, annotations)
-        arrived.append(lax.ppermute(outgoing, both, rim_pairs))
-    annotations, chi, _ = lax.optimization_barrier((annotations, test_statistic_table, outgoing))
-
-    chi_own = lax.dynamic_slice_in_dim(chi, n * block, block, 0)
-    chi_other = flipped(lax.dynamic_slice_in_dim(chi, (1 - n) * block, block, 0), "narrow", 1)
-    counts = wide_sum(jnp.sum(annotations, axis=1).astype(jnp.float32))
-
-    sums, turned = strip_sums(n_array, dosage, annot)
-    back = []
-    for order in range(2):
-        sums, part = rim_sums(order, n_array, arrived[order], turned, annot, sums)
-        back.append(lax.ppermute(part, both, back_pairs))
+    chi = test_statistic_table
+    outgoing, annot, counts, chi_given = prepared(n_array, dosage, annotations, chi)
+    arrived = lax.ppermute(outgoing, both, rim_pairs)
+    chi_other = flipped(chi_given, "narrow", 1)
+    counts = wide_sum(counts)
+    sums, turned = own_sums(n_array, dosage, annot)
+    sums = other_sums(n_array, dosage, annot, turned, sums)
+    sums, back = rim_sums(n_array, arrived, turned, annot, sums)
+    back = lax.ppermute(back, both, back_pairs)
 
     place = jnp.stack([n, 2 * w + n]).astype(jnp.int32)
     extended, payload = moments_of(total_variants, 2 * wide, place, counts, sums, back)
     scores = extended[:annots]
+    payload = split(payload)
     payload = payload + flipped(payload, "narrow", 1)
-    payload = split_wide_sum(payload)
-    proj_own, proj_other = (
+    payload = joined(long_sum(payload))
+
+    chi_own = lax.dynamic_slice_in_dim(chi, n * block, block, 0)
+    halves_of = [
         jnp.dot(
             extended, values, precision=lax.Precision.HIGH, preferred_element_type=jnp.float32
         )
-        for values in (chi_own, chi_other)
-    )
-    projection = proj_own + flipped(proj_other, "narrow", 1)
-    projection = split_wide_sum(projection)
+        for values in (chi_other, chi_own)
+    ]
+    projection = split(jnp.concatenate(halves_of, axis=1))
+    traits = chi.shape[1]
+    projection = projection[:, traits:] + flipped(projection[:, :traits], "narrow", 1)
+    projection = joined(long_sum(projection))
     scores_other = flipped(scores, "narrow", 1)
 
     inverse, moments = gram_inverse(total_variants, payload)

time: 112 us -> 108 us (0.964)
  starting transfers between devices: 36.9 us -> 25.7 us
  waiting for transfers between devices: 16.6 us -> 23.9 us
  local copies, waits for them, and re-layouts: 2.36 us -> 0.08 us
  Pallas kernels: 51.4 us -> 52.7 us
    ppermute x18, starting transfers between devices: 29 us -> 20.5 us  [flipped(): return lax.ppermute(value, axis, [(i, i ^ bit) for i in range(length)])]
    ppermute x18, waiting for transfers between devices: 16.6 us -> 23.8 us  [flipped(): return lax.ppermute(value, axis, [(i, i ^ bit) for i in range(length)])]
    ppermute x4 -> x2, starting transfers between devices: 7.88 us -> 5.23 us  [the longest x1 3.84 us: whole_step(): arrived = lax.ppermute(outgoing, both, rim_pairs)]
    pallas_call x1, Pallas kernels: 1.4 us -> 2.62 us  [moments_of(): pl.pallas_call(functools.partial(moments_kernel, total_variants), out_sha...]
    concatenate x1, other arithmetic: 1.17 us -> 0.02 us  [whole_step(): projection = split(jnp.concatenate(halves_of, axis=1))]
    dynamic_slice x3 -> x1, local copies, waits for them, and re-layouts: 1.15 us -> 0.01 us  [split(): given = lax.dynamic_slice_in_dim(value, (1 - low) * half, half, 0)]
    pallas_call x5 -> x4, Pallas kernels: 40.9 us -> 41 us  [the longest x1 13.1 us: other_sums(): pl.pallas_call(other_kernel, out_shape=jax.ShapeDtypeStruct(sums.shape, j...]
  transfers between devices with their start and end apart: 22 -> 20, of which waited for: 8 -> 11; matrix products, arithmetic and copies ran while one was open for 4% -> 3% of each run, Pallas kernels for 41% -> 43%
where the time goes in v1:
time: 108 us
  Pallas kernels  52.7 us (49%)
  starting transfers between devices  25.7 us (24%)
  waiting for transfers between devices  23.9 us (22%)
  matrix products  3.08 us (3%)
  other arithmetic  1.32 us (1%)
    ppermute x18, waiting for transfers between devices, flipped(): return lax.ppermute(value, axis, [(i, i ^ bit) for i in range(length)])  23.8 us
    ppermute x18, starting transfers between devices, flipped(): return lax.ppermute(value, axis, [(i, i ^ bit) for i in range(length)])  20.5 us
    pallas_call x1, Pallas kernels, other_sums(): pl.pallas_call(other_kernel, out_shape=jax.ShapeDtypeStruct(sums.shape, j...  13.1 us
    pallas_call x1, Pallas kernels, own_sums(): pl.pallas_call(own_kernel, out_shape=(jax.ShapeDtypeStruct((annot.shape[0...  13 us
    pallas_call x1, Pallas kernels, rim_sums(): pl.pallas_call(rim_kernel, out_shape=(jax.ShapeDtypeStruct(sums.shape, jn...  10.8 us
    pallas_call x1, Pallas kernels, gram_inverse(): pl.pallas_call(functools.partial(inverse_kernel, divisor), out_shape=(squ...  6.54 us
    pallas_call x1, Pallas kernels, prepared(): pl.pallas_call(prepare_kernel, out_shape=(jax.ShapeDtypeStruct((samples +...  4.11 us
    ppermute x1, starting transfers between devices, whole_step(): arrived = lax.ppermute(outgoing, both, rim_pairs)  3.84 us
  transfers between devices with their start and end apart: 20, of which 11 were waited for; matrix products, arithmetic and copies ran while one was open for 3% of the time, Pallas kernels for 43%

profile of v1, /device:TPU:0, one launch (start us, length us, event | category | flops | bytes accessed | tf_op | source)
XLA Modules:
  0.0 107.7 jit_solution(7030627265865483159)
XLA Ops:
  0.6 4.1 %prepare.1 = (bf16[2184,512]{1,0:T(8,128)(2,1)}, bf16[136,2048]{1,0:T(8,128)(2,1)}, f32[1,128]{1,0:T(1,128)}, f32[1024,256]{1,0:T(8,128)}) custom-call(s32[1]{0:T(128)} %bitcast.n_ref, bf16[2048,2048]{1,0:T(8,128)(2,1)} %dosage_ref.5, s32[128,2048]{1,0:T(8,128)} %annot_ref.1, f32[2048,256]{1,0:T(8,128)} %chi_ref.1), custom_call_target="tpu_custom_call" | custom-call | bytes 6291456 | tf_op jit(solution)/shard_map/prepare/pallas_call | solution.py:140
  4.8 3.8 %collective-permute-start.4 = (bf16[2184,512]{1,0:T(8,128)(2,1)}, bf16[2184,512]{1,0:T(8,128)(2,1)}, u32[]{:S(2)}, u32[]{:S(2)}) collective-permute-start(bf16[2184,512]{1,0:T(8,128)(2,1)} %get-tuple-element.15), channel_id=1, source_target_pairs={{0,2},{3,1},{2,4},{5,3},{4,6},{7,5},{6,8},{9,7},{8,10},{11,9},{10,... | collective-permute-start | bytes 6709256 | tf_op jit(solution)/shard_map/ppermute | solution.py:621
  8.6 0.5 collective-permute-start.12
  9.1 13.0 %own_sums.1 = (f32[136,1024]{1,0:T(8,128)}, bf16[4,16,256,128]{3,2,1,0:T(8,128)(2,1)}) custom-call(s32[1]{0:T(128)} %bitcast.n_ref, bf16[2048,2048]{1,0:T(8,128)(2,1)} %dosage_ref.5, bf16[136,2048]{1,0:T(8,128)(2,1)} %get-tuple-element.16.annot_ref), custom_call_target="tpu_custom_call" | custom-call | flops 4294967296 | bytes 8388608 | tf_op jit(solution)/shard_map/own_sums/pallas_call | solution.py:233
  22.1 13.1 %other_sums.1.sums_in = f32[136,1024]{1,0:T(8,128)} custom-call(s32[1]{0:T(128)} %bitcast.n_ref, bf16[2048,2048]{1,0:T(8,128)(2,1)} %dosage_ref.5, bf16[136,2048]{1,0:T(8,128)(2,1)} %get-tuple-element.16.annot_ref, bf16[4,16,256,128]{3,2,1,0:T(8,128)(2,1)} %get-tuple-element.17.turned_ref, f32[136,1024]{1,0:T(8,128)} %get-tuple-element.18.sums_in), custom_call_target="tpu_custom_call" | custom-call | flops 4294967296 | bytes 8388608 | tf_op jit(solution)/shard_map/other_sums/pallas_call | solution.py:248
  35.1 0.0 copy-start.1
  35.2 0.0 collective-permute-done.4.arrived_ref
  35.2 10.8 %rim_sums.1 = (f32[136,1024]{1,0:T(8,128)}, f32[136,512]{1,0:T(8,128)}) custom-call(s32[1]{0:T(128)} %bitcast.n_ref, bf16[2184,512]{1,0:T(8,128)(2,1)} %collective-permute-done.4.arrived_ref, bf16[4,16,256,128]{3,2,1,0:T(8,128)(2,1)} %get-tuple-element.17.turned_ref, bf16[136,2048]{1,0:T(8,128)(2,1)} %get-tuple-element.16.annot_ref, ...), custom_call_target="tpu_custom_call" | custom-call | flops 2147483648 | bytes 6291456 | tf_op jit(solution)/shard_map/rim_sums/pallas_call | solution.py:328
  46.0 1.4 %collective-permute-start.5 = (f32[136,512]{1,0:T(8,128)}, f32[136,512]{1,0:T(8,128)}, u32[]{:S(2)}, u32[]{:S(2)}) collective-permute-start(f32[136,512]{1,0:T(8,128)} %get-tuple-element.20), channel_id=1, source_target_pairs={{1,2},{2,1},{3,4},{4,3},{5,6},{6,5},{7,8},{8,7},{9,10},{10,9},{11,... | collective-permute-start | bytes 835592 | tf_op jit(solution)/shard_map/ppermute | solution.py:627
  47.4 1.5 %collective-permute-start = (f32[1,128]{1,0:T(1,128)S(1)}, f32[1,128]{1,0:T(1,128)S(1)}, u32[]{:S(2)}, u32[]{:S(2)}) collective-permute-start(f32[1,128]{1,0:T(1,128)S(1)} %copy-done.3), channel_id=1, source_target_pairs={{0,2},{2,0},{4,6},{6,4},{8,10},{10,8},{12,14},{14,12},{16,18},{18,... | collective-permute-start | bytes 1544 | tf_op jit(solution)/shard_map/ppermute | solution.py:563
  48.9 0.8 collective-permute-done
  49.7 1.6 %collective-permute-start.1 = (f32[1,128]{1,0:T(1,128)S(1)}, f32[1,128]{1,0:T(1,128)S(1)}, u32[]{:S(2)}, u32[]{:S(2)}) collective-permute-start(f32[1,128]{1,0:T(1,128)S(1)} %add.69), channel_id=1, source_target_pairs={{0,4},{2,6},{4,0},{6,2},{8,12},{10,14},{12,8},{14,10},{16,20},{18,... | collective-permute-start | bytes 1544 | tf_op jit(solution)/shard_map/ppermute | solution.py:563
  51.3 0.7 pad_add_fusion.place_ref
  52.0 2.9 %collective-permute-done.1 = f32[1,128]{1,0:T(1,128)S(1)} collective-permute-done((f32[1,128]{1,0:T(1,128)S(1)}, f32[1,128]{1,0:T(1,128)S(1)}, u32[]{:S(2)}, u32[]{:S(2)}) %collective-permute-start.1) | collective-permute-done | bytes 544 | tf_op jit(solution)/shard_map/ppermute | solution.py:563
  54.8 1.6 %collective-permute-start.2 = (f32[1,128]{1,0:T(1,128)S(1)}, f32[1,128]{1,0:T(1,128)S(1)}, u32[]{:S(2)}, u32[]{:S(2)}) collective-permute-start(f32[1,128]{1,0:T(1,128)S(1)} %add.70), channel_id=1, source_target_pairs={{0,8},{2,10},{4,12},{6,14},{8,0},{10,2},{12,4},{14,6},{16,24},{18,... | collective-permute-start | bytes 1544 | tf_op jit(solution)/shard_map/ppermute | solution.py:563
  56.4 2.0 %collective-permute-done.2 = f32[1,128]{1,0:T(1,128)S(1)} collective-permute-done((f32[1,128]{1,0:T(1,128)S(1)}, f32[1,128]{1,0:T(1,128)S(1)}, u32[]{:S(2)}, u32[]{:S(2)}) %collective-permute-start.2) | collective-permute-done | bytes 544 | tf_op jit(solution)/shard_map/ppermute | solution.py:563
  58.4 2.6 %collective-permute-start.3 = (f32[1,128]{1,0:T(1,128)S(1)}, f32[1,128]{1,0:T(1,128)S(1)}, u32[]{:S(2)}, u32[]{:S(2)}) collective-permute-start(f32[1,128]{1,0:T(1,128)S(1)} %add.71), channel_id=1, source_target_pairs={{0,16},{2,18},{4,20},{6,22},{8,24},{10,26},{12,28},{14,30},{16,0},... | collective-permute-start | bytes 1544 | tf_op jit(solution)/shard_map/ppermute | solution.py:563
  61.0 1.9 %collective-permute-done.3 = f32[1,128]{1,0:T(1,128)S(1)} collective-permute-done((f32[1,128]{1,0:T(1,128)S(1)}, f32[1,128]{1,0:T(1,128)S(1)}, u32[]{:S(2)}, u32[]{:S(2)}) %collective-permute-start.3) | collective-permute-done | bytes 544 | tf_op jit(solution)/shard_map/ppermute | solution.py:563
  62.9 0.5 add.72.counts_ref
  63.4 0.0 collective-permute-done.5.back_ref
  63.4 2.6 %moments.1 = (f32[144,1024]{1,0:T(8,128)}, f32[160,128]{1,0:T(8,128)}) custom-call(s32[2]{0:T(128)} %pad_add_fusion.place_ref, f32[1,128]{1,0:T(1,128)} %add.72.counts_ref, f32[136,1024]{1,0:T(8,128)} %get-tuple-element.19.sums_ref, f32[136,512]{1,0:T(8,128)} %collective-permute-done.5.back_ref), custom_call_target="tpu_custom_call" | custom-call | flops 201326592 | bytes 1572864 | tf_op jit(solution)/shard_map/moments/pallas_call | solution.py:402
  66.0 1.5 %fusion = f32[144,256]{1,0:T(8,128)S(1)} fusion(f32[144,1024]{1,0:T(8,128)} %get-tuple-element.24.scores_ref, f32[2048,256]{1,0:T(8,128)S(1)} %copy-done.1, s32[]{:T(128)S(6)} %select_n.50), kind=kOutput, calls=%fused_computation | convolution fusion | flops 226492416 | bytes 1785860 | tf_op jit(solution)/shard_map/dot_general | solution.py:638
  67.6 1.6 %fusion.6 = f32[144,256]{1,0:T(8,128)S(1)} fusion(f32[144,1024]{1,0:T(8,128)} %get-tuple-element.24.scores_ref, f32[1024,256]{1,0:T(8,128)S(1)} %collective-permute-done.12), kind=kOutput, calls=%fused_computation.16 | convolution fusion | flops 226492416 | bytes 1785856 | tf_op jit(solution)/shard_map/dot_general | solution.py:638
  69.2 0.1 collective-permute-start.13
  69.3 0.5 collective-permute-start.6
  69.8 0.9 collective-permute-done.13
  70.7 1.7 %collective-permute-start.14 = (f32[72,256]{1,0:T(8,128)S(1)}, f32[72,256]{1,0:T(8,128)S(1)}, u32[]{:S(2)}, u32[]{:S(2)}) collective-permute-start(f32[72,256]{1,0:T(8,128)S(1)} %slice.13), channel_id=1, source_target_pairs={{0,1},{1,0},{2,3},{3,2},{4,5},{5,4},{6,7},{7,6},{8,9},{9,8},{10,11... | collective-permute-start | bytes 221192 | tf_op jit(solution)/shard_map/ppermute | solution.py:563
  72.3 0.0 collective-permute-done.6
  72.3 0.5 collective-permute-start.7
  72.8 3.6 %collective-permute-done.7 = f32[80,128]{1,0:T(8,128)S(1)} collective-permute-done((f32[80,128]{1,0:T(8,128)S(1)}, f32[80,128]{1,0:T(8,128)S(1)}, u32[]{:S(2)}, u32[]{:S(2)}) %collective-permute-start.7) | collective-permute-done | bytes 40992 | tf_op jit(solution)/shard_map/ppermute | solution.py:563
  76.4 2.0 %collective-permute-start.8 = (f32[80,128]{1,0:T(8,128)S(1)}, f32[80,128]{1,0:T(8,128)S(1)}, u32[]{:S(2)}, u32[]{:S(2)}) collective-permute-start(f32[80,128]{1,0:T(8,128)S(1)} %add.76), channel_id=1, source_target_pairs={{0,4},{2,6},{4,0},{6,2},{8,12},{10,14},{12,8},{14,10},{16,20},{18,... | collective-permute-start | bytes 122888 | tf_op jit(solution)/shard_map/ppermute | solution.py:563
  78.4 0.0 collective-permute-done.14
  78.4 0.1 collective-permute-start.15
  78.5 2.3 %collective-permute-done.8 = f32[80,128]{1,0:T(8,128)S(1)} collective-permute-done((f32[80,128]{1,0:T(8,128)S(1)}, f32[80,128]{1,0:T(8,128)S(1)}, u32[]{:S(2)}, u32[]{:S(2)}) %collective-permute-start.8) | collective-permute-done | bytes 40992 | tf_op jit(solution)/shard_map/ppermute | solution.py:563
  80.8 1.6 %collective-permute-start.9 = (f32[80,128]{1,0:T(8,128)S(1)}, f32[80,128]{1,0:T(8,128)S(1)}, u32[]{:S(2)}, u32[]{:S(2)}) collective-permute-start(f32[80,128]{1,0:T(8,128)S(1)} %add.77), channel_id=1, source_target_pairs={{0,8},{2,10},{4,12},{6,14},{8,0},{10,2},{12,4},{14,6},{16,24},{18,... | collective-permute-start | bytes 122888 | tf_op jit(solution)/shard_map/ppermute | solution.py:563
  82.4 2.9 %collective-permute-done.9 = f32[80,128]{1,0:T(8,128)S(1)} collective-permute-done((f32[80,128]{1,0:T(8,128)S(1)}, f32[80,128]{1,0:T(8,128)S(1)}, u32[]{:S(2)}, u32[]{:S(2)}) %collective-permute-start.9) | collective-permute-done | bytes 40992 | tf_op jit(solution)/shard_map/ppermute | solution.py:563
  85.3 2.6 %collective-permute-start.10 = (f32[80,128]{1,0:T(8,128)S(1)}, f32[80,128]{1,0:T(8,128)S(1)}, u32[]{:S(2)}, u32[]{:S(2)}) collective-permute-start(f32[80,128]{1,0:T(8,128)S(1)} %add.78), channel_id=1, source_target_pairs={{0,16},{2,18},{4,20},{6,22},{8,24},{10,26},{12,28},{14,30},{16,0},... | collective-permute-start | bytes 122888 | tf_op jit(solution)/shard_map/ppermute | solution.py:563
  87.9 1.3 %collective-permute-start.16 = (f32[72,256]{1,0:T(8,128)S(1)}, f32[72,256]{1,0:T(8,128)S(1)}, u32[]{:S(2)}, u32[]{:S(2)}) collective-permute-start(f32[72,256]{1,0:T(8,128)S(1)} %add.85), channel_id=1, source_target_pairs={{0,8},{2,10},{4,12},{6,14},{8,0},{10,2},{12,4},{14,6},{16,24},{18,... | collective-permute-start | bytes 221192 | tf_op jit(solution)/shard_map/ppermute | solution.py:563
  89.2 1.0 collective-permute-done.10
  90.3 0.7 collective-permute-start.19
  91.0 1.3 %collective-permute-done.16 = f32[72,256]{1,0:T(8,128)S(1)} collective-permute-done((f32[72,256]{1,0:T(8,128)S(1)}, f32[72,256]{1,0:T(8,128)S(1)}, u32[]{:S(2)}, u32[]{:S(2)}) %collective-permute-start.16) | collective-permute-done | bytes 73760 | tf_op jit(solution)/shard_map/ppermute | solution.py:563
  92.3 1.7 %collective-permute-start.17 = (f32[72,256]{1,0:T(8,128)S(1)}, f32[72,256]{1,0:T(8,128)S(1)}, u32[]{:S(2)}, u32[]{:S(2)}) collective-permute-start(f32[72,256]{1,0:T(8,128)S(1)} %add.86), channel_id=1, source_target_pairs={{0,16},{2,18},{4,20},{6,22},{8,24},{10,26},{12,28},{14,30},{16,0},... | collective-permute-start | bytes 221192 | tf_op jit(solution)/shard_map/ppermute | solution.py:563
  94.0 0.0 collective-permute-done.11
  94.0 4.4 %collective-permute-done.17 = f32[72,256]{1,0:T(8,128)S(1)} collective-permute-done((f32[72,256]{1,0:T(8,128)S(1)}, f32[72,256]{1,0:T(8,128)S(1)}, u32[]{:S(2)}, u32[]{:S(2)}) %collective-permute-start.17) | collective-permute-done | bytes 73760 | tf_op jit(solution)/shard_map/ppermute | solution.py:563
  98.4 0.1 collective-permute-start.18
  98.5 6.5 %gram_inverse.1 = (f32[128,128]{1,0:T(8,128)S(1)}, f32[128,128]{1,0:T(8,128)S(1)}) custom-call(f32[160,128]{1,0:T(8,128)S(1)} %maximum_select_fusion.1.payload_ref), custom_call_target="tpu_custom_call" | custom-call | flops 20000000000 | bytes 65536 | tf_op jit(solution)/shard_map/gram_inverse/pallas_call | solution.py:494
  105.0 0.0 collective-permute-done.18
  105.1 2.6 %fitted_values.1 = (f32[128,1024]{1,0:T(8,128)}, f32[2048,256]{1,0:T(8,128)}) custom-call(s32[1]{0:T(128)} %bitcast.n_ref, f32[128,128]{1,0:T(8,128)S(1)} %get-tuple-element.22.inverse_ref, f32[128,128]{1,0:T(8,128)S(1)} %get-tuple-element.23.moments_ref, f32[144,256]{1,0:T(8,128)S(1)} %maximum_select_fusion.proj_ref, f32[144,1024]{1,0:T(8,128)S(1)} %copy-done, ...), custom_call_target="tpu_custom_call" | custom-call | flops 134217728 | bytes 2097152 | tf_op jit(solution)/shard_map/fitted_values/pallas_call | solution.py:545
  (30 shorter events, 0.2 us)
Async XLA Ops:
  4.8 30.4 %collective-permute-start.4 = (bf16[2184,512]{1,0:T(8,128)(2,1)}, bf16[2184,512]{1,0:T(8,128)(2,1)}, u32[]{:S(2)}, u32[]{:S(2)}) collective-permute-start(bf16[2184,512]{1,0:T(8,128)(2,1)} %get-tuple-element.15), channel_id=1, source_target_pairs={{0,2},{3,1},{2,4},{5,3},{4,6},{7,5},{6,8},{9,7},{8,10},{11,9},{10,... | collective-permute-start | bytes 6709256 | tf_op jit(solution)/shard_map/ppermute | solution.py:621
  8.6 59.0 %collective-permute-start.12 = (f32[1024,256]{1,0:T(8,128)}, f32[1024,256]{1,0:T(8,128)S(1)}, u32[]{:S(2)}, u32[]{:S(2)}) collective-permute-start(f32[1024,256]{1,0:T(8,128)} %get-tuple-element.25), channel_id=1, source_target_pairs={{0,1},{1,0},{2,3},{3,2},{4,5},{5,4},{6,7},{7,6},{8,9},{9,8},{10,11... | collective-permute-start | bytes 3145736 | tf_op jit(solution)/shard_map/ppermute | solution.py:563
  35.1 12.3 %copy-start.3 = (f32[1,128]{1,0:T(1,128)S(1)}, f32[1,128]{1,0:T(1,128)}, u32[]{:S(2)}) copy-start(f32[1,128]{1,0:T(1,128)} %get-tuple-element.14) | copy-start | bytes 1540
  35.1 30.9 %copy-start.1 = (f32[2048,256]{1,0:T(8,128)S(1)}, f32[2048,256]{1,0:T(8,128)}, u32[]{:S(2)}) copy-start(f32[2048,256]{1,0:T(8,128)} %chi_ref.1) | copy-start | bytes 6291460
  46.0 17.4 %collective-permute-start.5 = (f32[136,512]{1,0:T(8,128)}, f32[136,512]{1,0:T(8,128)}, u32[]{:S(2)}, u32[]{:S(2)}) collective-permute-start(f32[136,512]{1,0:T(8,128)} %get-tuple-element.20), channel_id=1, source_target_pairs={{1,2},{2,1},{3,4},{4,3},{5,6},{6,5},{7,8},{8,7},{9,10},{10,9},{11,... | collective-permute-start | bytes 835592 | tf_op jit(solution)/shard_map/ppermute | solution.py:627
  47.4 2.3 %collective-permute-start = (f32[1,128]{1,0:T(1,128)S(1)}, f32[1,128]{1,0:T(1,128)S(1)}, u32[]{:S(2)}, u32[]{:S(2)}) collective-permute-start(f32[1,128]{1,0:T(1,128)S(1)} %copy-done.3), channel_id=1, source_target_pairs={{0,2},{2,0},{4,6},{6,4},{8,10},{10,8},{12,14},{14,12},{16,18},{18,... | collective-permute-start | bytes 1544 | tf_op jit(solution)/shard_map/ppermute | solution.py:563
  49.7 5.1 %collective-permute-start.1 = (f32[1,128]{1,0:T(1,128)S(1)}, f32[1,128]{1,0:T(1,128)S(1)}, u32[]{:S(2)}, u32[]{:S(2)}) collective-permute-start(f32[1,128]{1,0:T(1,128)S(1)} %add.69), channel_id=1, source_target_pairs={{0,4},{2,6},{4,0},{6,2},{8,12},{10,14},{12,8},{14,10},{16,20},{18,... | collective-permute-start | bytes 1544 | tf_op jit(solution)/shard_map/ppermute | solution.py:563
  54.8 3.6 %collective-permute-start.2 = (f32[1,128]{1,0:T(1,128)S(1)}, f32[1,128]{1,0:T(1,128)S(1)}, u32[]{:S(2)}, u32[]{:S(2)}) collective-permute-start(f32[1,128]{1,0:T(1,128)S(1)} %add.70), channel_id=1, source_target_pairs={{0,8},{2,10},{4,12},{6,14},{8,0},{10,2},{12,4},{14,6},{16,24},{18,... | collective-permute-start | bytes 1544 | tf_op jit(solution)/shard_map/ppermute | solution.py:563
  58.4 4.5 %collective-permute-start.3 = (f32[1,128]{1,0:T(1,128)S(1)}, f32[1,128]{1,0:T(1,128)S(1)}, u32[]{:S(2)}, u32[]{:S(2)}) collective-permute-start(f32[1,128]{1,0:T(1,128)S(1)} %add.71), channel_id=1, source_target_pairs={{0,16},{2,18},{4,20},{6,22},{8,24},{10,26},{12,28},{14,30},{16,0},... | collective-permute-start | bytes 1544 | tf_op jit(solution)/shard_map/ppermute | solution.py:563
  66.0 3.3 %copy-start.2 = (f32[160,128]{1,0:T(8,128)S(1)}, f32[160,128]{1,0:T(8,128)}, u32[]{:S(2)}) copy-start(f32[160,128]{1,0:T(8,128)} %get-tuple-element.21) | copy-start | bytes 245764
  67.6 22.6 %copy-start = (f32[144,1024]{1,0:T(8,128)S(1)}, f32[144,1024]{1,0:T(8,128)}, u32[]{:S(2)}) copy-start(f32[144,1024]{1,0:T(8,128)} %get-tuple-element.24.scores_ref) | copy-start | bytes 1769476
  69.2 1.4 %collective-permute-start.13 = (f32[72,512]{1,0:T(8,128)S(1)}, f32[72,512]{1,0:T(8,128)S(1)}, u32[]{:S(2)}, u32[]{:S(2)}) collective-permute-start(f32[72,512]{1,0:T(8,128)S(1)} %fusion.2), channel_id=1, source_target_pairs={{0,2},{2,0},{4,6},{6,4},{8,10},{10,8},{12,14},{14,12},{16,18},{18,... | collective-permute-start | bytes 442376 | tf_op jit(solution)/shard_map/ppermute | solution.py:563
  69.3 3.0 %collective-permute-start.6 = (f32[80,128]{1,0:T(8,128)S(1)}, f32[80,128]{1,0:T(8,128)S(1)}, u32[]{:S(2)}, u32[]{:S(2)}) collective-permute-start(f32[80,128]{1,0:T(8,128)S(1)} %constant_dynamic-slice_fusion), channel_id=1, source_target_pairs={{0,2},{2,0},{4,6},{6,4},{8,10},{10,8},{12,14},{14,12},{16,18},{18,... | collective-permute-start | bytes 122888 | tf_op jit(solution)/shard_map/ppermute | solution.py:563
  70.7 7.8 %collective-permute-start.14 = (f32[72,256]{1,0:T(8,128)S(1)}, f32[72,256]{1,0:T(8,128)S(1)}, u32[]{:S(2)}, u32[]{:S(2)}) collective-permute-start(f32[72,256]{1,0:T(8,128)S(1)} %slice.13), channel_id=1, source_target_pairs={{0,1},{1,0},{2,3},{3,2},{4,5},{5,4},{6,7},{7,6},{8,9},{9,8},{10,11... | collective-permute-start | bytes 221192 | tf_op jit(solution)/shard_map/ppermute | solution.py:563
  72.3 4.1 %collective-permute-start.7 = (f32[80,128]{1,0:T(8,128)S(1)}, f32[80,128]{1,0:T(8,128)S(1)}, u32[]{:S(2)}, u32[]{:S(2)}) collective-permute-start(f32[80,128]{1,0:T(8,128)S(1)} %dynamic-slice_add_fusion), channel_id=1, source_target_pairs={{0,1},{1,0},{2,3},{3,2},{4,5},{5,4},{6,7},{7,6},{8,9},{9,8},{10,11... | collective-permute-start | bytes 122888 | tf_op jit(solution)/shard_map/ppermute | solution.py:563
  76.4 4.4 %collective-permute-start.8 = (f32[80,128]{1,0:T(8,128)S(1)}, f32[80,128]{1,0:T(8,128)S(1)}, u32[]{:S(2)}, u32[]{:S(2)}) collective-permute-start(f32[80,128]{1,0:T(8,128)S(1)} %add.76), channel_id=1, source_target_pairs={{0,4},{2,6},{4,0},{6,2},{8,12},{10,14},{12,8},{14,10},{16,20},{18,... | collective-permute-start | bytes 122888 | tf_op jit(solution)/shard_map/ppermute | solution.py:563
  78.4 9.4 %collective-permute-start.15 = (f32[72,256]{1,0:T(8,128)S(1)}, f32[72,256]{1,0:T(8,128)S(1)}, u32[]{:S(2)}, u32[]{:S(2)}) collective-permute-start(f32[72,256]{1,0:T(8,128)S(1)} %slice_add_fusion), channel_id=1, source_target_pairs={{0,4},{2,6},{4,0},{6,2},{8,12},{10,14},{12,8},{14,10},{16,20},{18,... | collective-permute-start | bytes 221192 | tf_op jit(solution)/shard_map/ppermute | solution.py:563
  80.8 4.4 %collective-permute-start.9 = (f32[80,128]{1,0:T(8,128)S(1)}, f32[80,128]{1,0:T(8,128)S(1)}, u32[]{:S(2)}, u32[]{:S(2)}) collective-permute-start(f32[80,128]{1,0:T(8,128)S(1)} %add.77), channel_id=1, source_target_pairs={{0,8},{2,10},{4,12},{6,14},{8,0},{10,2},{12,4},{14,6},{16,24},{18,... | collective-permute-start | bytes 122888 | tf_op jit(solution)/shard_map/ppermute | solution.py:563
  85.3 4.9 %collective-permute-start.10 = (f32[80,128]{1,0:T(8,128)S(1)}, f32[80,128]{1,0:T(8,128)S(1)}, u32[]{:S(2)}, u32[]{:S(2)}) collective-permute-start(f32[80,128]{1,0:T(8,128)S(1)} %add.78), channel_id=1, source_target_pairs={{0,16},{2,18},{4,20},{6,22},{8,24},{10,26},{12,28},{14,30},{16,0},... | collective-permute-start | bytes 122888 | tf_op jit(solution)/shard_map/ppermute | solution.py:563
  87.9 4.4 %collective-permute-start.16 = (f32[72,256]{1,0:T(8,128)S(1)}, f32[72,256]{1,0:T(8,128)S(1)}, u32[]{:S(2)}, u32[]{:S(2)}) collective-permute-start(f32[72,256]{1,0:T(8,128)S(1)} %add.85), channel_id=1, source_target_pairs={{0,8},{2,10},{4,12},{6,14},{8,0},{10,2},{12,4},{14,6},{16,24},{18,... | collective-permute-start | bytes 221192 | tf_op jit(solution)/shard_map/ppermute | solution.py:563
  90.2 3.8 %collective-permute-start.11 = (f32[80,128]{1,0:T(8,128)S(1)}, f32[80,128]{1,0:T(8,128)S(1)}, u32[]{:S(2)}, u32[]{:S(2)}) collective-permute-start(f32[80,128]{1,0:T(8,128)S(1)} %add.79), channel_id=1, source_target_pairs={{0,2},{2,0},{4,6},{6,4},{8,10},{10,8},{12,14},{14,12},{16,18},{18,... | collective-permute-start | bytes 122888 | tf_op jit(solution)/shard_map/ppermute | solution.py:563
  90.3 14.8 %collective-permute-start.19 = (f32[128,1024]{1,0:T(8,128)S(1)}, f32[128,1024]{1,0:T(8,128)S(1)}, u32[]{:S(2)}, u32[]{:S(2)}) collective-permute-start(f32[128,1024]{1,0:T(8,128)S(1)} %slice.11), channel_id=1, source_target_pairs={{0,1},{1,0},{2,3},{3,2},{4,5},{5,4},{6,7},{7,6},{8,9},{9,8},{10,11... | collective-permute-start | bytes 1572872 | tf_op jit(solution)/shard_map/ppermute | solution.py:563
  92.3 6.1 %collective-permute-start.17 = (f32[72,256]{1,0:T(8,128)S(1)}, f32[72,256]{1,0:T(8,128)S(1)}, u32[]{:S(2)}, u32[]{:S(2)}) collective-permute-start(f32[72,256]{1,0:T(8,128)S(1)} %add.86), channel_id=1, source_target_pairs={{0,16},{2,18},{4,20},{6,22},{8,24},{10,26},{12,28},{14,30},{16,0},... | collective-permute-start | bytes 221192 | tf_op jit(solution)/shard_map/ppermute | solution.py:563
  98.4 6.6 %collective-permute-start.18 = (f32[72,256]{1,0:T(8,128)S(1)}, f32[72,256]{1,0:T(8,128)S(1)}, u32[]{:S(2)}, u32[]{:S(2)}) collective-permute-start(f32[72,256]{1,0:T(8,128)S(1)} %add.87), channel_id=1, source_target_pairs={{0,2},{2,0},{4,6},{6,4},{8,10},{10,8},{12,14},{14,12},{16,18},{18,... | collective-permute-start | bytes 221192 | tf_op jit(solution)/shard_map/ppermute | solution.py:563

commit v2 on v1

--- a/solution.py
+++ b/solution.py
@@ -15,11 +15,12 @@
 PAD = 8
 PIVOTS = 4
 VMEM_LIMIT = 36 * 1024 * 1024
+WHOLE_VMEM = 67043328
 
 highest_precision = lax.Precision.HIGHEST
 both = ("wide", "narrow")
 in_vmem = pl.BlockSpec(memory_space=pltpu.VMEM)
-in_place = pl.BlockSpec(memory_space=pltpu.HBM)
+in_place = pl.BlockSpec(memory_space=pl.ANY)
 in_smem = pl.BlockSpec(memory_space=pltpu.SMEM)
 
 
@@ -166,11 +167,12 @@
     departures = [
         pltpu.make_async_copy(turned.at[t], turned_ref.at[t], went.at[t]) for t in range(mine)
     ]
-    for copy in arrivals:
-        copy.start()
+    arrivals[0].start()
     sums_ref[...] = jnp.zeros_like(sums_ref)
     for t in range(mine):
         arrivals[t].wait()
+        if t + 1 < mine:
+            arrivals[t + 1].start()
         standardized(lambda rows: given[t, rows, :], into(geno, t), wide_values, samples)
         for k in range(samples // LANES):
             for part in range(2):
@@ -193,36 +195,43 @@
 
 
 def other_kernel(
-    n_ref, dosage_ref, annot_ref, turned_ref, sums_in, sums_ref, given, geno, turned, wide_values, came, back
+    slots, n_ref, dosage_ref, annot_ref, turned_ref, sums_in, sums_ref,
+    given, geno, turned, wide_values, came, back,
 ):
     samples, strip = dosage_ref.shape
     mine = strip // (2 * TILE)
     n = n_ref[0]
+
+    def nearest(s):
+        return (1 - n) * s + n * (mine - 1 - s)
+
     arrivals = [
-        pltpu.make_async_copy(dosage_ref.at[:, cols_at((1 - n) * mine + t)], given.at[t], came.at[t])
-        for t in range(mine)
+        pltpu.make_async_copy(
+            dosage_ref.at[:, cols_at((1 - n) * mine + nearest(s))], given.at[s], came.at[s]
+        )
+        for s in slots
     ]
     returns = [
-        pltpu.make_async_copy(turned_ref.at[t], turned.at[t], back.at[t]) for t in range(mine)
-    ]
-    for copy in arrivals + returns:
-        copy.start()
+        pltpu.make_async_copy(turned_ref.at[nearest(h)], turned.at[h], back.at[h])
+        for h in range(slots[0], mine)
+    ]
+    arrivals[0].start()
     sums_ref[...] = sums_in[...]
-    for t in range(mine):
-        arrivals[t].wait()
-        standardized(lambda rows: given[t, rows, :], into(geno, t), wide_values, samples)
+    for i, s in enumerate(slots):
+        arrivals[i].wait()
+        for copy in [*arrivals, *returns][i + 1 : i + 2] if i + 1 < len(slots) else returns:
+            copy.start()
+        standardized(lambda rows: given[s, rows, :], into(geno, s), wide_values, samples)
     for copy in returns:
         copy.wait()
     inside = (1 - 2 * n) * tile_offset() >= 0
-    for high in range(mine):
-        for low in range(high + 1):
-            theirs = low + n * (high - low)
-            ours = high - n * (high - low)
+    for s in slots:
+        for h in range(s, mine):
             weights = band_weights(
-                rows_of(turned, ours), columns_of(geno, theirs), inside if low == high else None
+                rows_of(turned, h), columns_of(geno, s), inside if h == s else None
             )
-            sums_ref[:, cols_at(ours)] += along_columns(
-                annot_ref[:, cols_at((1 - n) * mine + theirs)], weights
+            sums_ref[:, cols_at(nearest(h))] += along_columns(
+                annot_ref[:, cols_at((1 - n) * mine + nearest(s))], weights
             )
 
 
@@ -244,14 +253,15 @@
     )(n, dosage, annot)
 
 
-def other_sums(n, dosage, annot, turned, sums):
+def other_sums(slots, n, dosage, annot, turned, sums):
     return pl.pallas_call(
-        other_kernel,
+        functools.partial(other_kernel, slots),
         out_shape=jax.ShapeDtypeStruct(sums.shape, jnp.float32),
         in_specs=[in_smem, in_place, in_vmem, in_place, in_vmem],
         out_specs=in_vmem,
         scratch_shapes=strip_scratch(dosage),
         cost_estimate=strip_cost(dosage),
+        compiler_params=pltpu.CompilerParams(vmem_limit_bytes=WHOLE_VMEM),
         name="other_sums",
     )(n, dosage, annot, turned, sums)
 
@@ -292,12 +302,13 @@
     returns = [
         pltpu.make_async_copy(turned_ref.at[t], turned.at[t], back.at[t]) for t in range(mine)
     ]
-    for copy in arrivals + returns:
-        copy.start()
+    arrivals[0].start()
     sums_ref[...] = sums_in[...]
     back_ref[...] = jnp.zeros_like(back_ref)
     for c in range(width):
         arrivals[c].wait()
+        for copy in arrivals[c + 1 : c + 2] if c + 1 < width else returns:
+            copy.start()
         standardized(lambda rows: given[c, rows, :], into(geno, c), wide_values, samples)
     for copy in returns:
         copy.wait()
@@ -367,11 +378,12 @@
     )
 
 
-def moments_kernel(total_variants, place_ref, counts_ref, sums_ref, back_ref, scores_ref, payload_ref, whole):
+def moments_kernel(total_variants, n_ref, w_ref, counts_ref, sums_ref, back_ref, scores_ref, payload_ref, whole):
     annots = counts_ref.shape[1]
     block = sums_ref.shape[1]
     width = back_ref.shape[1]
-    n, slot = place_ref[0], place_ref[1]
+    n = n_ref[0]
+    slot = 2 * w_ref[0] + n
     whole[...] = sums_ref[...]
     whole[:, pl.ds(pl.multiple_of(n * (block - width), width), width)] += back_ref[...]
     shares = upright(counts_ref[...]) / total_variants
@@ -396,7 +408,7 @@
     payload_ref[annots:, :] = jnp.where(at == slot, lying(mean), 0.0)
 
 
-def moments_of(total_variants, slots, place, counts, sums, back):
+def moments_of(total_variants, slots, n, w, counts, sums, back):
     annots = counts.shape[1]
     block = sums.shape[1]
     return pl.pallas_call(
@@ -405,14 +417,15 @@
             jax.ShapeDtypeStruct((annots + 2 * PAD, block), jnp.float32),
             jax.ShapeDtypeStruct((annots + slots, annots), jnp.float32),
         ),
-        in_specs=[in_smem] + [in_vmem] * 3,
+        in_specs=[in_smem] * 2 + [in_vmem] * 3,
         out_specs=(in_vmem, in_vmem),
         scratch_shapes=[pltpu.VMEM(sums.shape, jnp.float32)],
+        compiler_params=pltpu.CompilerParams(vmem_limit_bytes=VMEM_LIMIT),
         cost_estimate=pl.CostEstimate(
             flops=12 * annots * annots * block, bytes_accessed=12 * annots * block, transcendentals=0
         ),
         name="moments",
-    )(place, counts, sums, back)
+    )(n, w, counts, sums, back)
 
 
 def inverse_kernel(divisor, payload_ref, inverse_ref, moments_ref):
@@ -622,12 +635,16 @@
     chi_other = flipped(chi_given, "narrow", 1)
     counts = wide_sum(counts)
     sums, turned = own_sums(n_array, dosage, annot)
-    sums = other_sums(n_array, dosage, annot, turned, sums)
+    tiles = block // TILE
+    sums = other_sums(tuple(range(tiles // 2)), n_array, dosage, annot, turned, sums)
     sums, back = rim_sums(n_array, arrived, turned, annot, sums)
     back = lax.ppermute(back, both, back_pairs)
-
-    place = jnp.stack([n, 2 * w + n]).astype(jnp.int32)
-    extended, payload = moments_of(total_variants, 2 * wide, place, counts, sums, back)
+    sums = other_sums(tuple(range(tiles // 2, tiles)), n_array, dosage, annot, turned, sums)
+
+    w_array = jnp.reshape(w, (1,)).astype(jnp.int32)
+    extended, payload = moments_of(
+        total_variants, 2 * wide, n_array, w_array, counts, sums, back
+    )
     scores = extended[:annots]
     payload = split(payload)
     payload = payload + flipped(payload, "narrow", 1)

time: 108 us -> 119 us (1.10)
  Pallas kernels: 52.7 us -> 60.5 us
  starting transfers between devices: 25.7 us -> 31.7 us
  waiting for transfers between devices: 23.9 us -> 19 us
  local copies, waits for them, and re-layouts: 0.08 us -> 1.71 us
    pallas_call x1 -> x2, Pallas kernels: 13.1 us -> 19.6 us  [other_sums(): pl.pallas_call(functools.partial(other_kernel, slots), out_shape=jax.Shap...]
    ppermute x18, starting transfers between devices: 20.5 us -> 26.4 us  [flipped(): return lax.ppermute(value, axis, [(i, i ^ bit) for i in range(length)])]
    ppermute x18, waiting for transfers between devices: 23.8 us -> 19 us  [flipped(): return lax.ppermute(value, axis, [(i, i ^ bit) for i in range(length)])]
    unnamed x8 -> x4, local copies, waits for them, and re-layouts: 0.02 us -> 1.65 us
    pallas_call x1, Pallas kernels: 10.8 us -> 12 us  [rim_sums(): pl.pallas_call(rim_kernel, out_shape=(jax.ShapeDtypeStruct(sums.shape, jn...]
  transfers between devices with their start and end apart: 20 -> 20, of which waited for: 11 -> 9; matrix products, arithmetic and copies ran while one was open for 3% -> 3% of each run, Pallas kernels for 43% -> 45%
where the time goes in v2:
time: 119 us; the launch traced here: 118 us
  Pallas kernels  60.5 us (51%)
  starting transfers between devices  31.7 us (27%)
  waiting for transfers between devices  19 us (16%)
  matrix products  3.31 us (3%)
  local copies, waits for them, and re-layouts  1.71 us (1%)
  other arithmetic  1.33 us (1%)
    ppermute x18, starting transfers between devices, flipped(): return lax.ppermute(value, axis, [(i, i ^ bit) for i in range(length)])  26.4 us
    pallas_call x2, Pallas kernels, other_sums(): pl.pallas_call(functools.partial(other_kernel, slots), out_shape=jax.Shap...  19.6 us
    ppermute x18, waiting for transfers between devices, flipped(): return lax.ppermute(value, axis, [(i, i ^ bit) for i in range(length)])  19 us
    pallas_call x1, Pallas kernels, own_sums(): pl.pallas_call(own_kernel, out_shape=(jax.ShapeDtypeStruct((annot.shape[0...  13.8 us
    pallas_call x1, Pallas kernels, rim_sums(): pl.pallas_call(rim_kernel, out_shape=(jax.ShapeDtypeStruct(sums.shape, jn...  12 us
    pallas_call x1, Pallas kernels, gram_inverse(): pl.pallas_call(functools.partial(inverse_kernel, divisor), out_shape=(squ...  6.54 us
    pallas_call x1, Pallas kernels, prepared(): pl.pallas_call(prepare_kernel, out_shape=(jax.ShapeDtypeStruct((samples +...  4.11 us
    ppermute x1, starting transfers between devices, whole_step(): arrived = lax.ppermute(outgoing, both, rim_pairs)  3.85 us
  transfers between devices with their start and end apart: 20, of which 9 were waited for; matrix products, arithmetic and copies ran while one was open for 3% of the time, Pallas kernels for 45%

profile of v2, /device:TPU:0, one launch (start us, length us, event | category | flops | bytes accessed | tf_op | source)
XLA Modules:
  0.0 118.4 jit_solution(8256315230349965559)
XLA Ops:
  0.6 4.1 %prepare.1 = (bf16[2184,512]{1,0:T(8,128)(2,1)}, bf16[136,2048]{1,0:T(8,128)(2,1)}, f32[1,128]{1,0:T(1,128)}, f32[1024,256]{1,0:T(8,128)}) custom-call(s32[1]{0:T(128)} %bitcast.n_ref, bf16[2048,2048]{1,0:T(8,128)(2,1)} %dosage_ref.7, s32[128,2048]{1,0:T(8,128)} %annot_ref.1, f32[2048,256]{1,0:T(8,128)} %chi_ref.1), custom_call_target="tpu_custom_call" | custom-call | bytes 6291456 | tf_op jit(solution)/shard_map/prepare/pallas_call | solution.py:141
  4.8 3.9 %collective-permute-start.4 = (bf16[2184,512]{1,0:T(8,128)(2,1)}, bf16[2184,512]{1,0:T(8,128)(2,1)}, u32[]{:S(2)}, u32[]{:S(2)}) collective-permute-start(bf16[2184,512]{1,0:T(8,128)(2,1)} %get-tuple-element.17), channel_id=1, source_target_pairs={{0,2},{3,1},{2,4},{5,3},{4,6},{7,5},{6,8},{9,7},{8,10},{11,9},{10,... | collective-permute-start | bytes 6709256 | tf_op jit(solution)/shard_map/ppermute | solution.py:634
  8.6 1.2 %collective-permute-start = (f32[1,128]{1,0:T(1,128)}, f32[1,128]{1,0:T(1,128)}, u32[]{:S(2)}, u32[]{:S(2)}) collective-permute-start(f32[1,128]{1,0:T(1,128)} %get-tuple-element.14), channel_id=1, source_target_pairs={{0,2},{2,0},{4,6},{6,4},{8,10},{10,8},{12,14},{14,12},{16,18},{18,... | collective-permute-start | bytes 1544 | tf_op jit(solution)/shard_map/ppermute | solution.py:576
  9.8 0.4 collective-permute-start.12
  10.2 13.8 %own_sums.1 = (f32[136,1024]{1,0:T(8,128)}, bf16[4,16,256,128]{3,2,1,0:T(8,128)(2,1)}) custom-call(s32[1]{0:T(128)} %bitcast.n_ref, bf16[2048,2048]{1,0:T(8,128)(2,1)} %dosage_ref.7, bf16[136,2048]{1,0:T(8,128)(2,1)} %get-tuple-element.15.annot_ref), custom_call_target="tpu_custom_call" | custom-call | flops 4294967296 | bytes 8388608 | tf_op jit(solution)/shard_map/own_sums/pallas_call | solution.py:242
  24.1 11.5 %other_sums.2.sums_in = f32[136,1024]{1,0:T(8,128)} custom-call(s32[1]{0:T(128)} %bitcast.n_ref, bf16[2048,2048]{1,0:T(8,128)(2,1)} %dosage_ref.7, bf16[136,2048]{1,0:T(8,128)(2,1)} %get-tuple-element.15.annot_ref, bf16[4,16,256,128]{3,2,1,0:T(8,128)(2,1)} %get-tuple-element.16.turned_ref, f32[136,1024]{1,0:T(8,128)} %get-tuple-element.18.sums_in), custom_call_target="tpu_custom_call" | custom-call | flops 4294967296 | bytes 8388608 | tf_op jit(solution)/shard_map/other_sums/pallas_call | solution.py:257
  35.6 0.7 add.65
  36.3 1.5 %collective-permute-start.1 = (f32[1,128]{1,0:T(1,128)S(1)}, f32[1,128]{1,0:T(1,128)S(1)}, u32[]{:S(2)}, u32[]{:S(2)}) collective-permute-start(f32[1,128]{1,0:T(1,128)S(1)} %add.65), channel_id=1, source_target_pairs={{0,4},{2,6},{4,0},{6,2},{8,12},{10,14},{12,8},{14,10},{16,20},{18,... | collective-permute-start | bytes 1544 | tf_op jit(solution)/shard_map/ppermute | solution.py:576
  37.8 2.1 %collective-permute-done.1 = f32[1,128]{1,0:T(1,128)S(1)} collective-permute-done((f32[1,128]{1,0:T(1,128)S(1)}, f32[1,128]{1,0:T(1,128)S(1)}, u32[]{:S(2)}, u32[]{:S(2)}) %collective-permute-start.1) | collective-permute-done | bytes 544 | tf_op jit(solution)/shard_map/ppermute | solution.py:576
  39.9 2.0 %collective-permute-start.2 = (f32[1,128]{1,0:T(1,128)S(1)}, f32[1,128]{1,0:T(1,128)S(1)}, u32[]{:S(2)}, u32[]{:S(2)}) collective-permute-start(f32[1,128]{1,0:T(1,128)S(1)} %add.66), channel_id=1, source_target_pairs={{0,8},{2,10},{4,12},{6,14},{8,0},{10,2},{12,4},{14,6},{16,24},{18,... | collective-permute-start | bytes 1544 | tf_op jit(solution)/shard_map/ppermute | solution.py:576
  41.8 1.6 %collective-permute-done.2 = f32[1,128]{1,0:T(1,128)S(1)} collective-permute-done((f32[1,128]{1,0:T(1,128)S(1)}, f32[1,128]{1,0:T(1,128)S(1)}, u32[]{:S(2)}, u32[]{:S(2)}) %collective-permute-start.2) | collective-permute-done | bytes 544 | tf_op jit(solution)/shard_map/ppermute | solution.py:576
  43.5 3.0 %collective-permute-start.3 = (f32[1,128]{1,0:T(1,128)S(1)}, f32[1,128]{1,0:T(1,128)S(1)}, u32[]{:S(2)}, u32[]{:S(2)}) collective-permute-start(f32[1,128]{1,0:T(1,128)S(1)} %add.67), channel_id=1, source_target_pairs={{0,16},{2,18},{4,20},{6,22},{8,24},{10,26},{12,28},{14,30},{16,0},... | collective-permute-start | bytes 1544 | tf_op jit(solution)/shard_map/ppermute | solution.py:576
  46.4 1.5 %collective-permute-done.3 = f32[1,128]{1,0:T(1,128)S(1)} collective-permute-done((f32[1,128]{1,0:T(1,128)S(1)}, f32[1,128]{1,0:T(1,128)S(1)}, u32[]{:S(2)}, u32[]{:S(2)}) %collective-permute-start.3) | collective-permute-done | bytes 544 | tf_op jit(solution)/shard_map/ppermute | solution.py:576
  48.0 0.5 add.68.counts_ref
  48.5 12.0 %rim_sums.1 = (f32[136,1024]{1,0:T(8,128)}, f32[136,512]{1,0:T(8,128)}) custom-call(s32[1]{0:T(128)} %bitcast.n_ref, bf16[2184,512]{1,0:T(8,128)(2,1)} %collective-permute-done.4.arrived_ref, bf16[4,16,256,128]{3,2,1,0:T(8,128)(2,1)} %get-tuple-element.16.turned_ref, bf16[136,2048]{1,0:T(8,128)(2,1)} %get-tuple-element.15.annot_ref, ...), custom_call_target="tpu_custom_call" | custom-call | flops 2147483648 | bytes 6291456 | tf_op jit(solution)/shard_map/rim_sums/pallas_call | solution.py:339
  60.6 1.4 %collective-permute-start.5 = (f32[136,512]{1,0:T(8,128)}, f32[136,512]{1,0:T(8,128)}, u32[]{:S(2)}, u32[]{:S(2)}) collective-permute-start(f32[136,512]{1,0:T(8,128)} %get-tuple-element.20), channel_id=1, source_target_pairs={{1,2},{2,1},{3,4},{4,3},{5,6},{6,5},{7,8},{8,7},{9,10},{10,9},{11,... | collective-permute-start | bytes 835592 | tf_op jit(solution)/shard_map/ppermute | solution.py:641
  61.9 8.1 %other_sums.3.sums_ref = f32[136,1024]{1,0:T(8,128)} custom-call(s32[1]{0:T(128)} %bitcast.n_ref, bf16[2048,2048]{1,0:T(8,128)(2,1)} %dosage_ref.7, bf16[136,2048]{1,0:T(8,128)(2,1)} %get-tuple-element.15.annot_ref, bf16[4,16,256,128]{3,2,1,0:T(8,128)(2,1)} %get-tuple-element.16.turned_ref, f32[136,1024]{1,0:T(8,128)} %get-tuple-element.19.sums_in), custom_call_target="tpu_custom_call" | custom-call | flops 4294967296 | bytes 8388608 | tf_op jit(solution)/shard_map/other_sums/pallas_call | solution.py:257
  70.1 0.0 collective-permute-done.5.back_ref
  70.1 1.0 copy-done
  71.1 0.6 copy-done.1
  71.7 1.8 %moments.1 = (f32[144,1024]{1,0:T(8,128)S(1)}, f32[160,128]{1,0:T(8,128)S(1)}) custom-call(s32[1]{0:T(128)} %bitcast.n_ref, s32[1]{0:T(128)} %bitcast.1.w_ref, f32[1,128]{1,0:T(1,128)S(1)} %copy-done.1, f32[136,1024]{1,0:T(8,128)S(1)} %copy-done, f32[136,512]{1,0:T(8,128)} %collective-permute-done.5.back_ref), custom_call_target="tpu_custom_call" | custom-call | flops 201326592 | bytes 1572864 | tf_op jit(solution)/shard_map/moments/pallas_call | solution.py:414
  73.5 1.7 %fusion = f32[144,256]{1,0:T(8,128)S(1)} fusion(f32[144,1024]{1,0:T(8,128)S(1)} %get-tuple-element.24.scores_ref, f32[2048,256]{1,0:T(8,128)} %chi_ref.1, s32[]{:T(128)S(6)} %select_n.50), kind=kOutput, calls=%fused_computation | convolution fusion | flops 226492416 | bytes 1785860 | tf_op jit(solution)/shard_map/dot_general | solution.py:655
  75.2 0.0 collective-permute-done.12
  75.2 1.7 %fusion.6 = f32[144,256]{1,0:T(8,128)S(1)} fusion(f32[144,1024]{1,0:T(8,128)S(1)} %get-tuple-element.24.scores_ref, f32[1024,256]{1,0:T(8,128)} %collective-permute-done.12), kind=kOutput, calls=%fused_computation.15 | convolution fusion | flops 226492416 | bytes 1785856 | tf_op jit(solution)/shard_map/dot_general | solution.py:655
  76.9 0.1 collective-permute-start.13
  77.0 0.5 collective-permute-start.6
  77.5 0.9 collective-permute-done.13
  78.4 4.0 %collective-permute-start.14 = (f32[72,256]{1,0:T(8,128)S(1)}, f32[72,256]{1,0:T(8,128)S(1)}, u32[]{:S(2)}, u32[]{:S(2)}) collective-permute-start(f32[72,256]{1,0:T(8,128)S(1)} %slice.13), channel_id=1, source_target_pairs={{0,1},{1,0},{2,3},{3,2},{4,5},{5,4},{6,7},{7,6},{8,9},{9,8},{10,11... | collective-permute-start | bytes 221192 | tf_op jit(solution)/shard_map/ppermute | solution.py:576
  82.4 0.0 collective-permute-done.6
  82.4 0.2 collective-permute-start.7
  82.6 3.9 %collective-permute-done.7 = f32[80,128]{1,0:T(8,128)S(1)} collective-permute-done((f32[80,128]{1,0:T(8,128)S(1)}, f32[80,128]{1,0:T(8,128)S(1)}, u32[]{:S(2)}, u32[]{:S(2)}) %collective-permute-start.7) | collective-permute-done | bytes 40992 | tf_op jit(solution)/shard_map/ppermute | solution.py:576
  86.5 1.5 %collective-permute-start.8 = (f32[80,128]{1,0:T(8,128)S(1)}, f32[80,128]{1,0:T(8,128)S(1)}, u32[]{:S(2)}, u32[]{:S(2)}) collective-permute-start(f32[80,128]{1,0:T(8,128)S(1)} %add.72), channel_id=1, source_target_pairs={{0,4},{2,6},{4,0},{6,2},{8,12},{10,14},{12,8},{14,10},{16,20},{18,... | collective-permute-start | bytes 122888 | tf_op jit(solution)/shard_map/ppermute | solution.py:576
  88.0 0.6 collective-permute-start.15
  88.6 2.0 %collective-permute-done.8 = f32[80,128]{1,0:T(8,128)S(1)} collective-permute-done((f32[80,128]{1,0:T(8,128)S(1)}, f32[80,128]{1,0:T(8,128)S(1)}, u32[]{:S(2)}, u32[]{:S(2)}) %collective-permute-start.8) | collective-permute-done | bytes 40992 | tf_op jit(solution)/shard_map/ppermute | solution.py:576
  90.6 2.0 %collective-permute-start.9 = (f32[80,128]{1,0:T(8,128)S(1)}, f32[80,128]{1,0:T(8,128)S(1)}, u32[]{:S(2)}, u32[]{:S(2)}) collective-permute-start(f32[80,128]{1,0:T(8,128)S(1)} %add.73), channel_id=1, source_target_pairs={{0,8},{2,10},{4,12},{6,14},{8,0},{10,2},{12,4},{14,6},{16,24},{18,... | collective-permute-start | bytes 122888 | tf_op jit(solution)/shard_map/ppermute | solution.py:576
  92.5 2.0 %collective-permute-done.9 = f32[80,128]{1,0:T(8,128)S(1)} collective-permute-done((f32[80,128]{1,0:T(8,128)S(1)}, f32[80,128]{1,0:T(8,128)S(1)}, u32[]{:S(2)}, u32[]{:S(2)}) %collective-permute-start.9) | collective-permute-done | bytes 40992 | tf_op jit(solution)/shard_map/ppermute | solution.py:576
  94.6 3.2 %collective-permute-start.10 = (f32[80,128]{1,0:T(8,128)S(1)}, f32[80,128]{1,0:T(8,128)S(1)}, u32[]{:S(2)}, u32[]{:S(2)}) collective-permute-start(f32[80,128]{1,0:T(8,128)S(1)} %add.74), channel_id=1, source_target_pairs={{0,16},{2,18},{4,20},{6,22},{8,24},{10,26},{12,28},{14,30},{16,0},... | collective-permute-start | bytes 122888 | tf_op jit(solution)/shard_map/ppermute | solution.py:576
  97.8 0.0 collective-permute-done.15
  97.8 2.1 %collective-permute-start.16 = (f32[72,256]{1,0:T(8,128)S(1)}, f32[72,256]{1,0:T(8,128)S(1)}, u32[]{:S(2)}, u32[]{:S(2)}) collective-permute-start(f32[72,256]{1,0:T(8,128)S(1)} %add.81), channel_id=1, source_target_pairs={{0,8},{2,10},{4,12},{6,14},{8,0},{10,2},{12,4},{14,6},{16,24},{18,... | collective-permute-start | bytes 221192 | tf_op jit(solution)/shard_map/ppermute | solution.py:576
  99.9 0.0 collective-permute-done.10
  99.9 0.1 collective-permute-start.11
  100.1 1.6 %collective-permute-start.19 = (f32[128,1024]{1,0:T(8,128)S(1)}, f32[128,1024]{1,0:T(8,128)S(1)}, u32[]{:S(2)}, u32[]{:S(2)}) collective-permute-start(f32[128,1024]{1,0:T(8,128)S(1)} %slice.11), channel_id=1, source_target_pairs={{0,1},{1,0},{2,3},{3,2},{4,5},{5,4},{6,7},{7,6},{8,9},{9,8},{10,11... | collective-permute-start | bytes 1572872 | tf_op jit(solution)/shard_map/ppermute | solution.py:576
  101.7 0.6 collective-permute-done.16
  102.3 2.5 %collective-permute-start.17 = (f32[72,256]{1,0:T(8,128)S(1)}, f32[72,256]{1,0:T(8,128)S(1)}, u32[]{:S(2)}, u32[]{:S(2)}) collective-permute-start(f32[72,256]{1,0:T(8,128)S(1)} %add.82), channel_id=1, source_target_pairs={{0,16},{2,18},{4,20},{6,22},{8,24},{10,26},{12,28},{14,30},{16,0},... | collective-permute-start | bytes 221192 | tf_op jit(solution)/shard_map/ppermute | solution.py:576
  104.8 4.4 %collective-permute-done.17 = f32[72,256]{1,0:T(8,128)S(1)} collective-permute-done((f32[72,256]{1,0:T(8,128)S(1)}, f32[72,256]{1,0:T(8,128)S(1)}, u32[]{:S(2)}, u32[]{:S(2)}) %collective-permute-start.17) | collective-permute-done | bytes 73760 | tf_op jit(solution)/shard_map/ppermute | solution.py:576
  109.2 0.1 collective-permute-start.18
  109.3 6.5 %gram_inverse.1 = (f32[128,128]{1,0:T(8,128)S(1)}, f32[128,128]{1,0:T(8,128)S(1)}) custom-call(f32[160,128]{1,0:T(8,128)S(1)} %maximum_select_fusion.1.payload_ref), custom_call_target="tpu_custom_call" | custom-call | flops 20000000000 | bytes 65536 | tf_op jit(solution)/shard_map/gram_inverse/pallas_call | solution.py:507
  115.8 2.6 %fitted_values.1 = (f32[128,1024]{1,0:T(8,128)}, f32[2048,256]{1,0:T(8,128)}) custom-call(s32[1]{0:T(128)} %bitcast.n_ref, f32[128,128]{1,0:T(8,128)S(1)} %get-tuple-element.22.inverse_ref, f32[128,128]{1,0:T(8,128)S(1)} %get-tuple-element.23.moments_ref, f32[144,256]{1,0:T(8,128)S(1)} %maximum_select_fusion.proj_ref, ...), custom_call_target="tpu_custom_call" | custom-call | flops 134217728 | bytes 2097152 | tf_op jit(solution)/shard_map/fitted_values/pallas_call | solution.py:558
  (26 shorter events, 0.2 us)
Async XLA Ops:
  4.8 43.8 %collective-permute-start.4 = (bf16[2184,512]{1,0:T(8,128)(2,1)}, bf16[2184,512]{1,0:T(8,128)(2,1)}, u32[]{:S(2)}, u32[]{:S(2)}) collective-permute-start(bf16[2184,512]{1,0:T(8,128)(2,1)} %get-tuple-element.17), channel_id=1, source_target_pairs={{0,2},{3,1},{2,4},{5,3},{4,6},{7,5},{6,8},{9,7},{8,10},{11,9},{10,... | collective-permute-start | bytes 6709256 | tf_op jit(solution)/shard_map/ppermute | solution.py:634
  8.6 27.0 %collective-permute-start = (f32[1,128]{1,0:T(1,128)}, f32[1,128]{1,0:T(1,128)}, u32[]{:S(2)}, u32[]{:S(2)}) collective-permute-start(f32[1,128]{1,0:T(1,128)} %get-tuple-element.14), channel_id=1, source_target_pairs={{0,2},{2,0},{4,6},{6,4},{8,10},{10,8},{12,14},{14,12},{16,18},{18,... | collective-permute-start | bytes 1544 | tf_op jit(solution)/shard_map/ppermute | solution.py:576
  9.8 65.4 %collective-permute-start.12 = (f32[1024,256]{1,0:T(8,128)}, f32[1024,256]{1,0:T(8,128)}, u32[]{:S(2)}, u32[]{:S(2)}) collective-permute-start(f32[1024,256]{1,0:T(8,128)} %get-tuple-element.25), channel_id=1, source_target_pairs={{0,1},{1,0},{2,3},{3,2},{4,5},{5,4},{6,7},{7,6},{8,9},{9,8},{10,11... | collective-permute-start | bytes 3145736 | tf_op jit(solution)/shard_map/ppermute | solution.py:576
  36.3 3.6 %collective-permute-start.1 = (f32[1,128]{1,0:T(1,128)S(1)}, f32[1,128]{1,0:T(1,128)S(1)}, u32[]{:S(2)}, u32[]{:S(2)}) collective-permute-start(f32[1,128]{1,0:T(1,128)S(1)} %add.65), channel_id=1, source_target_pairs={{0,4},{2,6},{4,0},{6,2},{8,12},{10,14},{12,8},{14,10},{16,20},{18,... | collective-permute-start | bytes 1544 | tf_op jit(solution)/shard_map/ppermute | solution.py:576
  39.9 3.6 %collective-permute-start.2 = (f32[1,128]{1,0:T(1,128)S(1)}, f32[1,128]{1,0:T(1,128)S(1)}, u32[]{:S(2)}, u32[]{:S(2)}) collective-permute-start(f32[1,128]{1,0:T(1,128)S(1)} %add.66), channel_id=1, source_target_pairs={{0,8},{2,10},{4,12},{6,14},{8,0},{10,2},{12,4},{14,6},{16,24},{18,... | collective-permute-start | bytes 1544 | tf_op jit(solution)/shard_map/ppermute | solution.py:576
  43.5 4.5 %collective-permute-start.3 = (f32[1,128]{1,0:T(1,128)S(1)}, f32[1,128]{1,0:T(1,128)S(1)}, u32[]{:S(2)}, u32[]{:S(2)}) collective-permute-start(f32[1,128]{1,0:T(1,128)S(1)} %add.67), channel_id=1, source_target_pairs={{0,16},{2,18},{4,20},{6,22},{8,24},{10,26},{12,28},{14,30},{16,0},... | collective-permute-start | bytes 1544 | tf_op jit(solution)/shard_map/ppermute | solution.py:576
  60.6 9.5 %collective-permute-start.5 = (f32[136,512]{1,0:T(8,128)}, f32[136,512]{1,0:T(8,128)}, u32[]{:S(2)}, u32[]{:S(2)}) collective-permute-start(f32[136,512]{1,0:T(8,128)} %get-tuple-element.20), channel_id=1, source_target_pairs={{1,2},{2,1},{3,4},{4,3},{5,6},{6,5},{7,8},{8,7},{9,10},{10,9},{11,... | collective-permute-start | bytes 835592 | tf_op jit(solution)/shard_map/ppermute | solution.py:641
  70.1 1.1 copy-start
  71.1 0.6 copy-start.1
  76.9 1.4 %collective-permute-start.13 = (f32[72,512]{1,0:T(8,128)S(1)}, f32[72,512]{1,0:T(8,128)S(1)}, u32[]{:S(2)}, u32[]{:S(2)}) collective-permute-start(f32[72,512]{1,0:T(8,128)S(1)} %fusion.2), channel_id=1, source_target_pairs={{0,2},{2,0},{4,6},{6,4},{8,10},{10,8},{12,14},{14,12},{16,18},{18,... | collective-permute-start | bytes 442376 | tf_op jit(solution)/shard_map/ppermute | solution.py:576
  77.0 5.4 %collective-permute-start.6 = (f32[80,128]{1,0:T(8,128)S(1)}, f32[80,128]{1,0:T(8,128)S(1)}, u32[]{:S(2)}, u32[]{:S(2)}) collective-permute-start(f32[80,128]{1,0:T(8,128)S(1)} %constant_dynamic-slice_fusion), channel_id=1, source_target_pairs={{0,2},{2,0},{4,6},{6,4},{8,10},{10,8},{12,14},{14,12},{16,18},{18,... | collective-permute-start | bytes 122888 | tf_op jit(solution)/shard_map/ppermute | solution.py:576
  78.4 9.6 %collective-permute-start.14 = (f32[72,256]{1,0:T(8,128)S(1)}, f32[72,256]{1,0:T(8,128)S(1)}, u32[]{:S(2)}, u32[]{:S(2)}) collective-permute-start(f32[72,256]{1,0:T(8,128)S(1)} %slice.13), channel_id=1, source_target_pairs={{0,1},{1,0},{2,3},{3,2},{4,5},{5,4},{6,7},{7,6},{8,9},{9,8},{10,11... | collective-permute-start | bytes 221192 | tf_op jit(solution)/shard_map/ppermute | solution.py:576
  82.4 4.1 %collective-permute-start.7 = (f32[80,128]{1,0:T(8,128)S(1)}, f32[80,128]{1,0:T(8,128)S(1)}, u32[]{:S(2)}, u32[]{:S(2)}) collective-permute-start(f32[80,128]{1,0:T(8,128)S(1)} %dynamic-slice_add_fusion), channel_id=1, source_target_pairs={{0,1},{1,0},{2,3},{3,2},{4,5},{5,4},{6,7},{7,6},{8,9},{9,8},{10,11... | collective-permute-start | bytes 122888 | tf_op jit(solution)/shard_map/ppermute | solution.py:576
  86.5 4.1 %collective-permute-start.8 = (f32[80,128]{1,0:T(8,128)S(1)}, f32[80,128]{1,0:T(8,128)S(1)}, u32[]{:S(2)}, u32[]{:S(2)}) collective-permute-start(f32[80,128]{1,0:T(8,128)S(1)} %add.72), channel_id=1, source_target_pairs={{0,4},{2,6},{4,0},{6,2},{8,12},{10,14},{12,8},{14,10},{16,20},{18,... | collective-permute-start | bytes 122888 | tf_op jit(solution)/shard_map/ppermute | solution.py:576
  88.0 9.8 %collective-permute-start.15 = (f32[72,256]{1,0:T(8,128)S(1)}, f32[72,256]{1,0:T(8,128)S(1)}, u32[]{:S(2)}, u32[]{:S(2)}) collective-permute-start(f32[72,256]{1,0:T(8,128)S(1)} %slice_add_fusion), channel_id=1, source_target_pairs={{0,4},{2,6},{4,0},{6,2},{8,12},{10,14},{12,8},{14,10},{16,20},{18,... | collective-permute-start | bytes 221192 | tf_op jit(solution)/shard_map/ppermute | solution.py:576
  90.6 4.0 %collective-permute-start.9 = (f32[80,128]{1,0:T(8,128)S(1)}, f32[80,128]{1,0:T(8,128)S(1)}, u32[]{:S(2)}, u32[]{:S(2)}) collective-permute-start(f32[80,128]{1,0:T(8,128)S(1)} %add.73), channel_id=1, source_target_pairs={{0,8},{2,10},{4,12},{6,14},{8,0},{10,2},{12,4},{14,6},{16,24},{18,... | collective-permute-start | bytes 122888 | tf_op jit(solution)/shard_map/ppermute | solution.py:576
  94.6 5.4 %collective-permute-start.10 = (f32[80,128]{1,0:T(8,128)S(1)}, f32[80,128]{1,0:T(8,128)S(1)}, u32[]{:S(2)}, u32[]{:S(2)}) collective-permute-start(f32[80,128]{1,0:T(8,128)S(1)} %add.74), channel_id=1, source_target_pairs={{0,16},{2,18},{4,20},{6,22},{8,24},{10,26},{12,28},{14,30},{16,0},... | collective-permute-start | bytes 122888 | tf_op jit(solution)/shard_map/ppermute | solution.py:576
  97.8 4.5 %collective-permute-start.16 = (f32[72,256]{1,0:T(8,128)S(1)}, f32[72,256]{1,0:T(8,128)S(1)}, u32[]{:S(2)}, u32[]{:S(2)}) collective-permute-start(f32[72,256]{1,0:T(8,128)S(1)} %add.81), channel_id=1, source_target_pairs={{0,8},{2,10},{4,12},{6,14},{8,0},{10,2},{12,4},{14,6},{16,24},{18,... | collective-permute-start | bytes 221192 | tf_op jit(solution)/shard_map/ppermute | solution.py:576
  99.9 4.8 %collective-permute-start.11 = (f32[80,128]{1,0:T(8,128)S(1)}, f32[80,128]{1,0:T(8,128)S(1)}, u32[]{:S(2)}, u32[]{:S(2)}) collective-permute-start(f32[80,128]{1,0:T(8,128)S(1)} %add.75), channel_id=1, source_target_pairs={{0,2},{2,0},{4,6},{6,4},{8,10},{10,8},{12,14},{14,12},{16,18},{18,... | collective-permute-start | bytes 122888 | tf_op jit(solution)/shard_map/ppermute | solution.py:576
  100.1 15.8 %collective-permute-start.19 = (f32[128,1024]{1,0:T(8,128)S(1)}, f32[128,1024]{1,0:T(8,128)S(1)}, u32[]{:S(2)}, u32[]{:S(2)}) collective-permute-start(f32[128,1024]{1,0:T(8,128)S(1)} %slice.11), channel_id=1, source_target_pairs={{0,1},{1,0},{2,3},{3,2},{4,5},{5,4},{6,7},{7,6},{8,9},{9,8},{10,11... | collective-permute-start | bytes 1572872 | tf_op jit(solution)/shard_map/ppermute | solution.py:576
  102.3 6.9 %collective-permute-start.17 = (f32[72,256]{1,0:T(8,128)S(1)}, f32[72,256]{1,0:T(8,128)S(1)}, u32[]{:S(2)}, u32[]{:S(2)}) collective-permute-start(f32[72,256]{1,0:T(8,128)S(1)} %add.82), channel_id=1, source_target_pairs={{0,16},{2,18},{4,20},{6,22},{8,24},{10,26},{12,28},{14,30},{16,0},... | collective-permute-start | bytes 221192 | tf_op jit(solution)/shard_map/ppermute | solution.py:576
  109.2 6.6 %collective-permute-start.18 = (f32[72,256]{1,0:T(8,128)S(1)}, f32[72,256]{1,0:T(8,128)S(1)}, u32[]{:S(2)}, u32[]{:S(2)}) collective-permute-start(f32[72,256]{1,0:T(8,128)S(1)} %add.83), channel_id=1, source_target_pairs={{0,2},{2,0},{4,6},{6,4},{8,10},{10,8},{12,14},{14,12},{16,18},{18,... | collective-permute-start | bytes 221192 | tf_op jit(solution)/shard_map/ppermute | solution.py:576

commit v3 on v2

--- a/solution.py
+++ b/solution.py
@@ -14,8 +14,7 @@
 ROWS = 256
 PAD = 8
 PIVOTS = 4
-VMEM_LIMIT = 36 * 1024 * 1024
-WHOLE_VMEM = 67043328
+VMEM_LIMIT = 16 * 1024 * 1024
 
 highest_precision = lax.Precision.HIGHEST
 both = ("wide", "narrow")
@@ -156,33 +155,23 @@
     )(n, dosage, annotations, chi)
 
 
-def own_kernel(n_ref, dosage_ref, annot_ref, sums_ref, turned_ref, given, geno, turned, wide_values, came, went):
+def own_kernel(n_ref, dosage_ref, annot_ref, sums_ref, turned_ref, geno, wide_values):
     samples, strip = dosage_ref.shape
     mine = strip // (2 * TILE)
     n = n_ref[0]
-    arrivals = [
-        pltpu.make_async_copy(dosage_ref.at[:, cols_at(n * mine + t)], given.at[t], came.at[t])
-        for t in range(mine)
-    ]
-    departures = [
-        pltpu.make_async_copy(turned.at[t], turned_ref.at[t], went.at[t]) for t in range(mine)
-    ]
-    arrivals[0].start()
     sums_ref[...] = jnp.zeros_like(sums_ref)
     for t in range(mine):
-        arrivals[t].wait()
-        if t + 1 < mine:
-            arrivals[t + 1].start()
-        standardized(lambda rows: given[t, rows, :], into(geno, t), wide_values, samples)
+        standardized(
+            lambda rows: dosage_ref[rows, cols_at(n * mine + t)], into(geno, t), wide_values, samples
+        )
         for k in range(samples // LANES):
             for part in range(2):
-                turned[t, k, part * LANES : (part + 1) * LANES, :] = geno[
+                turned_ref[t, k, part * LANES : (part + 1) * LANES, :] = geno[
                     2 * t + part, k * LANES : (k + 1) * LANES, :
                 ].T
-        departures[t].start()
     for y in range(mine):
         for x in range(y + 1):
-            weights = band_weights(rows_of(turned, x), columns_of(geno, y))
+            weights = band_weights(rows_of(turned_ref, x), columns_of(geno, y))
             sums_ref[:, y * TILE : (y + 1) * TILE] += along_rows(
                 annot_ref[:, cols_at(n * mine + x)], weights
             )
@@ -190,13 +179,10 @@
                 sums_ref[:, x * TILE : (x + 1) * TILE] += along_columns(
                     annot_ref[:, cols_at(n * mine + y)], weights
                 )
-    for copy in departures:
-        copy.wait()
 
 
 def other_kernel(
-    slots, n_ref, dosage_ref, annot_ref, turned_ref, sums_in, sums_ref,
-    given, geno, turned, wide_values, came, back,
+    slots, n_ref, dosage_ref, annot_ref, turned_ref, sums_in, sums_ref, geno, wide_values
 ):
     samples, strip = dosage_ref.shape
     mine = strip // (2 * TILE)
@@ -205,30 +191,19 @@
     def nearest(s):
         return (1 - n) * s + n * (mine - 1 - s)
 
-    arrivals = [
-        pltpu.make_async_copy(
-            dosage_ref.at[:, cols_at((1 - n) * mine + nearest(s))], given.at[s], came.at[s]
+    sums_ref[...] = sums_in[...]
+    for s in slots:
+        standardized(
+            lambda rows: dosage_ref[rows, cols_at((1 - n) * mine + nearest(s))],
+            into(geno, s),
+            wide_values,
+            samples,
         )
-        for s in slots
-    ]
-    returns = [
-        pltpu.make_async_copy(turned_ref.at[nearest(h)], turned.at[h], back.at[h])
-        for h in range(slots[0], mine)
-    ]
-    arrivals[0].start()
-    sums_ref[...] = sums_in[...]
-    for i, s in enumerate(slots):
-        arrivals[i].wait()
-        for copy in [*arrivals, *returns][i + 1 : i + 2] if i + 1 < len(slots) else returns:
-            copy.start()
-        standardized(lambda rows: given[s, rows, :], into(geno, s), wide_values, samples)
-    for copy in returns:
-        copy.wait()
     inside = (1 - 2 * n) * tile_offset() >= 0
     for s in slots:
         for h in range(s, mine):
             weights = band_weights(
-                rows_of(turned, h), columns_of(geno, s), inside if h == s else None
+                rows_of(turned_ref, nearest(h)), columns_of(geno, s), inside if h == s else None
             )
             sums_ref[:, cols_at(nearest(h))] += along_columns(
                 annot_ref[:, cols_at((1 - n) * mine + nearest(s))], weights
@@ -245,10 +220,11 @@
             jax.ShapeDtypeStruct((annot.shape[0], strip // 2), jnp.float32),
             jax.ShapeDtypeStruct(turned, jnp.bfloat16),
         ),
-        in_specs=[in_smem, in_place, in_vmem],
-        out_specs=(in_vmem, in_place),
+        in_specs=[in_smem, in_vmem, in_vmem],
+        out_specs=(in_vmem, in_vmem),
         scratch_shapes=strip_scratch(dosage),
         cost_estimate=strip_cost(dosage),
+        compiler_params=pltpu.CompilerParams(vmem_limit_bytes=VMEM_LIMIT),
         name="own_sums",
     )(n, dosage, annot)
 
@@ -257,11 +233,11 @@
     return pl.pallas_call(
         functools.partial(other_kernel, slots),
         out_shape=jax.ShapeDtypeStruct(sums.shape, jnp.float32),
-        in_specs=[in_smem, in_place, in_vmem, in_place, in_vmem],
+        in_specs=[in_smem] + [in_vmem] * 4,
         out_specs=in_vmem,
         scratch_shapes=strip_scratch(dosage),
         cost_estimate=strip_cost(dosage),
-        compiler_params=pltpu.CompilerParams(vmem_limit_bytes=WHOLE_VMEM),
+        compiler_params=pltpu.CompilerParams(vmem_limit_bytes=VMEM_LIMIT),
         name="other_sums",
     )(n, dosage, annot, turned, sums)
 
@@ -269,12 +245,8 @@
 def strip_scratch(dosage):
     samples, _, mine = sizes(dosage)
     return [
-        pltpu.VMEM((mine, samples, TILE), jnp.bfloat16),
         pltpu.VMEM((2 * mine, samples, LANES), jnp.bfloat16),
-        pltpu.VMEM((mine, samples // LANES, TILE, LANES), jnp.bfloat16),
         pltpu.VMEM((samples, TILE), jnp.float32),
-        pltpu.SemaphoreType.DMA((mine,)),
-        pltpu.SemaphoreType.DMA((mine,)),
     ]
 
 
@@ -286,39 +258,23 @@
 
 
 def rim_kernel(
-    n_ref, arrived_ref, turned_ref, annot_ref, sums_in, sums_ref, back_ref,
-    given, geno, turned, wide_values, came, back,
+    n_ref, arrived_ref, turned_ref, annot_ref, sums_in, sums_ref, back_ref, geno, wide_values
 ):
     mine = turned_ref.shape[0]
     samples = geno.shape[1]
     width = mine // 2
     n = n_ref[0]
-    arrivals = [
-        pltpu.make_async_copy(
-            arrived_ref.at[:, c * TILE : (c + 1) * TILE], given.at[c], came.at[c]
-        )
-        for c in range(width)
-    ]
-    returns = [
-        pltpu.make_async_copy(turned_ref.at[t], turned.at[t], back.at[t]) for t in range(mine)
-    ]
-    arrivals[0].start()
     sums_ref[...] = sums_in[...]
     back_ref[...] = jnp.zeros_like(back_ref)
     for c in range(width):
-        arrivals[c].wait()
-        for copy in arrivals[c + 1 : c + 2] if c + 1 < width else returns:
-            copy.start()
-        standardized(lambda rows: given[c, rows, :], into(geno, c), wide_values, samples)
-    for copy in returns:
-        copy.wait()
+        columns = slice(c * TILE, (c + 1) * TILE)
+        standardized(lambda rows: arrived_ref[rows, columns], into(geno, c), wide_values, samples)
 
     def add(c, y, inside=None):
-        weights = band_weights(rows_of(turned, y), columns_of(geno, c), inside)
-        sums_ref[:, cols_at(y)] += along_columns(given[c, samples:, :], weights)
-        back_ref[:, c * TILE : (c + 1) * TILE] += along_rows(
-            annot_ref[:, cols_at(n * mine + y)], weights
-        )
+        columns = slice(c * TILE, (c + 1) * TILE)
+        weights = band_weights(rows_of(turned_ref, y), columns_of(geno, c), inside)
+        sums_ref[:, cols_at(y)] += along_columns(arrived_ref[samples:, columns], weights)
+        back_ref[:, columns] += along_rows(annot_ref[:, cols_at(n * mine + y)], weights)
 
     diagonal = (1 - 2 * n) * tile_offset() <= 0
     for c in range(width):
@@ -342,16 +298,13 @@
             jax.ShapeDtypeStruct(sums.shape, jnp.float32),
             jax.ShapeDtypeStruct((sums.shape[0], width * TILE), jnp.float32),
         ),
-        in_specs=[in_smem, in_place, in_place, in_vmem, in_vmem],
+        in_specs=[in_smem] + [in_vmem] * 4,
         out_specs=(in_vmem, in_vmem),
         scratch_shapes=[
-            pltpu.VMEM((width, arrived.shape[0], TILE), jnp.bfloat16),
             pltpu.VMEM((2 * width, samples, LANES), jnp.bfloat16),
-            pltpu.VMEM(turned.shape, jnp.bfloat16),
             pltpu.VMEM((samples, TILE), jnp.float32),
-            pltpu.SemaphoreType.DMA((width,)),
-            pltpu.SemaphoreType.DMA((mine,)),
         ],
+        compiler_params=pltpu.CompilerParams(vmem_limit_bytes=VMEM_LIMIT),
         cost_estimate=pl.CostEstimate(
             flops=2 * samples * width * TILE * mine * TILE,
             bytes_accessed=2 * samples * TILE * (mine + width),
@@ -586,9 +539,24 @@
     return bits
 
 
+def added_kernel(first_ref, second_ref, out_ref):
+    out_ref[...] = first_ref[...] + second_ref[...]
+
+
+def added(first, second):
+    return pl.pallas_call(
+        added_kernel,
+        out_shape=jax.ShapeDtypeStruct(first.shape, first.dtype),
+        in_specs=[in_vmem, in_vmem],
+        out_specs=in_vmem,
+        compiler_params=pltpu.CompilerParams(vmem_limit_bytes=VMEM_LIMIT // 4),
+        name="added",
+    )(first, second)
+
+
 def wide_sum(value):
     for bit in wide_bits():
-        value = value + flipped(value, "wide", bit)
+        value = added(value, flipped(value, "wide", bit))
     return value
 
 

time: 119 us -> 104 us (0.87)
  Pallas kernels: 60.5 us -> 39.2 us
  local copies, waits for them, and re-layouts: 1.71 us -> 12 us
  starting transfers between devices: 31.7 us -> 27.9 us
  waiting for transfers between devices: 19 us -> 21.6 us
  matrix products: 3.31 us -> 2.09 us
  other arithmetic: 1.33 us -> 0.14 us
    unnamed x4 -> x18, local copies, waits for them, and re-layouts: 1.65 us -> 12 us
    pallas_call x2, Pallas kernels: 19.6 us -> 9.36 us  [other_sums(): pl.pallas_call(functools.partial(other_kernel, slots), out_shape=jax.Shap...]
    pallas_call x1, Pallas kernels: 12 us -> 6.5 us  [rim_sums(): pl.pallas_call(rim_kernel, out_shape=(jax.ShapeDtypeStruct(sums.shape, jn...]
    pallas_call x1, Pallas kernels: 13.8 us -> 9.22 us  [own_sums(): pl.pallas_call(own_kernel, out_shape=(jax.ShapeDtypeStruct((annot.shape[0...]
    ppermute x18, waiting for transfers between devices: 19 us -> 21.6 us  [flipped(): return lax.ppermute(value, axis, [(i, i ^ bit) for i in range(length)])]
    ppermute x18, starting transfers between devices: 26.4 us -> 24.5 us  [flipped(): return lax.ppermute(value, axis, [(i, i ^ bit) for i in range(length)])]
    ppermute x1, starting transfers between devices: 3.85 us -> 2.54 us  [whole_step(): arrived = lax.ppermute(outgoing, both, rim_pairs)]
    dot_general x2, matrix products: 3.31 us -> 2.09 us  [whole_step(): jnp.dot(extended, values, precision=lax.Precision.HIGH, preferred_element...]
  transfers between devices with their start and end apart: 20 -> 20, of which waited for: 9 -> 10; matrix products, arithmetic and copies ran while one was open for 3% -> 1% of each run, Pallas kernels for 45% -> 31%
where the time goes in v3:
time: 104 us
  Pallas kernels  39.2 us (38%)
  starting transfers between devices  27.9 us (27%)
  waiting for transfers between devices  21.6 us (21%)
  local copies, waits for them, and re-layouts  12 us (12%)
  matrix products  2.09 us (2%)
    ppermute x18, starting transfers between devices, flipped(): return lax.ppermute(value, axis, [(i, i ^ bit) for i in range(length)])  24.5 us
    ppermute x18, waiting for transfers between devices, flipped(): return lax.ppermute(value, axis, [(i, i ^ bit) for i in range(length)])  21.6 us
    unnamed x18, local copies, waits for them, and re-layouts  12 us
    pallas_call x2, Pallas kernels, other_sums(): pl.pallas_call(functools.partial(other_kernel, slots), out_shape=jax.Shap...  9.36 us
    pallas_call x1, Pallas kernels, own_sums(): pl.pallas_call(own_kernel, out_shape=(jax.ShapeDtypeStruct((annot.shape[0...  9.22 us
    pallas_call x1, Pallas kernels, gram_inverse(): pl.pallas_call(functools.partial(inverse_kernel, divisor), out_shape=(squ...  6.54 us
    pallas_call x1, Pallas kernels, rim_sums(): pl.pallas_call(rim_kernel, out_shape=(jax.ShapeDtypeStruct(sums.shape, jn...  6.5 us
    pallas_call x1, Pallas kernels, prepared(): pl.pallas_call(prepare_kernel, out_shape=(jax.ShapeDtypeStruct((samples +...  4.11 us
  transfers between devices with their start and end apart: 20, of which 10 were waited for; matrix products, arithmetic and copies ran while one was open for 1% of the time, Pallas kernels for 31%

profile of v3, /device:TPU:0, one launch (start us, length us, event | category | flops | bytes accessed | tf_op | source)
XLA Modules:
  0.0 103.8 jit_solution(8139977881300056685)
XLA Ops:
  0.6 4.1 %prepare.1 = (bf16[2184,512]{1,0:T(8,128)(2,1)}, bf16[136,2048]{1,0:T(8,128)(2,1)}, f32[1,128]{1,0:T(1,128)}, f32[1024,256]{1,0:T(8,128)}) custom-call(s32[1]{0:T(128)} %bitcast.n_ref, bf16[2048,2048]{1,0:T(8,128)(2,1)} %dosage_ref.7, s32[128,2048]{1,0:T(8,128)} %annot_ref.1, f32[2048,256]{1,0:T(8,128)} %chi_ref.1), custom_call_target="tpu_custom_call" | custom-call | bytes 6291456 | tf_op jit(solution)/shard_map/prepare/pallas_call | solution.py:140
  4.8 2.5 %collective-permute-start.4 = (bf16[2184,512]{1,0:T(8,128)(2,1)}, bf16[2184,512]{1,0:T(8,128)(2,1)S(1)}, u32[]{:S(2)}, u32[]{:S(2)}) collective-permute-start(bf16[2184,512]{1,0:T(8,128)(2,1)} %get-tuple-element.17), channel_id=1, source_target_pairs={{0,2},{3,1},{2,4},{5,3},{4,6},{7,5},{6,8},{9,7},{8,10},{11,9},{10,... | collective-permute-start | bytes 6709256 | tf_op jit(solution)/shard_map/ppermute | solution.py:602
  7.3 2.5 %collective-permute-start = (f32[1,128]{1,0:T(1,128)}, f32[1,128]{1,0:T(1,128)S(1)}, u32[]{:S(2)}, u32[]{:S(2)}) collective-permute-start(f32[1,128]{1,0:T(1,128)} %get-tuple-element.14.first_ref), channel_id=1, source_target_pairs={{0,2},{2,0},{4,6},{6,4},{8,10},{10,8},{12,14},{14,12},{16,18},{18,... | collective-permute-start | bytes 1544 | tf_op jit(solution)/shard_map/ppermute | solution.py:529
  9.8 0.4 collective-permute-start.12
  10.2 3.4 %copy-done = bf16[2048,2048]{1,0:T(8,128)(2,1)S(1)} copy-done((bf16[2048,2048]{1,0:T(8,128)(2,1)S(1)}, bf16[2048,2048]{1,0:T(8,128)(2,1)}, u32[]{:S(2)}) %copy-start) | copy-done | bytes 8388632
  13.6 1.1 %copy-done.2 = bf16[136,2048]{1,0:T(8,128)(2,1)S(1)} copy-done((bf16[136,2048]{1,0:T(8,128)(2,1)S(1)}, bf16[136,2048]{1,0:T(8,128)(2,1)}, u32[]{:S(2)}) %copy-start.2) | copy-done | bytes 557080
  14.7 9.2 %own_sums.1 = (f32[136,1024]{1,0:T(8,128)S(1)}, bf16[4,16,256,128]{3,2,1,0:T(8,128)(2,1)S(1)}) custom-call(s32[1]{0:T(128)} %bitcast.n_ref, bf16[2048,2048]{1,0:T(8,128)(2,1)S(1)} %copy-done, bf16[136,2048]{1,0:T(8,128)(2,1)S(1)} %copy-done.2), custom_call_target="tpu_custom_call" | custom-call | flops 4294967296 | bytes 8388608 | tf_op jit(solution)/shard_map/own_sums/pallas_call | solution.py:217
  23.9 0.0 copy-start.4
  23.9 6.1 %other_sums.2.sums_in = f32[136,1024]{1,0:T(8,128)S(1)} custom-call(s32[1]{0:T(128)} %bitcast.n_ref, bf16[2048,2048]{1,0:T(8,128)(2,1)S(1)} %copy-done, bf16[136,2048]{1,0:T(8,128)(2,1)S(1)} %copy-done.2, bf16[4,16,256,128]{3,2,1,0:T(8,128)(2,1)S(1)} %get-tuple-element.16.turned_ref, f32[136,1024]{1,0:T(8,128)S(1)} %get-tuple-element.18.sums_in), custom_call_target="tpu_custom_call" | custom-call | flops 4294967296 | bytes 8388608 | tf_op jit(solution)/shard_map/other_sums/pallas_call | solution.py:233
  30.0 2.0 %copy-done.5 = bf16[4,16,256,128]{3,2,1,0:T(8,128)(2,1)} copy-done((bf16[4,16,256,128]{3,2,1,0:T(8,128)(2,1)}, bf16[4,16,256,128]{3,2,1,0:T(8,128)(2,1)S(1)}, u32[]{:S(2)}) %copy-start.5) | copy-done | bytes 4194328
  32.0 0.0 collective-permute-done.second_ref
  32.0 1.6 %collective-permute-start.1 = (f32[1,128]{1,0:T(1,128)S(1)}, f32[1,128]{1,0:T(1,128)S(1)}, u32[]{:S(2)}, u32[]{:S(2)}) collective-permute-start(f32[1,128]{1,0:T(1,128)S(1)} %added.4.first_ref), channel_id=1, source_target_pairs={{0,4},{2,6},{4,0},{6,2},{8,12},{10,14},{12,8},{14,10},{16,20},{18,... | collective-permute-start | bytes 1544 | tf_op jit(solution)/shard_map/ppermute | solution.py:529
  33.5 2.1 %collective-permute-done.1.second_ref = f32[1,128]{1,0:T(1,128)S(1)} collective-permute-done((f32[1,128]{1,0:T(1,128)S(1)}, f32[1,128]{1,0:T(1,128)S(1)}, u32[]{:S(2)}, u32[]{:S(2)}) %collective-permute-start.1) | collective-permute-done | bytes 544 | tf_op jit(solution)/shard_map/ppermute | solution.py:529
  35.6 2.0 %collective-permute-start.2 = (f32[1,128]{1,0:T(1,128)S(1)}, f32[1,128]{1,0:T(1,128)S(1)}, u32[]{:S(2)}, u32[]{:S(2)}) collective-permute-start(f32[1,128]{1,0:T(1,128)S(1)} %added.5.first_ref), channel_id=1, source_target_pairs={{0,8},{2,10},{4,12},{6,14},{8,0},{10,2},{12,4},{14,6},{16,24},{18,... | collective-permute-start | bytes 1544 | tf_op jit(solution)/shard_map/ppermute | solution.py:529
  37.6 1.6 %collective-permute-done.2.second_ref = f32[1,128]{1,0:T(1,128)S(1)} collective-permute-done((f32[1,128]{1,0:T(1,128)S(1)}, f32[1,128]{1,0:T(1,128)S(1)}, u32[]{:S(2)}, u32[]{:S(2)}) %collective-permute-start.2) | collective-permute-done | bytes 544 | tf_op jit(solution)/shard_map/ppermute | solution.py:529
  39.2 3.0 %collective-permute-start.3 = (f32[1,128]{1,0:T(1,128)S(1)}, f32[1,128]{1,0:T(1,128)S(1)}, u32[]{:S(2)}, u32[]{:S(2)}) collective-permute-start(f32[1,128]{1,0:T(1,128)S(1)} %added.6.first_ref), channel_id=1, source_target_pairs={{0,16},{2,18},{4,20},{6,22},{8,24},{10,26},{12,28},{14,30},{16,0},... | collective-permute-start | bytes 1544 | tf_op jit(solution)/shard_map/ppermute | solution.py:529
  42.2 1.5 %collective-permute-done.3.second_ref = f32[1,128]{1,0:T(1,128)S(1)} collective-permute-done((f32[1,128]{1,0:T(1,128)S(1)}, f32[1,128]{1,0:T(1,128)S(1)}, u32[]{:S(2)}, u32[]{:S(2)}) %collective-permute-start.3) | collective-permute-done | bytes 544 | tf_op jit(solution)/shard_map/ppermute | solution.py:529
  43.8 2.2 %copy-done.6 = bf16[4,16,256,128]{3,2,1,0:T(8,128)(2,1)S(1)} copy-done((bf16[4,16,256,128]{3,2,1,0:T(8,128)(2,1)S(1)}, bf16[4,16,256,128]{3,2,1,0:T(8,128)(2,1)}, u32[]{:S(2)}) %copy-start.6) | copy-done | bytes 4194328
  45.9 6.5 %rim_sums.1 = (f32[136,1024]{1,0:T(8,128)S(1)}, f32[136,512]{1,0:T(8,128)S(1)}) custom-call(s32[1]{0:T(128)} %bitcast.n_ref, bf16[2184,512]{1,0:T(8,128)(2,1)S(1)} %collective-permute-done.4.arrived_ref, bf16[4,16,256,128]{3,2,1,0:T(8,128)(2,1)S(1)} %copy-done.6, bf16[136,2048]{1,0:T(8,128)(2,1)S(1)} %copy-done.3, f32[136,1024]{1,0:T(8,128)S(1)} %other_sums.2.sums_in), custom_call_target="tpu_custom_call" | custom-call | flops 2147483648 | bytes 6291456 | tf_op jit(solution)/shard_map/rim_sums/pallas_call | solution.py:295
  52.4 0.9 collective-permute-start.5
  53.3 0.0 copy-start.1
  53.3 3.4 %copy-done.1 = bf16[2048,2048]{1,0:T(8,128)(2,1)S(1)} copy-done((bf16[2048,2048]{1,0:T(8,128)(2,1)S(1)}, bf16[2048,2048]{1,0:T(8,128)(2,1)}, u32[]{:S(2)}) %copy-start.1) | copy-done | bytes 8388632
  56.7 3.3 %other_sums.3.sums_ref = f32[136,1024]{1,0:T(8,128)S(1)} custom-call(s32[1]{0:T(128)} %bitcast.n_ref, bf16[2048,2048]{1,0:T(8,128)(2,1)S(1)} %copy-done.1, bf16[136,2048]{1,0:T(8,128)(2,1)S(1)} %copy-done.3, bf16[4,16,256,128]{3,2,1,0:T(8,128)(2,1)S(1)} %copy-done.7, f32[136,1024]{1,0:T(8,128)S(1)} %get-tuple-element.19.sums_in), custom_call_target="tpu_custom_call" | custom-call | flops 4294967296 | bytes 8388608 | tf_op jit(solution)/shard_map/other_sums/pallas_call | solution.py:233
  60.0 0.0 collective-permute-done.5.back_ref
  60.0 0.9 moments.1
  60.9 0.4 fusion
  61.3 1.7 %fusion.6 = f32[144,256]{1,0:T(8,128)S(1)} fusion(f32[144,1024]{1,0:T(8,128)S(1)} %get-tuple-element.24.scores_ref, f32[1024,256]{1,0:T(8,128)} %collective-permute-done.12), kind=kOutput, calls=%fused_computation.15 | convolution fusion | flops 226492416 | bytes 1785856 | tf_op jit(solution)/shard_map/dot_general | solution.py:623
  63.0 0.1 collective-permute-start.13
  63.1 0.5 collective-permute-start.6
  63.6 0.9 collective-permute-done.13
  64.5 3.9 %collective-permute-start.14 = (f32[72,256]{1,0:T(8,128)S(1)}, f32[72,256]{1,0:T(8,128)S(1)}, u32[]{:S(2)}, u32[]{:S(2)}) collective-permute-start(f32[72,256]{1,0:T(8,128)S(1)} %slice.13), channel_id=1, source_target_pairs={{0,1},{1,0},{2,3},{3,2},{4,5},{5,4},{6,7},{7,6},{8,9},{9,8},{10,11... | collective-permute-start | bytes 221192 | tf_op jit(solution)/shard_map/ppermute | solution.py:529
  68.4 0.2 collective-permute-start.7
  68.6 3.9 %collective-permute-done.7 = f32[80,128]{1,0:T(8,128)S(1)} collective-permute-done((f32[80,128]{1,0:T(8,128)S(1)}, f32[80,128]{1,0:T(8,128)S(1)}, u32[]{:S(2)}, u32[]{:S(2)}) %collective-permute-start.7) | collective-permute-done | bytes 40992 | tf_op jit(solution)/shard_map/ppermute | solution.py:529
  72.5 1.9 %collective-permute-start.8 = (f32[80,128]{1,0:T(8,128)S(1)}, f32[80,128]{1,0:T(8,128)S(1)}, u32[]{:S(2)}, u32[]{:S(2)}) collective-permute-start(f32[80,128]{1,0:T(8,128)S(1)} %add.56), channel_id=1, source_target_pairs={{0,4},{2,6},{4,0},{6,2},{8,12},{10,14},{12,8},{14,10},{16,20},{18,... | collective-permute-start | bytes 122888 | tf_op jit(solution)/shard_map/ppermute | solution.py:529
  74.5 0.1 collective-permute-start.15
  74.6 2.3 %collective-permute-done.8 = f32[80,128]{1,0:T(8,128)S(1)} collective-permute-done((f32[80,128]{1,0:T(8,128)S(1)}, f32[80,128]{1,0:T(8,128)S(1)}, u32[]{:S(2)}, u32[]{:S(2)}) %collective-permute-start.8) | collective-permute-done | bytes 40992 | tf_op jit(solution)/shard_map/ppermute | solution.py:529
  77.0 1.6 %collective-permute-start.9 = (f32[80,128]{1,0:T(8,128)S(1)}, f32[80,128]{1,0:T(8,128)S(1)}, u32[]{:S(2)}, u32[]{:S(2)}) collective-permute-start(f32[80,128]{1,0:T(8,128)S(1)} %add.57), channel_id=1, source_target_pairs={{0,8},{2,10},{4,12},{6,14},{8,0},{10,2},{12,4},{14,6},{16,24},{18,... | collective-permute-start | bytes 122888 | tf_op jit(solution)/shard_map/ppermute | solution.py:529
  78.5 2.4 %collective-permute-done.9 = f32[80,128]{1,0:T(8,128)S(1)} collective-permute-done((f32[80,128]{1,0:T(8,128)S(1)}, f32[80,128]{1,0:T(8,128)S(1)}, u32[]{:S(2)}, u32[]{:S(2)}) %collective-permute-start.9) | collective-permute-done | bytes 40992 | tf_op jit(solution)/shard_map/ppermute | solution.py:529
  81.0 3.0 %collective-permute-start.10 = (f32[80,128]{1,0:T(8,128)S(1)}, f32[80,128]{1,0:T(8,128)S(1)}, u32[]{:S(2)}, u32[]{:S(2)}) collective-permute-start(f32[80,128]{1,0:T(8,128)S(1)} %add.58), channel_id=1, source_target_pairs={{0,16},{2,18},{4,20},{6,22},{8,24},{10,26},{12,28},{14,30},{16,0},... | collective-permute-start | bytes 122888 | tf_op jit(solution)/shard_map/ppermute | solution.py:529
  84.0 1.3 %collective-permute-start.16 = (f32[72,256]{1,0:T(8,128)S(1)}, f32[72,256]{1,0:T(8,128)S(1)}, u32[]{:S(2)}, u32[]{:S(2)}) collective-permute-start(f32[72,256]{1,0:T(8,128)S(1)} %add.65), channel_id=1, source_target_pairs={{0,8},{2,10},{4,12},{6,14},{8,0},{10,2},{12,4},{14,6},{16,24},{18,... | collective-permute-start | bytes 221192 | tf_op jit(solution)/shard_map/ppermute | solution.py:529
  85.3 0.7 collective-permute-done.10
  86.0 1.0 collective-permute-start.19
  87.1 1.4 %collective-permute-done.16 = f32[72,256]{1,0:T(8,128)S(1)} collective-permute-done((f32[72,256]{1,0:T(8,128)S(1)}, f32[72,256]{1,0:T(8,128)S(1)}, u32[]{:S(2)}, u32[]{:S(2)}) %collective-permute-start.16) | collective-permute-done | bytes 73760 | tf_op jit(solution)/shard_map/ppermute | solution.py:529
  88.5 1.3 %collective-permute-start.17 = (f32[72,256]{1,0:T(8,128)S(1)}, f32[72,256]{1,0:T(8,128)S(1)}, u32[]{:S(2)}, u32[]{:S(2)}) collective-permute-start(f32[72,256]{1,0:T(8,128)S(1)} %add.66), channel_id=1, source_target_pairs={{0,16},{2,18},{4,20},{6,22},{8,24},{10,26},{12,28},{14,30},{16,0},... | collective-permute-start | bytes 221192 | tf_op jit(solution)/shard_map/ppermute | solution.py:529
  89.8 4.8 %collective-permute-done.17 = f32[72,256]{1,0:T(8,128)S(1)} collective-permute-done((f32[72,256]{1,0:T(8,128)S(1)}, f32[72,256]{1,0:T(8,128)S(1)}, u32[]{:S(2)}, u32[]{:S(2)}) %collective-permute-start.17) | collective-permute-done | bytes 73760 | tf_op jit(solution)/shard_map/ppermute | solution.py:529
  94.6 0.1 collective-permute-start.18
  94.7 6.5 %gram_inverse.1 = (f32[128,128]{1,0:T(8,128)S(1)}, f32[128,128]{1,0:T(8,128)S(1)}) custom-call(f32[160,128]{1,0:T(8,128)S(1)} %maximum_select_fusion.1.payload_ref), custom_call_target="tpu_custom_call" | custom-call | flops 20000000000 | bytes 65536 | tf_op jit(solution)/shard_map/gram_inverse/pallas_call | solution.py:460
  101.2 2.6 %fitted_values.1 = (f32[128,1024]{1,0:T(8,128)}, f32[2048,256]{1,0:T(8,128)}) custom-call(s32[1]{0:T(128)} %bitcast.n_ref, f32[128,128]{1,0:T(8,128)S(1)} %get-tuple-element.22.inverse_ref, f32[128,128]{1,0:T(8,128)S(1)} %get-tuple-element.23.moments_ref, f32[144,256]{1,0:T(8,128)S(1)} %maximum_select_fusion.proj_ref, ...), custom_call_target="tpu_custom_call" | custom-call | flops 134217728 | bytes 2097152 | tf_op jit(solution)/shard_map/fitted_values/pallas_call | solution.py:511
  (40 shorter events, 0.2 us)
Async XLA Ops:
  4.8 39.0 %collective-permute-start.4 = (bf16[2184,512]{1,0:T(8,128)(2,1)}, bf16[2184,512]{1,0:T(8,128)(2,1)S(1)}, u32[]{:S(2)}, u32[]{:S(2)}) collective-permute-start(bf16[2184,512]{1,0:T(8,128)(2,1)} %get-tuple-element.17), channel_id=1, source_target_pairs={{0,2},{3,1},{2,4},{5,3},{4,6},{7,5},{6,8},{9,7},{8,10},{11,9},{10,... | collective-permute-start | bytes 6709256 | tf_op jit(solution)/shard_map/ppermute | solution.py:602
  7.3 24.7 %collective-permute-start = (f32[1,128]{1,0:T(1,128)}, f32[1,128]{1,0:T(1,128)S(1)}, u32[]{:S(2)}, u32[]{:S(2)}) collective-permute-start(f32[1,128]{1,0:T(1,128)} %get-tuple-element.14.first_ref), channel_id=1, source_target_pairs={{0,2},{2,0},{4,6},{6,4},{8,10},{10,8},{12,14},{14,12},{16,18},{18,... | collective-permute-start | bytes 1544 | tf_op jit(solution)/shard_map/ppermute | solution.py:529
  9.8 51.5 %collective-permute-start.12 = (f32[1024,256]{1,0:T(8,128)}, f32[1024,256]{1,0:T(8,128)}, u32[]{:S(2)}, u32[]{:S(2)}) collective-permute-start(f32[1024,256]{1,0:T(8,128)} %get-tuple-element.25), channel_id=1, source_target_pairs={{0,1},{1,0},{2,3},{3,2},{4,5},{5,4},{6,7},{7,6},{8,9},{9,8},{10,11... | collective-permute-start | bytes 3145736 | tf_op jit(solution)/shard_map/ppermute | solution.py:529
  10.2 3.4 %copy-start = (bf16[2048,2048]{1,0:T(8,128)(2,1)S(1)}, bf16[2048,2048]{1,0:T(8,128)(2,1)}, u32[]{:S(2)}) copy-start(bf16[2048,2048]{1,0:T(8,128)(2,1)} %dosage_ref.7) | copy-start | bytes 25165828
  13.6 1.1 %copy-start.2 = (bf16[136,2048]{1,0:T(8,128)(2,1)S(1)}, bf16[136,2048]{1,0:T(8,128)(2,1)}, u32[]{:S(2)}) copy-start(bf16[136,2048]{1,0:T(8,128)(2,1)} %get-tuple-element.15.annot_ref) | copy-start | bytes 1671172
  23.9 8.1 %copy-start.4 = (f32[1,128]{1,0:T(1,128)S(1)}, f32[1,128]{1,0:T(1,128)}, u32[]{:S(2)}) copy-start(f32[1,128]{1,0:T(1,128)} %get-tuple-element.14.first_ref) | copy-start | bytes 1540
  23.9 19.8 %copy-start.3 = (bf16[136,2048]{1,0:T(8,128)(2,1)S(1)}, bf16[136,2048]{1,0:T(8,128)(2,1)}, u32[]{:S(2)}) copy-start(bf16[136,2048]{1,0:T(8,128)(2,1)} %get-tuple-element.15.annot_ref) | copy-start | bytes 1671172
  30.0 2.0 %copy-start.5 = (bf16[4,16,256,128]{3,2,1,0:T(8,128)(2,1)}, bf16[4,16,256,128]{3,2,1,0:T(8,128)(2,1)S(1)}, u32[]{:S(2)}) copy-start(bf16[4,16,256,128]{3,2,1,0:T(8,128)(2,1)S(1)} %get-tuple-element.16.turned_ref) | copy-start | bytes 12582916
  32.0 3.6 %collective-permute-start.1 = (f32[1,128]{1,0:T(1,128)S(1)}, f32[1,128]{1,0:T(1,128)S(1)}, u32[]{:S(2)}, u32[]{:S(2)}) collective-permute-start(f32[1,128]{1,0:T(1,128)S(1)} %added.4.first_ref), channel_id=1, source_target_pairs={{0,4},{2,6},{4,0},{6,2},{8,12},{10,14},{12,8},{14,10},{16,20},{18,... | collective-permute-start | bytes 1544 | tf_op jit(solution)/shard_map/ppermute | solution.py:529
  35.6 3.6 %collective-permute-start.2 = (f32[1,128]{1,0:T(1,128)S(1)}, f32[1,128]{1,0:T(1,128)S(1)}, u32[]{:S(2)}, u32[]{:S(2)}) collective-permute-start(f32[1,128]{1,0:T(1,128)S(1)} %added.5.first_ref), channel_id=1, source_target_pairs={{0,8},{2,10},{4,12},{6,14},{8,0},{10,2},{12,4},{14,6},{16,24},{18,... | collective-permute-start | bytes 1544 | tf_op jit(solution)/shard_map/ppermute | solution.py:529
  39.2 4.5 %collective-permute-start.3 = (f32[1,128]{1,0:T(1,128)S(1)}, f32[1,128]{1,0:T(1,128)S(1)}, u32[]{:S(2)}, u32[]{:S(2)}) collective-permute-start(f32[1,128]{1,0:T(1,128)S(1)} %added.6.first_ref), channel_id=1, source_target_pairs={{0,16},{2,18},{4,20},{6,22},{8,24},{10,26},{12,28},{14,30},{16,0},... | collective-permute-start | bytes 1544 | tf_op jit(solution)/shard_map/ppermute | solution.py:529
  43.7 2.2 %copy-start.6 = (bf16[4,16,256,128]{3,2,1,0:T(8,128)(2,1)S(1)}, bf16[4,16,256,128]{3,2,1,0:T(8,128)(2,1)}, u32[]{:S(2)}) copy-start(bf16[4,16,256,128]{3,2,1,0:T(8,128)(2,1)} %copy-done.5) | copy-start | bytes 12582916
  45.9 7.4 %copy-start.7 = (bf16[4,16,256,128]{3,2,1,0:T(8,128)(2,1)S(1)}, bf16[4,16,256,128]{3,2,1,0:T(8,128)(2,1)}, u32[]{:S(2)}) copy-start(bf16[4,16,256,128]{3,2,1,0:T(8,128)(2,1)} %copy-done.5) | copy-start | bytes 12582916
  52.4 7.5 %collective-permute-start.5 = (f32[136,512]{1,0:T(8,128)S(1)}, f32[136,512]{1,0:T(8,128)S(1)}, u32[]{:S(2)}, u32[]{:S(2)}) collective-permute-start(f32[136,512]{1,0:T(8,128)S(1)} %get-tuple-element.20), channel_id=1, source_target_pairs={{1,2},{2,1},{3,4},{4,3},{5,6},{6,5},{7,8},{8,7},{9,10},{10,9},{11,... | collective-permute-start | bytes 835592 | tf_op jit(solution)/shard_map/ppermute | solution.py:609
  53.3 3.4 %copy-start.1 = (bf16[2048,2048]{1,0:T(8,128)(2,1)S(1)}, bf16[2048,2048]{1,0:T(8,128)(2,1)}, u32[]{:S(2)}) copy-start(bf16[2048,2048]{1,0:T(8,128)(2,1)} %dosage_ref.7) | copy-start | bytes 25165828
  56.7 4.2 %copy-start.8 = (f32[2048,256]{1,0:T(8,128)S(1)}, f32[2048,256]{1,0:T(8,128)}, u32[]{:S(2)}) copy-start(f32[2048,256]{1,0:T(8,128)} %chi_ref.1) | copy-start | bytes 6291460
  63.0 1.4 %collective-permute-start.13 = (f32[72,512]{1,0:T(8,128)S(1)}, f32[72,512]{1,0:T(8,128)S(1)}, u32[]{:S(2)}, u32[]{:S(2)}) collective-permute-start(f32[72,512]{1,0:T(8,128)S(1)} %fusion.2), channel_id=1, source_target_pairs={{0,2},{2,0},{4,6},{6,4},{8,10},{10,8},{12,14},{14,12},{16,18},{18,... | collective-permute-start | bytes 442376 | tf_op jit(solution)/shard_map/ppermute | solution.py:529
  63.1 5.3 %collective-permute-start.6 = (f32[80,128]{1,0:T(8,128)S(1)}, f32[80,128]{1,0:T(8,128)S(1)}, u32[]{:S(2)}, u32[]{:S(2)}) collective-permute-start(f32[80,128]{1,0:T(8,128)S(1)} %constant_dynamic-slice_fusion), channel_id=1, source_target_pairs={{0,2},{2,0},{4,6},{6,4},{8,10},{10,8},{12,14},{14,12},{16,18},{18,... | collective-permute-start | bytes 122888 | tf_op jit(solution)/shard_map/ppermute | solution.py:529
  64.5 10.0 %collective-permute-start.14 = (f32[72,256]{1,0:T(8,128)S(1)}, f32[72,256]{1,0:T(8,128)S(1)}, u32[]{:S(2)}, u32[]{:S(2)}) collective-permute-start(f32[72,256]{1,0:T(8,128)S(1)} %slice.13), channel_id=1, source_target_pairs={{0,1},{1,0},{2,3},{3,2},{4,5},{5,4},{6,7},{7,6},{8,9},{9,8},{10,11... | collective-permute-start | bytes 221192 | tf_op jit(solution)/shard_map/ppermute | solution.py:529
  68.4 4.1 %collective-permute-start.7 = (f32[80,128]{1,0:T(8,128)S(1)}, f32[80,128]{1,0:T(8,128)S(1)}, u32[]{:S(2)}, u32[]{:S(2)}) collective-permute-start(f32[80,128]{1,0:T(8,128)S(1)} %dynamic-slice_add_fusion), channel_id=1, source_target_pairs={{0,1},{1,0},{2,3},{3,2},{4,5},{5,4},{6,7},{7,6},{8,9},{9,8},{10,11... | collective-permute-start | bytes 122888 | tf_op jit(solution)/shard_map/ppermute | solution.py:529
  72.5 4.4 %collective-permute-start.8 = (f32[80,128]{1,0:T(8,128)S(1)}, f32[80,128]{1,0:T(8,128)S(1)}, u32[]{:S(2)}, u32[]{:S(2)}) collective-permute-start(f32[80,128]{1,0:T(8,128)S(1)} %add.56), channel_id=1, source_target_pairs={{0,4},{2,6},{4,0},{6,2},{8,12},{10,14},{12,8},{14,10},{16,20},{18,... | collective-permute-start | bytes 122888 | tf_op jit(solution)/shard_map/ppermute | solution.py:529
  74.5 9.5 %collective-permute-start.15 = (f32[72,256]{1,0:T(8,128)S(1)}, f32[72,256]{1,0:T(8,128)S(1)}, u32[]{:S(2)}, u32[]{:S(2)}) collective-permute-start(f32[72,256]{1,0:T(8,128)S(1)} %slice_add_fusion), channel_id=1, source_target_pairs={{0,4},{2,6},{4,0},{6,2},{8,12},{10,14},{12,8},{14,10},{16,20},{18,... | collective-permute-start | bytes 221192 | tf_op jit(solution)/shard_map/ppermute | solution.py:529
  77.0 4.0 %collective-permute-start.9 = (f32[80,128]{1,0:T(8,128)S(1)}, f32[80,128]{1,0:T(8,128)S(1)}, u32[]{:S(2)}, u32[]{:S(2)}) collective-permute-start(f32[80,128]{1,0:T(8,128)S(1)} %add.57), channel_id=1, source_target_pairs={{0,8},{2,10},{4,12},{6,14},{8,0},{10,2},{12,4},{14,6},{16,24},{18,... | collective-permute-start | bytes 122888 | tf_op jit(solution)/shard_map/ppermute | solution.py:529
  81.0 5.0 %collective-permute-start.10 = (f32[80,128]{1,0:T(8,128)S(1)}, f32[80,128]{1,0:T(8,128)S(1)}, u32[]{:S(2)}, u32[]{:S(2)}) collective-permute-start(f32[80,128]{1,0:T(8,128)S(1)} %add.58), channel_id=1, source_target_pairs={{0,16},{2,18},{4,20},{6,22},{8,24},{10,26},{12,28},{14,30},{16,0},... | collective-permute-start | bytes 122888 | tf_op jit(solution)/shard_map/ppermute | solution.py:529
  84.0 4.4 %collective-permute-start.16 = (f32[72,256]{1,0:T(8,128)S(1)}, f32[72,256]{1,0:T(8,128)S(1)}, u32[]{:S(2)}, u32[]{:S(2)}) collective-permute-start(f32[72,256]{1,0:T(8,128)S(1)} %add.65), channel_id=1, source_target_pairs={{0,8},{2,10},{4,12},{6,14},{8,0},{10,2},{12,4},{14,6},{16,24},{18,... | collective-permute-start | bytes 221192 | tf_op jit(solution)/shard_map/ppermute | solution.py:529
  86.0 3.8 %collective-permute-start.11 = (f32[80,128]{1,0:T(8,128)S(1)}, f32[80,128]{1,0:T(8,128)S(1)}, u32[]{:S(2)}, u32[]{:S(2)}) collective-permute-start(f32[80,128]{1,0:T(8,128)S(1)} %add.59), channel_id=1, source_target_pairs={{0,2},{2,0},{4,6},{6,4},{8,10},{10,8},{12,14},{14,12},{16,18},{18,... | collective-permute-start | bytes 122888 | tf_op jit(solution)/shard_map/ppermute | solution.py:529
  86.0 15.2 %collective-permute-start.19 = (f32[128,1024]{1,0:T(8,128)S(1)}, f32[128,1024]{1,0:T(8,128)S(1)}, u32[]{:S(2)}, u32[]{:S(2)}) collective-permute-start(f32[128,1024]{1,0:T(8,128)S(1)} %slice.11), channel_id=1, source_target_pairs={{0,1},{1,0},{2,3},{3,2},{4,5},{5,4},{6,7},{7,6},{8,9},{9,8},{10,11... | collective-permute-start | bytes 1572872 | tf_op jit(solution)/shard_map/ppermute | solution.py:529
  88.5 6.1 %collective-permute-start.17 = (f32[72,256]{1,0:T(8,128)S(1)}, f32[72,256]{1,0:T(8,128)S(1)}, u32[]{:S(2)}, u32[]{:S(2)}) collective-permute-start(f32[72,256]{1,0:T(8,128)S(1)} %add.66), channel_id=1, source_target_pairs={{0,16},{2,18},{4,20},{6,22},{8,24},{10,26},{12,28},{14,30},{16,0},... | collective-permute-start | bytes 221192 | tf_op jit(solution)/shard_map/ppermute | solution.py:529
  94.6 6.6 %collective-permute-start.18 = (f32[72,256]{1,0:T(8,128)S(1)}, f32[72,256]{1,0:T(8,128)S(1)}, u32[]{:S(2)}, u32[]{:S(2)}) collective-permute-start(f32[72,256]{1,0:T(8,128)S(1)} %add.67), channel_id=1, source_target_pairs={{0,2},{2,0},{4,6},{6,4},{8,10},{10,8},{12,14},{14,12},{16,18},{18,... | collective-permute-start | bytes 221192 | tf_op jit(solution)/shard_map/ppermute | solution.py:529

commit v4 on v3

--- a/solution.py
+++ b/solution.py
@@ -103,56 +103,85 @@
     return samples, strip, strip // (2 * TILE)
 
 
-def prepare_kernel(
-    n_ref, dosage_ref, annot_ref, chi_ref, out_ref, annot_out_ref, counts_ref, chi_out_ref, given_annot, came
-):
+def outgoing_kernel(n_ref, dosage_ref, annot_ref, first_ref, second_ref, given_annot, came):
     samples, strip = dosage_ref.shape
     annots = annot_ref.shape[0]
-    block = strip // 2
-    width = out_ref.shape[1]
     n = n_ref[0]
-    column = pl.ds(pl.multiple_of((1 - n) * (strip - width), width), width)
-    rows = pl.ds(pl.multiple_of((1 - n) * block, block), block)
-    copies = [
-        pltpu.make_async_copy(annot_ref, given_annot, came.at[0]),
-        pltpu.make_async_copy(dosage_ref.at[:, column], out_ref.at[:samples, :], came.at[1]),
-        pltpu.make_async_copy(chi_ref.at[rows, :], chi_out_ref, came.at[2]),
-    ]
+    outs = (first_ref, second_ref)
+    copies = []
+    for order, out_ref in enumerate(outs):
+        column = cols_at((1 - n) * (strip // TILE - 1 - order) + n * order)
+        copies += [
+            pltpu.make_async_copy(
+                dosage_ref.at[:, column], out_ref.at[:samples, :], came.at[2 * order]
+            ),
+            pltpu.make_async_copy(
+                annot_ref.at[:, column], given_annot.at[order], came.at[2 * order + 1]
+            ),
+        ]
     for copy in copies:
         copy.start()
+    row = lax.broadcasted_iota(jnp.int32, (PAD, TILE), 0)
+    for order, out_ref in enumerate(outs):
+        out_ref[samples + annots :, :] = jnp.where(row == 0, 1.0, 0.0).astype(jnp.bfloat16)
+        copies[2 * order + 1].wait()
+        out_ref[samples : samples + annots, :] = (
+            given_annot[order].astype(jnp.float32).astype(jnp.bfloat16)
+        )
+    for order in range(2):
+        copies[2 * order].wait()
+
+
+def outgoing_columns(n, dosage, annotations):
+    samples = dosage.shape[0]
+    annots = annotations.shape[0]
+    out = jax.ShapeDtypeStruct((samples + annots + PAD, TILE), jnp.bfloat16)
+    return pl.pallas_call(
+        outgoing_kernel,
+        out_shape=(out, out),
+        in_specs=[in_smem, in_place, in_place],
+        out_specs=(in_vmem, in_vmem),
+        scratch_shapes=[pltpu.VMEM((2, annots, TILE), jnp.int32), pltpu.SemaphoreType.DMA((4,))],
+        cost_estimate=pl.CostEstimate(
+            flops=0, bytes_accessed=8 * samples * TILE, transcendentals=0
+        ),
+        name="outgoing",
+    )(n, dosage, annotations)
+
+
+def prepare_kernel(n_ref, annot_ref, chi_ref, annot_out_ref, counts_ref, chi_out_ref, came):
+    annots, strip = annot_ref.shape
+    block = strip // 2
+    n = n_ref[0]
+    rows = pl.ds(pl.multiple_of((1 - n) * block, block), block)
+    copy = pltpu.make_async_copy(chi_ref.at[rows, :], chi_out_ref, came)
+    copy.start()
     row = lax.broadcasted_iota(jnp.int32, (PAD, strip), 0)
     annot_out_ref[annots:, :] = jnp.where(row == 0, 1.0, 0.0).astype(jnp.bfloat16)
-    copies[0].wait()
-    members = given_annot[...].astype(jnp.float32)
+    members = annot_ref[...].astype(jnp.float32)
     annot_out_ref[:annots, :] = members.astype(jnp.bfloat16)
-    counts = jnp.sum(members, axis=1, keepdims=True)
-    counts_ref[...] = lying(counts)
-    out_ref[samples:, :] = annot_out_ref[:, column]
-    for copy in copies[1:]:
-        copy.wait()
-
-
-def prepared(n, dosage, annotations, chi):
-    samples, strip, _ = sizes(dosage)
-    annots = annotations.shape[0]
-    rows = annots + PAD
-    width = strip // 4
+    counts_ref[...] = lying(jnp.sum(members, axis=1, keepdims=True))
+    copy.wait()
+
+
+def prepared(n, annotations, chi):
+    annots, strip = annotations.shape
     return pl.pallas_call(
         prepare_kernel,
         out_shape=(
-            jax.ShapeDtypeStruct((samples + rows, width), jnp.bfloat16),
-            jax.ShapeDtypeStruct((rows, strip), jnp.bfloat16),
+            jax.ShapeDtypeStruct((annots + PAD, strip), jnp.bfloat16),
             jax.ShapeDtypeStruct((1, annots), jnp.float32),
             jax.ShapeDtypeStruct((strip // 2, chi.shape[1]), jnp.float32),
         ),
-        in_specs=[in_smem, in_place, in_place, in_place],
-        out_specs=(in_vmem,) * 4,
-        scratch_shapes=[pltpu.VMEM(annotations.shape, jnp.int32), pltpu.SemaphoreType.DMA((3,))],
+        in_specs=[in_smem, in_vmem, in_place],
+        out_specs=(in_vmem,) * 3,
+        scratch_shapes=[pltpu.SemaphoreType.DMA],
+        compiler_params=pltpu.CompilerParams(vmem_limit_bytes=VMEM_LIMIT),
         cost_estimate=pl.CostEstimate(
-            flops=0, bytes_accessed=4 * samples * width + 8 * strip * annots, transcendentals=0
+            flops=0, bytes_accessed=16 * strip * annots, transcendentals=0
         ),
         name="prepare",
-    )(n, dosage, annotations, chi)
+    )(n, annotations, chi)
 
 
 def own_kernel(n_ref, dosage_ref, annot_ref, sums_ref, turned_ref, geno, wide_values):
@@ -258,56 +287,50 @@
 
 
 def rim_kernel(
-    n_ref, arrived_ref, turned_ref, annot_ref, sums_in, sums_ref, back_ref, geno, wide_values
+    order, n_ref, arrived_ref, turned_ref, annot_ref, sums_in, sums_ref, back_ref, geno, wide_values
 ):
     mine = turned_ref.shape[0]
     samples = geno.shape[1]
-    width = mine // 2
     n = n_ref[0]
     sums_ref[...] = sums_in[...]
     back_ref[...] = jnp.zeros_like(back_ref)
-    for c in range(width):
-        columns = slice(c * TILE, (c + 1) * TILE)
-        standardized(lambda rows: arrived_ref[rows, columns], into(geno, c), wide_values, samples)
-
-    def add(c, y, inside=None):
-        columns = slice(c * TILE, (c + 1) * TILE)
-        weights = band_weights(rows_of(turned_ref, y), columns_of(geno, c), inside)
-        sums_ref[:, cols_at(y)] += along_columns(arrived_ref[samples:, columns], weights)
-        back_ref[:, columns] += along_rows(annot_ref[:, cols_at(n * mine + y)], weights)
-
-    diagonal = (1 - 2 * n) * tile_offset() <= 0
-    for c in range(width):
-        add(c, c + (1 - n) * width, diagonal)
-        for y in range(mine):
-            first, second = y < c + width, c < y < width
-            if first or second:
-
-                @pl.when(True if first and second else (n == 0 if first else n == 1))
-                def _(c=c, y=y):
-                    add(c, y)
-
-
-def rim_sums(n, arrived, turned, annot, sums):
+    standardized(lambda rows: arrived_ref[rows, :], into(geno, 0), wide_values, samples)
+
+    def add(y, inside=None):
+        weights = band_weights(rows_of(turned_ref, y), columns_of(geno, 0), inside)
+        sums_ref[:, cols_at(y)] += along_columns(arrived_ref[samples:, :], weights)
+        back_ref[...] += along_rows(annot_ref[:, cols_at(n * mine + y)], weights)
+
+    low, high = order, mine - 1 - order
+    add((1 - n) * high + n * low, (1 - 2 * n) * tile_offset() <= 0)
+    for y in range(mine):
+        first, second = y < high, low < y < mine // 2
+        if first or second:
+
+            @pl.when(True if first and second else (n == 0 if first else n == 1))
+            def _(y=y):
+                add(y)
+
+
+def rim_sums(order, n, arrived, turned, annot, sums):
     mine, chunks, _, _ = turned.shape
     samples = chunks * LANES
-    width = mine // 2
-    return pl.pallas_call(
-        rim_kernel,
+    return pl.pallas_call(
+        functools.partial(rim_kernel, order),
         out_shape=(
             jax.ShapeDtypeStruct(sums.shape, jnp.float32),
-            jax.ShapeDtypeStruct((sums.shape[0], width * TILE), jnp.float32),
+            jax.ShapeDtypeStruct((sums.shape[0], TILE), jnp.float32),
         ),
         in_specs=[in_smem] + [in_vmem] * 4,
         out_specs=(in_vmem, in_vmem),
         scratch_shapes=[
-            pltpu.VMEM((2 * width, samples, LANES), jnp.bfloat16),
+            pltpu.VMEM((2, samples, LANES), jnp.bfloat16),
             pltpu.VMEM((samples, TILE), jnp.float32),
         ],
         compiler_params=pltpu.CompilerParams(vmem_limit_bytes=VMEM_LIMIT),
         cost_estimate=pl.CostEstimate(
-            flops=2 * samples * width * TILE * mine * TILE,
-            bytes_accessed=2 * samples * TILE * (mine + width),
+            flops=2 * samples * TILE * mine * TILE,
+            bytes_accessed=2 * samples * TILE * (mine + 1),
             transcendentals=0,
         ),
         name="rim_sums",
@@ -331,14 +354,15 @@
     )
 
 
-def moments_kernel(total_variants, n_ref, w_ref, counts_ref, sums_ref, back_ref, scores_ref, payload_ref, whole):
+def moments_kernel(total_variants, n_ref, w_ref, counts_ref, sums_ref, first_ref, second_ref, scores_ref, payload_ref, whole):
     annots = counts_ref.shape[1]
     block = sums_ref.shape[1]
-    width = back_ref.shape[1]
+    mine = block // TILE
     n = n_ref[0]
     slot = 2 * w_ref[0] + n
     whole[...] = sums_ref[...]
-    whole[:, pl.ds(pl.multiple_of(n * (block - width), width), width)] += back_ref[...]
+    for order, back_ref in enumerate((first_ref, second_ref)):
+        whole[:, cols_at((1 - n) * order + n * (mine - 1 - order))] += back_ref[...]
     shares = upright(counts_ref[...]) / total_variants
     high = (1.0 - shares).astype(jnp.bfloat16).astype(jnp.float32)
     low = (0.0 - shares).astype(jnp.bfloat16).astype(jnp.float32)
@@ -370,7 +394,7 @@
             jax.ShapeDtypeStruct((annots + 2 * PAD, block), jnp.float32),
             jax.ShapeDtypeStruct((annots + slots, annots), jnp.float32),
         ),
-        in_specs=[in_smem] * 2 + [in_vmem] * 3,
+        in_specs=[in_smem] * 2 + [in_vmem] * 4,
         out_specs=(in_vmem, in_vmem),
         scratch_shapes=[pltpu.VMEM(sums.shape, jnp.float32)],
         compiler_params=pltpu.CompilerParams(vmem_limit_bytes=VMEM_LIMIT),
@@ -378,7 +402,7 @@
             flops=12 * annots * annots * block, bytes_accessed=12 * annots * block, transcendentals=0
         ),
         name="moments",
-    )(n, w, counts, sums, back)
+    )(n, w, counts, sums, *back)
 
 
 def inverse_kernel(divisor, payload_ref, inverse_ref, moments_ref):
@@ -555,7 +579,8 @@
 
 
 def wide_sum(value):
-    for bit in wide_bits():
+    bits = wide_bits()
+    for bit in bits[:1] + bits[2:] + bits[1:2]:
         value = added(value, flipped(value, "wide", bit))
     return value
 
@@ -598,16 +623,20 @@
         rim_pairs += [(2 * i, 2 * i + 2), (2 * i + 3, 2 * i + 1)]
         back_pairs += [(2 * i + 1, 2 * i + 2), (2 * i + 2, 2 * i + 1)]
     chi = test_statistic_table
-    outgoing, annot, counts, chi_given = prepared(n_array, dosage, annotations, chi)
-    arrived = lax.ppermute(outgoing, both, rim_pairs)
+    arrived = []
+    for outgoing in outgoing_columns(n_array, dosage, annotations):
+        arrived.append(lax.ppermute(outgoing, both, rim_pairs))
+    annot, counts, chi_given = prepared(n_array, annotations, chi)
     chi_other = flipped(chi_given, "narrow", 1)
     counts = wide_sum(counts)
     sums, turned = own_sums(n_array, dosage, annot)
     tiles = block // TILE
-    sums = other_sums(tuple(range(tiles // 2)), n_array, dosage, annot, turned, sums)
-    sums, back = rim_sums(n_array, arrived, turned, annot, sums)
-    back = lax.ppermute(back, both, back_pairs)
-    sums = other_sums(tuple(range(tiles // 2, tiles)), n_array, dosage, annot, turned, sums)
+    pieces = tuple(range(tiles // 2)), tuple(range(tiles // 2, tiles))
+    back = []
+    for order in range(2):
+        sums, part = rim_sums(order, n_array, arrived[order], turned, annot, sums)
+        back.append(lax.ppermute(part, both, back_pairs))
+        sums = other_sums(pieces[order], n_array, dosage, annot, turned, sums)
 
     w_array = jnp.reshape(w, (1,)).astype(jnp.int32)
     extended, payload = moments_of(

time: 104 us -> 115 us (1.11)
  starting transfers between devices: 27.9 us -> 34.2 us
  Pallas kernels: 39.2 us -> 42.2 us
    ppermute x2 -> x4, starting transfers between devices: 3.4 us -> 9.45 us  [the longest x2 7.93 us: whole_step(): arrived.append(lax.ppermute(outgoing, both, rim_pairs))]
    pallas_call x2 -> x4, Pallas kernels: 10.6 us -> 13.6 us  [the longest x2 9.11 us: rim_sums(): pl.pallas_call(functools.partial(rim_kernel, order), out_shape=(jax.Shape...]
    unnamed x18 -> x16, local copies, waits for them, and re-layouts: 12 us -> 12.1 us
  transfers between devices with their start and end apart: 20 -> 22, of which waited for: 10 -> 10; matrix products, arithmetic and copies ran while one was open for 1% -> 1% of each run, Pallas kernels for 31% -> 32%
where the time goes in v4:
time: 115 us; the launch traced here: 114 us
  Pallas kernels  42.2 us (37%)
  starting transfers between devices  34.2 us (30%)
  waiting for transfers between devices  22.4 us (19%)
  local copies, waits for them, and re-layouts  12.2 us (11%)
  matrix products  2.09 us (2%)
    ppermute x18, starting transfers between devices, flipped(): return lax.ppermute(value, axis, [(i, i ^ bit) for i in range(length)])  24.7 us
    ppermute x18, waiting for transfers between devices, flipped(): return lax.ppermute(value, axis, [(i, i ^ bit) for i in range(length)])  22.4 us
    unnamed x16, local copies, waits for them, and re-layouts  12.1 us
    pallas_call x2, Pallas kernels, other_sums(): pl.pallas_call(functools.partial(other_kernel, slots), out_shape=jax.Shap...  9.39 us
    pallas_call x1, Pallas kernels, own_sums(): pl.pallas_call(own_kernel, out_shape=(jax.ShapeDtypeStruct((annot.shape[0...  9.22 us
    pallas_call x2, Pallas kernels, rim_sums(): pl.pallas_call(functools.partial(rim_kernel, order), out_shape=(jax.Shape...  9.11 us
    ppermute x2, starting transfers between devices, whole_step(): arrived.append(lax.ppermute(outgoing, both, rim_pairs))  7.93 us
    pallas_call x1, Pallas kernels, gram_inverse(): pl.pallas_call(functools.partial(inverse_kernel, divisor), out_shape=(squ...  6.54 us
  transfers between devices with their start and end apart: 22, of which 10 were waited for; matrix products, arithmetic and copies ran while one was open for 1% of the time, Pallas kernels for 32%

profile of v4, /device:TPU:0, one launch (start us, length us, event | category | flops | bytes accessed | tf_op | source)
XLA Modules:
  0.0 114.1 jit_solution(14421276532810544505)
XLA Ops:
  0.6 3.2 %outgoing.1 = (bf16[2184,256]{1,0:T(8,128)(2,1)}, bf16[2184,256]{1,0:T(8,128)(2,1)}) custom-call(s32[1]{0:T(128)} %bitcast.n_ref, bf16[2048,2048]{1,0:T(8,128)(2,1)} %dosage_ref.7, s32[128,2048]{1,0:T(8,128)} %annot_ref.3), custom_call_target="tpu_custom_call" | custom-call | bytes 4194304 | tf_op jit(solution)/shard_map/outgoing/pallas_call | solution.py:139
  3.9 3.4 %collective-permute-start.5 = (bf16[2184,256]{1,0:T(8,128)(2,1)}, bf16[2184,256]{1,0:T(8,128)(2,1)}, u32[]{:S(2)}, u32[]{:S(2)}) collective-permute-start(bf16[2184,256]{1,0:T(8,128)(2,1)} %get-tuple-element.21), channel_id=1, source_target_pairs={{0,2},{3,1},{2,4},{5,3},{4,6},{7,5},{6,8},{9,7},{8,10},{11,9},{10,... | collective-permute-start | bytes 3354632 | tf_op jit(solution)/shard_map/ppermute | solution.py:628
  7.3 4.5 %collective-permute-start.4 = (bf16[2184,256]{1,0:T(8,128)(2,1)}, bf16[2184,256]{1,0:T(8,128)(2,1)}, u32[]{:S(2)}, u32[]{:S(2)}) collective-permute-start(bf16[2184,256]{1,0:T(8,128)(2,1)} %get-tuple-element.20), channel_id=1, source_target_pairs={{0,2},{3,1},{2,4},{5,3},{4,6},{7,5},{6,8},{9,7},{8,10},{11,9},{10,... | collective-permute-start | bytes 3354632 | tf_op jit(solution)/shard_map/ppermute | solution.py:628
  11.8 1.2 %copy-done.7 = s32[128,2048]{1,0:T(8,128)S(1)} copy-done((s32[128,2048]{1,0:T(8,128)S(1)}, s32[128,2048]{1,0:T(8,128)}, u32[]{:S(2)}) %copy-start.7) | copy-done | bytes 1048600
  13.0 1.3 %prepare.1 = (bf16[136,2048]{1,0:T(8,128)(2,1)S(1)}, f32[1,128]{1,0:T(1,128)S(1)}, f32[1024,256]{1,0:T(8,128)}) custom-call(s32[1]{0:T(128)} %bitcast.n_ref, s32[128,2048]{1,0:T(8,128)S(1)} %copy-done.7, f32[2048,256]{1,0:T(8,128)S(1)} %copy-done.6), custom_call_target="tpu_custom_call" | custom-call | bytes 4194304 | tf_op jit(solution)/shard_map/prepare/pallas_call | solution.py:169
  14.3 0.1 collective-permute-start
  14.4 0.1 collective-permute-start.14
  14.5 3.4 %copy-done.3 = bf16[2048,2048]{1,0:T(8,128)(2,1)S(1)} copy-done((bf16[2048,2048]{1,0:T(8,128)(2,1)S(1)}, bf16[2048,2048]{1,0:T(8,128)(2,1)}, u32[]{:S(2)}) %copy-start.3) | copy-done | bytes 8388632
  17.9 9.2 %own_sums.1 = (f32[136,1024]{1,0:T(8,128)S(1)}, bf16[4,16,256,128]{3,2,1,0:T(8,128)(2,1)S(1)}) custom-call(s32[1]{0:T(128)} %bitcast.n_ref, bf16[2048,2048]{1,0:T(8,128)(2,1)S(1)} %copy-done.3, bf16[136,2048]{1,0:T(8,128)(2,1)S(1)} %get-tuple-element.18.annot_ref), custom_call_target="tpu_custom_call" | custom-call | flops 4294967296 | bytes 8388608 | tf_op jit(solution)/shard_map/own_sums/pallas_call | solution.py:246
  27.1 2.0 %copy-done = bf16[4,16,256,128]{3,2,1,0:T(8,128)(2,1)} copy-done((bf16[4,16,256,128]{3,2,1,0:T(8,128)(2,1)}, bf16[4,16,256,128]{3,2,1,0:T(8,128)(2,1)S(1)}, u32[]{:S(2)}) %copy-start) | copy-done | bytes 4194328
  29.1 2.0 %collective-permute-start.1 = (f32[1,128]{1,0:T(1,128)S(1)}, f32[1,128]{1,0:T(1,128)S(1)}, u32[]{:S(2)}, u32[]{:S(2)}) collective-permute-start(f32[1,128]{1,0:T(1,128)S(1)} %added.4.first_ref), channel_id=1, source_target_pairs={{0,8},{2,10},{4,12},{6,14},{8,0},{10,2},{12,4},{14,6},{16,24},{18,... | collective-permute-start | bytes 1544 | tf_op jit(solution)/shard_map/ppermute | solution.py:553
  31.0 1.6 %collective-permute-done.1.second_ref = f32[1,128]{1,0:T(1,128)S(1)} collective-permute-done((f32[1,128]{1,0:T(1,128)S(1)}, f32[1,128]{1,0:T(1,128)S(1)}, u32[]{:S(2)}, u32[]{:S(2)}) %collective-permute-start.1) | collective-permute-done | bytes 544 | tf_op jit(solution)/shard_map/ppermute | solution.py:553
  32.6 3.0 %collective-permute-start.2 = (f32[1,128]{1,0:T(1,128)S(1)}, f32[1,128]{1,0:T(1,128)S(1)}, u32[]{:S(2)}, u32[]{:S(2)}) collective-permute-start(f32[1,128]{1,0:T(1,128)S(1)} %added.5.first_ref), channel_id=1, source_target_pairs={{0,16},{2,18},{4,20},{6,22},{8,24},{10,26},{12,28},{14,30},{16,0},... | collective-permute-start | bytes 1544 | tf_op jit(solution)/shard_map/ppermute | solution.py:553
  35.6 1.5 %collective-permute-done.2.second_ref = f32[1,128]{1,0:T(1,128)S(1)} collective-permute-done((f32[1,128]{1,0:T(1,128)S(1)}, f32[1,128]{1,0:T(1,128)S(1)}, u32[]{:S(2)}, u32[]{:S(2)}) %collective-permute-start.2) | collective-permute-done | bytes 544 | tf_op jit(solution)/shard_map/ppermute | solution.py:553
  37.2 1.4 %collective-permute-start.3 = (f32[1,128]{1,0:T(1,128)S(1)}, f32[1,128]{1,0:T(1,128)S(1)}, u32[]{:S(2)}, u32[]{:S(2)}) collective-permute-start(f32[1,128]{1,0:T(1,128)S(1)} %added.6.first_ref), channel_id=1, source_target_pairs={{0,4},{2,6},{4,0},{6,2},{8,12},{10,14},{12,8},{14,10},{16,20},{18,... | collective-permute-start | bytes 1544 | tf_op jit(solution)/shard_map/ppermute | solution.py:553
  38.5 2.2 %collective-permute-done.3.second_ref = f32[1,128]{1,0:T(1,128)S(1)} collective-permute-done((f32[1,128]{1,0:T(1,128)S(1)}, f32[1,128]{1,0:T(1,128)S(1)}, u32[]{:S(2)}, u32[]{:S(2)}) %collective-permute-start.3) | collective-permute-done | bytes 544 | tf_op jit(solution)/shard_map/ppermute | solution.py:553
  40.7 2.2 %copy-done.1 = bf16[4,16,256,128]{3,2,1,0:T(8,128)(2,1)S(1)} copy-done((bf16[4,16,256,128]{3,2,1,0:T(8,128)(2,1)S(1)}, bf16[4,16,256,128]{3,2,1,0:T(8,128)(2,1)}, u32[]{:S(2)}) %copy-start.1) | copy-done | bytes 4194328
  42.9 4.9 %rim_sums.2 = (f32[136,1024]{1,0:T(8,128)S(1)}, f32[136,256]{1,0:T(8,128)S(1)}) custom-call(s32[1]{0:T(128)} %bitcast.n_ref, bf16[2184,256]{1,0:T(8,128)(2,1)} %collective-permute-done.5.arrived_ref, bf16[4,16,256,128]{3,2,1,0:T(8,128)(2,1)S(1)} %copy-done.1, bf16[136,2048]{1,0:T(8,128)(2,1)S(1)} %get-tuple-element.18.annot_ref, ...), custom_call_target="tpu_custom_call" | custom-call | flops 1073741824 | bytes 5242880 | tf_op jit(solution)/shard_map/rim_sums/pallas_call | solution.py:318
  47.9 3.4 %copy-done.4 = bf16[2048,2048]{1,0:T(8,128)(2,1)S(1)} copy-done((bf16[2048,2048]{1,0:T(8,128)(2,1)S(1)}, bf16[2048,2048]{1,0:T(8,128)(2,1)}, u32[]{:S(2)}) %copy-start.4) | copy-done | bytes 8388632
  51.3 6.1 %other_sums.2.sums_in = f32[136,1024]{1,0:T(8,128)S(1)} custom-call(s32[1]{0:T(128)} %bitcast.n_ref, bf16[2048,2048]{1,0:T(8,128)(2,1)S(1)} %copy-done.4, bf16[136,2048]{1,0:T(8,128)(2,1)S(1)} %get-tuple-element.18.annot_ref, bf16[4,16,256,128]{3,2,1,0:T(8,128)(2,1)S(1)} %copy-done.2, f32[136,1024]{1,0:T(8,128)S(1)} %get-tuple-element.23.sums_in), custom_call_target="tpu_custom_call" | custom-call | flops 4294967296 | bytes 8388608 | tf_op jit(solution)/shard_map/other_sums/pallas_call | solution.py:262
  57.4 4.2 %rim_sums.3 = (f32[136,1024]{1,0:T(8,128)S(1)}, f32[136,256]{1,0:T(8,128)S(1)}) custom-call(s32[1]{0:T(128)} %bitcast.n_ref, bf16[2184,256]{1,0:T(8,128)(2,1)} %collective-permute-done.4.arrived_ref, bf16[4,16,256,128]{3,2,1,0:T(8,128)(2,1)S(1)} %copy-done.2, bf16[136,2048]{1,0:T(8,128)(2,1)S(1)} %get-tuple-element.18.annot_ref, ...), custom_call_target="tpu_custom_call" | custom-call | flops 1073741824 | bytes 5242880 | tf_op jit(solution)/shard_map/rim_sums/pallas_call | solution.py:318
  61.6 0.7 collective-permute-start.7
  62.2 0.8 collective-permute-start.6
  63.1 3.3 %other_sums.3.sums_ref = f32[136,1024]{1,0:T(8,128)S(1)} custom-call(s32[1]{0:T(128)} %bitcast.n_ref, bf16[2048,2048]{1,0:T(8,128)(2,1)S(1)} %copy-done.5, bf16[136,2048]{1,0:T(8,128)(2,1)S(1)} %get-tuple-element.18.annot_ref, bf16[4,16,256,128]{3,2,1,0:T(8,128)(2,1)S(1)} %copy-done.2, f32[136,1024]{1,0:T(8,128)S(1)} %get-tuple-element.24.sums_in), custom_call_target="tpu_custom_call" | custom-call | flops 4294967296 | bytes 8388608 | tf_op jit(solution)/shard_map/other_sums/pallas_call | solution.py:262
  66.4 0.9 moments.1
  67.3 0.4 fusion
  67.7 1.7 %fusion.6 = f32[144,256]{1,0:T(8,128)S(1)} fusion(f32[144,1024]{1,0:T(8,128)S(1)} %get-tuple-element.30.scores_ref, f32[1024,256]{1,0:T(8,128)} %collective-permute-done.14), kind=kOutput, calls=%fused_computation.15 | convolution fusion | flops 226492416 | bytes 1785856 | tf_op jit(solution)/shard_map/dot_general | solution.py:652
  69.4 4.8 %collective-permute-start.15 = (f32[72,512]{1,0:T(8,128)S(1)}, f32[72,512]{1,0:T(8,128)S(1)}, u32[]{:S(2)}, u32[]{:S(2)}) collective-permute-start(f32[72,512]{1,0:T(8,128)S(1)} %fusion.2), channel_id=1, source_target_pairs={{0,2},{2,0},{4,6},{6,4},{8,10},{10,8},{12,14},{14,12},{16,18},{18,... | collective-permute-start | bytes 442376 | tf_op jit(solution)/shard_map/ppermute | solution.py:553
  74.3 0.1 collective-permute-start.8
  74.4 0.9 collective-permute-done.15
  75.3 2.6 %collective-permute-start.16 = (f32[72,256]{1,0:T(8,128)S(1)}, f32[72,256]{1,0:T(8,128)S(1)}, u32[]{:S(2)}, u32[]{:S(2)}) collective-permute-start(f32[72,256]{1,0:T(8,128)S(1)} %slice.13), channel_id=1, source_target_pairs={{0,1},{1,0},{2,3},{3,2},{4,5},{5,4},{6,7},{7,6},{8,9},{9,8},{10,11... | collective-permute-start | bytes 221192 | tf_op jit(solution)/shard_map/ppermute | solution.py:553
  77.9 0.2 collective-permute-start.9
  78.1 3.9 %collective-permute-done.9 = f32[80,128]{1,0:T(8,128)S(1)} collective-permute-done((f32[80,128]{1,0:T(8,128)S(1)}, f32[80,128]{1,0:T(8,128)S(1)}, u32[]{:S(2)}, u32[]{:S(2)}) %collective-permute-start.9) | collective-permute-done | bytes 40992 | tf_op jit(solution)/shard_map/ppermute | solution.py:553
  82.0 2.9 %collective-permute-start.10 = (f32[80,128]{1,0:T(8,128)S(1)}, f32[80,128]{1,0:T(8,128)S(1)}, u32[]{:S(2)}, u32[]{:S(2)}) collective-permute-start(f32[80,128]{1,0:T(8,128)S(1)} %add.56), channel_id=1, source_target_pairs={{0,4},{2,6},{4,0},{6,2},{8,12},{10,14},{12,8},{14,10},{16,20},{18,... | collective-permute-start | bytes 122888 | tf_op jit(solution)/shard_map/ppermute | solution.py:553
  84.9 0.1 collective-permute-start.17
  85.0 2.3 %collective-permute-done.10 = f32[80,128]{1,0:T(8,128)S(1)} collective-permute-done((f32[80,128]{1,0:T(8,128)S(1)}, f32[80,128]{1,0:T(8,128)S(1)}, u32[]{:S(2)}, u32[]{:S(2)}) %collective-permute-start.10) | collective-permute-done | bytes 40992 | tf_op jit(solution)/shard_map/ppermute | solution.py:553
  87.3 1.6 %collective-permute-start.11 = (f32[80,128]{1,0:T(8,128)S(1)}, f32[80,128]{1,0:T(8,128)S(1)}, u32[]{:S(2)}, u32[]{:S(2)}) collective-permute-start(f32[80,128]{1,0:T(8,128)S(1)} %add.57), channel_id=1, source_target_pairs={{0,8},{2,10},{4,12},{6,14},{8,0},{10,2},{12,4},{14,6},{16,24},{18,... | collective-permute-start | bytes 122888 | tf_op jit(solution)/shard_map/ppermute | solution.py:553
  88.9 2.4 %collective-permute-done.11 = f32[80,128]{1,0:T(8,128)S(1)} collective-permute-done((f32[80,128]{1,0:T(8,128)S(1)}, f32[80,128]{1,0:T(8,128)S(1)}, u32[]{:S(2)}, u32[]{:S(2)}) %collective-permute-start.11) | collective-permute-done | bytes 40992 | tf_op jit(solution)/shard_map/ppermute | solution.py:553
  91.3 3.0 %collective-permute-start.12 = (f32[80,128]{1,0:T(8,128)S(1)}, f32[80,128]{1,0:T(8,128)S(1)}, u32[]{:S(2)}, u32[]{:S(2)}) collective-permute-start(f32[80,128]{1,0:T(8,128)S(1)} %add.58), channel_id=1, source_target_pairs={{0,16},{2,18},{4,20},{6,22},{8,24},{10,26},{12,28},{14,30},{16,0},... | collective-permute-start | bytes 122888 | tf_op jit(solution)/shard_map/ppermute | solution.py:553
  94.3 0.7 collective-permute-start.18
  95.1 1.2 %collective-permute-done.12 = f32[80,128]{1,0:T(8,128)S(1)} collective-permute-done((f32[80,128]{1,0:T(8,128)S(1)}, f32[80,128]{1,0:T(8,128)S(1)}, u32[]{:S(2)}, u32[]{:S(2)}) %collective-permute-start.12) | collective-permute-done | bytes 40992 | tf_op jit(solution)/shard_map/ppermute | solution.py:553
  96.4 0.9 collective-permute-start.21
  97.3 1.5 %collective-permute-done.18 = f32[72,256]{1,0:T(8,128)S(1)} collective-permute-done((f32[72,256]{1,0:T(8,128)S(1)}, f32[72,256]{1,0:T(8,128)S(1)}, u32[]{:S(2)}, u32[]{:S(2)}) %collective-permute-start.18) | collective-permute-done | bytes 73760 | tf_op jit(solution)/shard_map/ppermute | solution.py:553
  98.8 1.3 %collective-permute-start.19 = (f32[72,256]{1,0:T(8,128)S(1)}, f32[72,256]{1,0:T(8,128)S(1)}, u32[]{:S(2)}, u32[]{:S(2)}) collective-permute-start(f32[72,256]{1,0:T(8,128)S(1)} %add.66), channel_id=1, source_target_pairs={{0,16},{2,18},{4,20},{6,22},{8,24},{10,26},{12,28},{14,30},{16,0},... | collective-permute-start | bytes 221192 | tf_op jit(solution)/shard_map/ppermute | solution.py:553
  100.1 4.8 %collective-permute-done.19 = f32[72,256]{1,0:T(8,128)S(1)} collective-permute-done((f32[72,256]{1,0:T(8,128)S(1)}, f32[72,256]{1,0:T(8,128)S(1)}, u32[]{:S(2)}, u32[]{:S(2)}) %collective-permute-start.19) | collective-permute-done | bytes 73760 | tf_op jit(solution)/shard_map/ppermute | solution.py:553
  104.9 0.1 collective-permute-start.20
  105.0 6.5 %gram_inverse.1 = (f32[128,128]{1,0:T(8,128)S(1)}, f32[128,128]{1,0:T(8,128)S(1)}) custom-call(f32[160,128]{1,0:T(8,128)S(1)} %maximum_select_fusion.1.payload_ref), custom_call_target="tpu_custom_call" | custom-call | flops 20000000000 | bytes 65536 | tf_op jit(solution)/shard_map/gram_inverse/pallas_call | solution.py:484
  111.6 2.6 %fitted_values.1 = (f32[128,1024]{1,0:T(8,128)}, f32[2048,256]{1,0:T(8,128)}) custom-call(s32[1]{0:T(128)} %bitcast.n_ref, f32[128,128]{1,0:T(8,128)S(1)} %get-tuple-element.28.inverse_ref, f32[128,128]{1,0:T(8,128)S(1)} %get-tuple-element.29.moments_ref, f32[144,256]{1,0:T(8,128)S(1)} %maximum_select_fusion.proj_ref, ...), custom_call_target="tpu_custom_call" | custom-call | flops 134217728 | bytes 2097152 | tf_op jit(solution)/shard_map/fitted_values/pallas_call | solution.py:535
  (44 shorter events, 0.3 us)
Async XLA Ops:
  0.6 11.2 %copy-start.6 = (f32[2048,256]{1,0:T(8,128)S(1)}, f32[2048,256]{1,0:T(8,128)}, u32[]{:S(2)}) copy-start(f32[2048,256]{1,0:T(8,128)} %chi_ref.1) | copy-start | bytes 6291460
  3.9 36.9 %collective-permute-start.5 = (bf16[2184,256]{1,0:T(8,128)(2,1)}, bf16[2184,256]{1,0:T(8,128)(2,1)}, u32[]{:S(2)}, u32[]{:S(2)}) collective-permute-start(bf16[2184,256]{1,0:T(8,128)(2,1)} %get-tuple-element.21), channel_id=1, source_target_pairs={{0,2},{3,1},{2,4},{5,3},{4,6},{7,5},{6,8},{9,7},{8,10},{11,9},{10,... | collective-permute-start | bytes 3354632 | tf_op jit(solution)/shard_map/ppermute | solution.py:628
  7.3 50.1 %collective-permute-start.4 = (bf16[2184,256]{1,0:T(8,128)(2,1)}, bf16[2184,256]{1,0:T(8,128)(2,1)}, u32[]{:S(2)}, u32[]{:S(2)}) collective-permute-start(bf16[2184,256]{1,0:T(8,128)(2,1)} %get-tuple-element.20), channel_id=1, source_target_pairs={{0,2},{3,1},{2,4},{5,3},{4,6},{7,5},{6,8},{9,7},{8,10},{11,9},{10,... | collective-permute-start | bytes 3354632 | tf_op jit(solution)/shard_map/ppermute | solution.py:628
  11.8 1.2 %copy-start.7 = (s32[128,2048]{1,0:T(8,128)S(1)}, s32[128,2048]{1,0:T(8,128)}, u32[]{:S(2)}) copy-start(s32[128,2048]{1,0:T(8,128)} %annot_ref.3) | copy-start | bytes 3145732
  14.3 14.7 %collective-permute-start = (f32[1,128]{1,0:T(1,128)S(1)}, f32[1,128]{1,0:T(1,128)S(1)}, u32[]{:S(2)}, u32[]{:S(2)}) collective-permute-start(f32[1,128]{1,0:T(1,128)S(1)} %get-tuple-element.17.first_ref), channel_id=1, source_target_pairs={{0,2},{2,0},{4,6},{6,4},{8,10},{10,8},{12,14},{14,12},{16,18},{18,... | collective-permute-start | bytes 1544 | tf_op jit(solution)/shard_map/ppermute | solution.py:553
  14.4 53.3 %collective-permute-start.14 = (f32[1024,256]{1,0:T(8,128)}, f32[1024,256]{1,0:T(8,128)}, u32[]{:S(2)}, u32[]{:S(2)}) collective-permute-start(f32[1024,256]{1,0:T(8,128)} %get-tuple-element.31), channel_id=1, source_target_pairs={{0,1},{1,0},{2,3},{3,2},{4,5},{5,4},{6,7},{7,6},{8,9},{9,8},{10,11... | collective-permute-start | bytes 3145736 | tf_op jit(solution)/shard_map/ppermute | solution.py:553
  14.5 3.4 %copy-start.3 = (bf16[2048,2048]{1,0:T(8,128)(2,1)S(1)}, bf16[2048,2048]{1,0:T(8,128)(2,1)}, u32[]{:S(2)}) copy-start(bf16[2048,2048]{1,0:T(8,128)(2,1)} %dosage_ref.7) | copy-start | bytes 25165828
  27.1 2.0 %copy-start = (bf16[4,16,256,128]{3,2,1,0:T(8,128)(2,1)}, bf16[4,16,256,128]{3,2,1,0:T(8,128)(2,1)S(1)}, u32[]{:S(2)}) copy-start(bf16[4,16,256,128]{3,2,1,0:T(8,128)(2,1)S(1)} %get-tuple-element.19.turned_ref) | copy-start | bytes 12582916
  29.1 3.6 %collective-permute-start.1 = (f32[1,128]{1,0:T(1,128)S(1)}, f32[1,128]{1,0:T(1,128)S(1)}, u32[]{:S(2)}, u32[]{:S(2)}) collective-permute-start(f32[1,128]{1,0:T(1,128)S(1)} %added.4.first_ref), channel_id=1, source_target_pairs={{0,8},{2,10},{4,12},{6,14},{8,0},{10,2},{12,4},{14,6},{16,24},{18,... | collective-permute-start | bytes 1544 | tf_op jit(solution)/shard_map/ppermute | solution.py:553
  32.6 4.5 %collective-permute-start.2 = (f32[1,128]{1,0:T(1,128)S(1)}, f32[1,128]{1,0:T(1,128)S(1)}, u32[]{:S(2)}, u32[]{:S(2)}) collective-permute-start(f32[1,128]{1,0:T(1,128)S(1)} %added.5.first_ref), channel_id=1, source_target_pairs={{0,16},{2,18},{4,20},{6,22},{8,24},{10,26},{12,28},{14,30},{16,0},... | collective-permute-start | bytes 1544 | tf_op jit(solution)/shard_map/ppermute | solution.py:553
  37.2 3.6 %collective-permute-start.3 = (f32[1,128]{1,0:T(1,128)S(1)}, f32[1,128]{1,0:T(1,128)S(1)}, u32[]{:S(2)}, u32[]{:S(2)}) collective-permute-start(f32[1,128]{1,0:T(1,128)S(1)} %added.6.first_ref), channel_id=1, source_target_pairs={{0,4},{2,6},{4,0},{6,2},{8,12},{10,14},{12,8},{14,10},{16,20},{18,... | collective-permute-start | bytes 1544 | tf_op jit(solution)/shard_map/ppermute | solution.py:553
  40.7 2.2 %copy-start.1 = (bf16[4,16,256,128]{3,2,1,0:T(8,128)(2,1)S(1)}, bf16[4,16,256,128]{3,2,1,0:T(8,128)(2,1)}, u32[]{:S(2)}) copy-start(bf16[4,16,256,128]{3,2,1,0:T(8,128)(2,1)} %copy-done) | copy-start | bytes 12582916
  42.9 4.9 %copy-start.2 = (bf16[4,16,256,128]{3,2,1,0:T(8,128)(2,1)S(1)}, bf16[4,16,256,128]{3,2,1,0:T(8,128)(2,1)}, u32[]{:S(2)}) copy-start(bf16[4,16,256,128]{3,2,1,0:T(8,128)(2,1)} %copy-done) | copy-start | bytes 12582916
  47.9 3.4 %copy-start.4 = (bf16[2048,2048]{1,0:T(8,128)(2,1)S(1)}, bf16[2048,2048]{1,0:T(8,128)(2,1)}, u32[]{:S(2)}) copy-start(bf16[2048,2048]{1,0:T(8,128)(2,1)} %dosage_ref.7) | copy-start | bytes 25165828
  51.3 11.8 %copy-start.5 = (bf16[2048,2048]{1,0:T(8,128)(2,1)S(1)}, bf16[2048,2048]{1,0:T(8,128)(2,1)}, u32[]{:S(2)}) copy-start(bf16[2048,2048]{1,0:T(8,128)(2,1)} %dosage_ref.7) | copy-start | bytes 25165828
  61.6 4.8 %collective-permute-start.7 = (f32[136,256]{1,0:T(8,128)S(1)}, f32[136,256]{1,0:T(8,128)S(1)}, u32[]{:S(2)}, u32[]{:S(2)}) collective-permute-start(f32[136,256]{1,0:T(8,128)S(1)} %get-tuple-element.26), channel_id=1, source_target_pairs={{1,2},{2,1},{3,4},{4,3},{5,6},{6,5},{7,8},{8,7},{9,10},{10,9},{11,... | collective-permute-start | bytes 417800 | tf_op jit(solution)/shard_map/ppermute | solution.py:638
  62.2 4.2 %collective-permute-start.6 = (f32[136,256]{1,0:T(8,128)S(1)}, f32[136,256]{1,0:T(8,128)S(1)}, u32[]{:S(2)}, u32[]{:S(2)}) collective-permute-start(f32[136,256]{1,0:T(8,128)S(1)} %get-tuple-element.25), channel_id=1, source_target_pairs={{1,2},{2,1},{3,4},{4,3},{5,6},{6,5},{7,8},{8,7},{9,10},{10,9},{11,... | collective-permute-start | bytes 417800 | tf_op jit(solution)/shard_map/ppermute | solution.py:638
  69.4 5.8 %collective-permute-start.15 = (f32[72,512]{1,0:T(8,128)S(1)}, f32[72,512]{1,0:T(8,128)S(1)}, u32[]{:S(2)}, u32[]{:S(2)}) collective-permute-start(f32[72,512]{1,0:T(8,128)S(1)} %fusion.2), channel_id=1, source_target_pairs={{0,2},{2,0},{4,6},{6,4},{8,10},{10,8},{12,14},{14,12},{16,18},{18,... | collective-permute-start | bytes 442376 | tf_op jit(solution)/shard_map/ppermute | solution.py:553
  74.3 3.6 %collective-permute-start.8 = (f32[80,128]{1,0:T(8,128)S(1)}, f32[80,128]{1,0:T(8,128)S(1)}, u32[]{:S(2)}, u32[]{:S(2)}) collective-permute-start(f32[80,128]{1,0:T(8,128)S(1)} %constant_dynamic-slice_fusion), channel_id=1, source_target_pairs={{0,2},{2,0},{4,6},{6,4},{8,10},{10,8},{12,14},{14,12},{16,18},{18,... | collective-permute-start | bytes 122888 | tf_op jit(solution)/shard_map/ppermute | solution.py:553
  75.3 9.6 %collective-permute-start.16 = (f32[72,256]{1,0:T(8,128)S(1)}, f32[72,256]{1,0:T(8,128)S(1)}, u32[]{:S(2)}, u32[]{:S(2)}) collective-permute-start(f32[72,256]{1,0:T(8,128)S(1)} %slice.13), channel_id=1, source_target_pairs={{0,1},{1,0},{2,3},{3,2},{4,5},{5,4},{6,7},{7,6},{8,9},{9,8},{10,11... | collective-permute-start | bytes 221192 | tf_op jit(solution)/shard_map/ppermute | solution.py:553
  77.9 4.1 %collective-permute-start.9 = (f32[80,128]{1,0:T(8,128)S(1)}, f32[80,128]{1,0:T(8,128)S(1)}, u32[]{:S(2)}, u32[]{:S(2)}) collective-permute-start(f32[80,128]{1,0:T(8,128)S(1)} %dynamic-slice_add_fusion), channel_id=1, source_target_pairs={{0,1},{1,0},{2,3},{3,2},{4,5},{5,4},{6,7},{7,6},{8,9},{9,8},{10,11... | collective-permute-start | bytes 122888 | tf_op jit(solution)/shard_map/ppermute | solution.py:553
  82.0 5.3 %collective-permute-start.10 = (f32[80,128]{1,0:T(8,128)S(1)}, f32[80,128]{1,0:T(8,128)S(1)}, u32[]{:S(2)}, u32[]{:S(2)}) collective-permute-start(f32[80,128]{1,0:T(8,128)S(1)} %add.56), channel_id=1, source_target_pairs={{0,4},{2,6},{4,0},{6,2},{8,12},{10,14},{12,8},{14,10},{16,20},{18,... | collective-permute-start | bytes 122888 | tf_op jit(solution)/shard_map/ppermute | solution.py:553
  84.9 9.4 %collective-permute-start.17 = (f32[72,256]{1,0:T(8,128)S(1)}, f32[72,256]{1,0:T(8,128)S(1)}, u32[]{:S(2)}, u32[]{:S(2)}) collective-permute-start(f32[72,256]{1,0:T(8,128)S(1)} %slice_add_fusion), channel_id=1, source_target_pairs={{0,4},{2,6},{4,0},{6,2},{8,12},{10,14},{12,8},{14,10},{16,20},{18,... | collective-permute-start | bytes 221192 | tf_op jit(solution)/shard_map/ppermute | solution.py:553
  87.3 4.0 %collective-permute-start.11 = (f32[80,128]{1,0:T(8,128)S(1)}, f32[80,128]{1,0:T(8,128)S(1)}, u32[]{:S(2)}, u32[]{:S(2)}) collective-permute-start(f32[80,128]{1,0:T(8,128)S(1)} %add.57), channel_id=1, source_target_pairs={{0,8},{2,10},{4,12},{6,14},{8,0},{10,2},{12,4},{14,6},{16,24},{18,... | collective-permute-start | bytes 122888 | tf_op jit(solution)/shard_map/ppermute | solution.py:553
  91.3 5.0 %collective-permute-start.12 = (f32[80,128]{1,0:T(8,128)S(1)}, f32[80,128]{1,0:T(8,128)S(1)}, u32[]{:S(2)}, u32[]{:S(2)}) collective-permute-start(f32[80,128]{1,0:T(8,128)S(1)} %add.58), channel_id=1, source_target_pairs={{0,16},{2,18},{4,20},{6,22},{8,24},{10,26},{12,28},{14,30},{16,0},... | collective-permute-start | bytes 122888 | tf_op jit(solution)/shard_map/ppermute | solution.py:553
  94.3 4.4 %collective-permute-start.18 = (f32[72,256]{1,0:T(8,128)S(1)}, f32[72,256]{1,0:T(8,128)S(1)}, u32[]{:S(2)}, u32[]{:S(2)}) collective-permute-start(f32[72,256]{1,0:T(8,128)S(1)} %add.65), channel_id=1, source_target_pairs={{0,8},{2,10},{4,12},{6,14},{8,0},{10,2},{12,4},{14,6},{16,24},{18,... | collective-permute-start | bytes 221192 | tf_op jit(solution)/shard_map/ppermute | solution.py:553
  96.3 3.8 %collective-permute-start.13 = (f32[80,128]{1,0:T(8,128)S(1)}, f32[80,128]{1,0:T(8,128)S(1)}, u32[]{:S(2)}, u32[]{:S(2)}) collective-permute-start(f32[80,128]{1,0:T(8,128)S(1)} %add.59), channel_id=1, source_target_pairs={{0,2},{2,0},{4,6},{6,4},{8,10},{10,8},{12,14},{14,12},{16,18},{18,... | collective-permute-start | bytes 122888 | tf_op jit(solution)/shard_map/ppermute | solution.py:553
  96.4 15.2 %collective-permute-start.21 = (f32[128,1024]{1,0:T(8,128)S(1)}, f32[128,1024]{1,0:T(8,128)S(1)}, u32[]{:S(2)}, u32[]{:S(2)}) collective-permute-start(f32[128,1024]{1,0:T(8,128)S(1)} %slice.11), channel_id=1, source_target_pairs={{0,1},{1,0},{2,3},{3,2},{4,5},{5,4},{6,7},{7,6},{8,9},{9,8},{10,11... | collective-permute-start | bytes 1572872 | tf_op jit(solution)/shard_map/ppermute | solution.py:553
  98.8 6.1 %collective-permute-start.19 = (f32[72,256]{1,0:T(8,128)S(1)}, f32[72,256]{1,0:T(8,128)S(1)}, u32[]{:S(2)}, u32[]{:S(2)}) collective-permute-start(f32[72,256]{1,0:T(8,128)S(1)} %add.66), channel_id=1, source_target_pairs={{0,16},{2,18},{4,20},{6,22},{8,24},{10,26},{12,28},{14,30},{16,0},... | collective-permute-start | bytes 221192 | tf_op jit(solution)/shard_map/ppermute | solution.py:553
  104.9 6.6 %collective-permute-start.20 = (f32[72,256]{1,0:T(8,128)S(1)}, f32[72,256]{1,0:T(8,128)S(1)}, u32[]{:S(2)}, u32[]{:S(2)}) collective-permute-start(f32[72,256]{1,0:T(8,128)S(1)} %add.67), channel_id=1, source_target_pairs={{0,2},{2,0},{4,6},{6,4},{8,10},{10,8},{12,14},{14,12},{16,18},{18,... | collective-permute-start | bytes 221192 | tf_op jit(solution)/shard_map/ppermute | solution.py:553
